TPU v7x, 32 devices: a whole 2x2x4 slice. The times are simulated.
32 devices in a mesh: seq: 4 (over z), head: 8 (over y, x, core).
Axes of the slice: x: 2, y: 2, z: 4, core: 2. Of those that a mesh axis runs over, the one named last changes fastest.
Arguments:
- inputs: bfloat16 [2048, 8192], P('seq'), may hold values from -6 to 6
- w_qkv: bfloat16 [3, 8192, 2048], P(None, None, 'head'), may hold values from -0.0625 to 0.0625
- w_out: bfloat16 [2048, 8192], P('head'), may hold values from -0.1875 to 0.1875
- turn_ids: int32 [4, 512], P('seq'), may hold values from 0 to 15, never falling along the last dimension, each value on 1 to 64 neighbouring positions
- picked: int32 [4, 64], P('seq'), may hold values from 0 to 511
- owners: int32 [256, 1], P('seq'), may hold values from 0 to 7; in each aligned block of 64 rows (0 to 63, 64 to 127, ...) at most 32 rows name the same one
- candidates: bfloat16 [2048, 8192], P(('seq', 'head')), may hold values from -0.25 to 0.25
Outputs:
- mixed: bfloat16 [2048, 8192], P('seq', 'head')
- scores: float32 [1024, 64], P(('seq', 'head'))
Inputs may be any that keep to these rules, and one draw needn't show every extreme that they name: `turn_ids`: within each session turn numbers start at 0, never fall, and each turn has 1 to 64 tokens. `owners`: among the 64 picked rows of one session no owner is named more than 32 times.
All inputs are finite; a program needn't handle non-finite values.
Results may differ from a plain program's by a relative error of at most 0.008.
Values may be sent and summed in bfloat16 or wider, within the bound.
No kernel may reach another device: no remote copies, remote signals or barrier semaphores. Data moves between devices by JAX's collectives and lax.ppermute only.
A program may use at most 128 MiB of HBM per device.

v0:
```python
import functools
import jax
import jax.numpy as jnp
from jax import lax
from jax.experimental import pallas as pl
from jax.experimental.pallas import tpu as pltpu
from jax.sharding import PartitionSpec as P


HDIM = 128
F32 = jnp.float32
BF16 = jnp.bfloat16
VMEM = pl.BlockSpec(memory_space=pltpu.VMEM)
HBM = pl.BlockSpec(memory_space=pltpu.HBM)
ANY = pl.BlockSpec(memory_space=pl.ANY)


def move(value, masks):
    n = lax.axis_size("head")
    return lax.ppermute(value, "head", [(i, i ^ masks[i % 2]) for i in range(n)])


def dot(a, b):
    return jnp.dot(a, b, preferred_element_type=F32)


def masks_of(half_bits, m):
    return (m << 1, m << (1 + half_bits))


def place(half_bits, m, r):
    head = lax.axis_index("head")
    a, c = masks_of(half_bits, m), masks_of(half_bits, r)[::-1]
    return head ^ jnp.where(lax.bitwise_and(head, 1) == 0, a[0] ^ c[0], a[1] ^ c[1])


def block_of(index, size):
    return pl.ds(pl.multiple_of(index * size, size), size)


def kv_kernel(x_ref, w_ref, k_ref, v_ref, s_ref, x_buf, w_buf, acc, sems, *, steps):
    depth = x_ref.shape[1] // steps
    copies = []
    for s in range(steps):
        at = pl.ds(s * depth, depth)
        copies.append(
            [pltpu.make_async_copy(x_ref.at[:, at], x_buf.at[:, at], sems.at[0, s])]
            + [
                pltpu.make_async_copy(w_ref.at[1 + i, at], w_buf.at[i, at], sems.at[1 + i, s])
                for i in range(2)
            ]
        )
        for copy in copies[-1]:
            copy.start()
    for s in range(steps):
        for copy in copies[s]:
            copy.wait()
        at = pl.ds(s * depth, depth)
        for i in range(2):
            part = dot(x_buf[:, at], w_buf[i, at])
            acc[i] = part if s == 0 else acc[i] + part
    k_ref[...] = acc[0].astype(BF16)
    v_ref[...] = acc[1].astype(BF16)
    for h in range(k_ref.shape[1] // HDIM):
        of = pl.ds(h * HDIM, HDIM)
        state = lax.dot_general(
            k_ref[:, of], v_ref[:, of], (((0,), (0,)), ((), ())), preferred_element_type=F32
        )
        s_ref[h] = state.astype(BF16)


def q_kernel(x_ref, w_ref, k_ref, v_ref, q_ref, l_ref, w_buf, acc, sems, *, steps):
    depth = x_ref.shape[1] // steps
    copies = []
    for s in range(steps):
        at = pl.ds(s * depth, depth)
        copies.append(pltpu.make_async_copy(w_ref.at[0, at], w_buf.at[at], sems.at[s]))
        copies[-1].start()
    for s in range(steps):
        copies[s].wait()
        at = pl.ds(s * depth, depth)
        part = dot(x_ref[:, at], w_buf[at])
        acc[...] = part if s == 0 else acc[...] + part
    q_ref[...] = acc[...].astype(BF16)
    rows = q_ref.shape[0]
    block = min(rows, 256)
    for h in range(q_ref.shape[1] // HDIM):
        of = pl.ds(h * HDIM, HDIM)
        for b in range(0, rows, block):
            seen = b + block
            sc = lax.dot_general(
                q_ref[pl.ds(b, block), of],
                k_ref[pl.ds(0, seen), of],
                (((1,), (1,)), ((), ())),
                preferred_element_type=F32,
            )
            t = lax.broadcasted_iota(jnp.int32, sc.shape, 0) + b
            s = lax.broadcasted_iota(jnp.int32, sc.shape, 1)
            sc = jnp.where(t >= s, sc, 0.0).astype(BF16)
            l_ref[pl.ds(b, block), of] = dot(sc, v_ref[pl.ds(0, seen), of])


def attend_kernel(*refs, others):
    q_ref, l_ref, m_ref = refs[:3]
    states, out_ref = refs[3 : 3 + others], refs[3 + others]
    rows = q_ref.shape[0]
    seq = lax.axis_index("seq")
    for h in range(q_ref.shape[1] // HDIM):
        of = pl.ds(h * HDIM, HDIM)
        prefix = jnp.zeros((HDIM, HDIM), F32)
        for i, state in enumerate(states):
            prefix = prefix + jnp.where((seq ^ (i + 1)) < seq, state[h].astype(F32), 0.0)
        summed = l_ref[:, of] + dot(q_ref[:, of], prefix.astype(BF16))
        scale = lax.rsqrt(jnp.mean(summed * summed, axis=-1, keepdims=True) + 1e-05)
        attn = (summed * scale).astype(BF16)
        out_ref[pl.ds(0, rows), of] = attn
        out_ref[pl.ds(rows, m_ref.shape[0]), of] = dot(m_ref[...], attn).astype(BF16)


def stay(x):
    return pltpu.with_memory_space_constraint(x, pltpu.HBM)


def cut_kernel(w_ref, out_ref, sems, *, m, half_bits):
    count = 1 << half_bits
    cols = out_ref.shape[1] // count
    copies = [
        pltpu.make_async_copy(
            w_ref.at[:, block_of(place(half_bits, m, r), cols)],
            out_ref.at[:, pl.ds(r * cols, cols)],
            sems.at[r],
        )
        for r in range(count)
    ]
    for copy in copies:
        copy.start()
    for copy in copies:
        copy.wait()


def here_kernel(own_ref, peer_ref, m_ref, x_ref, w_ref, wp_ref, out_ref, x_buf, w_buf, sems, *, half_bits):
    side = 1 << half_bits
    cols = out_ref.shape[2]
    rows = m_ref.shape[1]
    order = list(range(1, side)) + [0]
    copies = {}
    for r in order:
        at = block_of(place(half_bits, 0, r), cols)
        for i, ref in enumerate((w_ref, wp_ref)):
            copies[r, i] = pltpu.make_async_copy(ref.at[:, at], w_buf.at[r, i], sems.at[r, i])
            copies[r, i].start()
    own = pltpu.make_async_copy(
        x_ref.at[:, block_of(lax.axis_index("head"), cols)], x_buf, sems.at[side, 0]
    )
    own.start()
    for r in order:
        total = None
        for i, ext in enumerate((own_ref, peer_ref)):
            copies[r, i].wait()
            part = dot(ext[...], w_buf[r, i])
            total = part if total is None else total + part
        out_ref[r] = total
    own.wait()
    out_ref[0, pl.ds(0, rows)] += x_buf[...].astype(F32)
    out_ref[0, pl.ds(rows, m_ref.shape[0])] += dot(m_ref[...], x_buf[...])


def add_kernel(*refs, count, r, rows):
    ext, w, base = refs[:count], refs[count : 2 * count], refs[2 * count]
    r_ref, p_ref = refs[2 * count + 1 :]
    cols = r_ref.shape[1]
    half = cols // 2
    for c in range(0, cols, half):
        total = base[r, :, pl.ds(c, half)]
        for e, b in zip(ext, w):
            total = total + dot(e[...], b[:, pl.ds(r * cols + c, half)])
        r_ref[:, pl.ds(c, half)] = total[:rows].astype(r_ref.dtype)
        p_ref[:, pl.ds(c, half)] = total[rows:].astype(p_ref.dtype)


def per_device(inputs, w_qkv, w_out, turn_ids, picked, owners, candidates):
    tokens_here, model_width = inputs.shape
    width = w_qkv.shape[2]
    heads_here = width // HDIM
    n_head = lax.axis_size("head")
    n_seq = lax.axis_size("seq")
    chips = n_head // 2
    half_bits = (chips.bit_length() - 1) // 2
    side = 1 << half_bits
    head = lax.axis_index("head")
    cols = model_width // n_head
    r_dev = picked.shape[1]
    steps = 8

    def along(m):
        return masks_of(half_bits, m)

    def across(r):
        return along(r)[::-1]

    def for_columns(w, m):
        return pl.pallas_call(
            functools.partial(cut_kernel, m=m, half_bits=half_bits),
            out_shape=jax.ShapeDtypeStruct((width, side * cols), BF16),
            in_specs=[ANY],
            out_specs=VMEM,
            scratch_shapes=[pltpu.SemaphoreType.DMA((side,))],
            cost_estimate=pl.CostEstimate(
                flops=0, bytes_accessed=4 * width * side * cols, transcendentals=0
            ),
            compiler_params=pltpu.CompilerParams(vmem_limit_bytes=4 << 20),
        )(w)

    w_in = [move(for_columns(stay(w_out), m), along(m)) for m in range(1, side)]
    w_peer = move(w_out, (1, 1))

    scratch = pltpu.VMEM
    keys, values, states, x_here = pl.pallas_call(
        functools.partial(kv_kernel, steps=steps),
        out_shape=[
            jax.ShapeDtypeStruct((tokens_here, width), BF16),
            jax.ShapeDtypeStruct((tokens_here, width), BF16),
            jax.ShapeDtypeStruct((heads_here, HDIM, HDIM), BF16),
            jax.ShapeDtypeStruct((tokens_here, model_width), BF16),
        ],
        in_specs=[HBM, HBM],
        out_specs=[VMEM] * 4,
        scratch_shapes=[
            scratch((2, model_width, width), BF16),
            scratch((2, tokens_here, width), F32),
            pltpu.SemaphoreType.DMA((3, steps)),
        ],
        cost_estimate=pl.CostEstimate(
            flops=4 * tokens_here * model_width * width,
            bytes_accessed=2 * model_width * (tokens_here + 2 * width),
            transcendentals=0,
        ),
        compiler_params=pltpu.CompilerParams(vmem_limit_bytes=24 << 20),
        name="kv",
    )(stay(inputs), stay(w_qkv))

    earlier = [
        lax.ppermute(states, "seq", [(i, i ^ s) for i in range(n_seq)]) for s in range(1, n_seq)
    ]

    w_in_peer = [move(for_columns(w_peer, m), along(m)) for m in range(1, side)]

    query, local = pl.pallas_call(
        functools.partial(q_kernel, steps=steps),
        out_shape=[
            jax.ShapeDtypeStruct((tokens_here, width), BF16),
            jax.ShapeDtypeStruct((tokens_here, width), F32),
        ],
        in_specs=[VMEM, HBM, VMEM, VMEM],
        out_specs=[VMEM] * 2,
        scratch_shapes=[
            scratch((model_width, width), BF16),
            scratch((tokens_here, width), F32),
            pltpu.SemaphoreType.DMA((steps,)),
        ],
        cost_estimate=pl.CostEstimate(
            flops=2 * tokens_here * model_width * width,
            bytes_accessed=2 * model_width * width,
            transcendentals=0,
        ),
        compiler_params=pltpu.CompilerParams(vmem_limit_bytes=10 << 20),
        name="qlocal",
    )(x_here, stay(w_qkv), keys, values)

    turn_row = turn_ids[0]
    pick_row = picked[0]
    tok_pos = jnp.arange(tokens_here, dtype=jnp.int32)
    pick_hot = tok_pos[None, :] == pick_row[:, None]
    sel_turn = jnp.sum(jnp.where(pick_hot, turn_row[None, :], 0), axis=1)
    member = (turn_row[None, :] == sel_turn[:, None]) & (tok_pos[None, :] <= pick_row[:, None])
    row_count = jnp.sum(member.astype(F32), axis=1)
    member = member.astype(BF16)

    ext = pl.pallas_call(
        functools.partial(attend_kernel, others=n_seq - 1),
        out_shape=jax.ShapeDtypeStruct((tokens_here + r_dev, width), BF16),
        in_specs=[VMEM] * (3 + n_seq - 1),
        out_specs=VMEM,
        compiler_params=pltpu.CompilerParams(vmem_limit_bytes=8 << 20),
        name="attend",
    )(query, local, member, *earlier)

    ext_peer = move(ext, (1, 1))
    ext_in = [move(ext, along(m)) for m in range(1, side)]
    ext_in_peer = [move(ext_peer, along(m)) for m in range(1, side)]

    height = tokens_here + r_dev
    base = pl.pallas_call(
        functools.partial(here_kernel, half_bits=half_bits),
        out_shape=jax.ShapeDtypeStruct((side, height, cols), F32),
        in_specs=[VMEM] * 3 + [HBM, HBM, ANY],
        out_specs=VMEM,
        scratch_shapes=[
            scratch((tokens_here, cols), BF16),
            scratch((side, 2, width, cols), BF16),
            pltpu.SemaphoreType.DMA((side + 1, 2)),
        ],
        cost_estimate=pl.CostEstimate(
            flops=4 * height * side * cols * width,
            bytes_accessed=4 * width * side * cols,
            transcendentals=0,
        ),
        compiler_params=pltpu.CompilerParams(vmem_limit_bytes=24 << 20),
        name="here",
    )(ext, ext_peer, member, stay(inputs), stay(w_out), w_peer)

    stacks = [*ext_in, *ext_in_peer]
    weights = [*w_in, *w_in_peer]

    def project(r, kind):
        return pl.pallas_call(
            functools.partial(add_kernel, count=len(stacks), r=r, rows=tokens_here),
            out_shape=[
                jax.ShapeDtypeStruct((tokens_here, cols), kind),
                jax.ShapeDtypeStruct((r_dev, cols), kind),
            ],
            in_specs=[VMEM] * (2 * len(stacks) + 1),
            out_specs=[VMEM] * 2,
            cost_estimate=pl.CostEstimate(
                flops=2 * height * cols * width * len(stacks),
                bytes_accessed=2 * width * cols * len(stacks),
                transcendentals=0,
            ),
            compiler_params=pltpu.CompilerParams(vmem_limit_bytes=12 << 20),
        )(*stacks, *weights, base)

    given = [project(r, BF16) for r in range(1, side)]
    pool_in = [move(p, across(r + 1)) for r, (_, p) in enumerate(given)]
    rows_in = [move(b, across(r + 1)) for r, (b, _) in enumerate(given)]
    rows_here, pooled = project(0, F32)

    for p in pool_in:
        pooled = pooled + p.astype(F32)
    summary = (pooled / row_count[:, None]).astype(BF16)
    summary_peer = move(summary, (1, 1))

    cap_rows = 4 * r_dev // n_head
    owner_row = owners[:, 0]
    row_pos = jnp.arange(r_dev, dtype=jnp.int32)
    head_pos = jnp.arange(n_head, dtype=jnp.int32)
    own_hot = (owner_row[:, None] == head_pos[None, :]).astype(jnp.int32)
    before = (row_pos[:, None] > row_pos[None, :]).astype(jnp.int32)
    slot_rank = jnp.sum(jnp.dot(before, own_hot) * own_hot, axis=1)
    slots = jnp.arange(cap_rows, dtype=jnp.int32)
    both = jnp.concatenate([summary, summary_peer], axis=1)
    scores = 0.0
    for j in range(chips):
        wanted = (owner_row == (head ^ (2 * j)))[None, :] & (slot_rank[None, :] == slots[:, None])
        rows = dot(wanted.astype(BF16), both).astype(BF16)
        if j:
            rows = move(rows, (2 * j, 2 * j))
        for c in range(2):
            cand = lax.dynamic_slice_in_dim(candidates, (head ^ (2 * j) ^ c) * cols, cols, 1)
            scores = scores + lax.dot_general(
                rows[:, c * cols : (c + 1) * cols],
                cand,
                (((1,), (1,)), ((), ())),
                preferred_element_type=F32,
            )

    total = rows_here
    for b in rows_in:
        total = total + b.astype(F32)
    return (total.astype(BF16), scores)


def solution(mesh):
    return jax.shard_map(
        per_device,
        mesh=mesh,
        in_specs=(
            P("seq", None),
            P(None, None, "head"),
            P("head", None),
            P("seq", None),
            P("seq", None),
            P("seq", None),
            P(("seq", "head"), None),
        ),
        out_specs=(P("seq", "head"), P(("seq", "head"), None)),
        check_vma=False,
    )
```

profile of v0, /device:TPU:0, one launch (start us, length us, event | category | flops | bytes accessed | tf_op | source)
XLA Modules:
  0.0 79.8 jit_solution(7099302854348418673)
XLA Ops:
  1.2 7.4 %kv.1 = (bf16[512,256]{1,0:T(8,128)(2,1)S(1)}, bf16[512,256]{1,0:T(8,128)(2,1)S(1)}, bf16[2,128,128]{2,1,0:T(8,128)(2,1)S(1)}, bf16[512,8192]{1,0:T(8,128)(2,1)S(1)}) custom-call(bf16[512,8192]{1,0:T(8,128)(2,1)} %x_ref.3, bf16[3,8192,256]{2,1,0:T(8,128)(2,1)} %w_ref.5), custom_call_target="tpu_custom_call" | custom-call | flops 4294967296 | bytes 16777216 | tf_op jit(solution)/shard_map/kv/pallas_call | solution.py:218
  8.6 2.6 %collective-permute-start = (bf16[2,128,128]{2,1,0:T(8,128)(2,1)S(1)}, bf16[2,128,128]{2,1,0:T(8,128)(2,1)S(1)}, u32[]{:S(2)}, u32[]{:S(2)}) collective-permute-start(bf16[2,128,128]{2,1,0:T(8,128)(2,1)S(1)} %get-tuple-element.17), channel_id=1, source_target_pairs={{0,8},{8,0},{16,24},{24,16},{1,9},{9,1},{17,25},{25,17},{2,10},{10... | collective-permute-start | bytes 196616 | tf_op jit(solution)/shard_map/ppermute | solution.py:243
  11.3 2.6 %collective-permute-start.1 = (bf16[2,128,128]{2,1,0:T(8,128)(2,1)S(1)}, bf16[2,128,128]{2,1,0:T(8,128)(2,1)S(1)}, u32[]{:S(2)}, u32[]{:S(2)}) collective-permute-start(bf16[2,128,128]{2,1,0:T(8,128)(2,1)S(1)} %get-tuple-element.17), channel_id=1, source_target_pairs={{0,16},{8,24},{16,0},{24,8},{1,17},{9,25},{17,1},{25,9},{2,18},{10... | collective-permute-start | bytes 196616 | tf_op jit(solution)/shard_map/ppermute | solution.py:243
  13.9 2.2 %shard_map.86 = bf16[256,2048]{1,0:T(8,128)(2,1)} custom-call(bf16[256,8192]{1,0:T(8,128)(2,1)} %w_ref.7), custom_call_target="tpu_custom_call" | custom-call | bytes 2097152 | tf_op jit(solution)/shard_map/pallas_call | solution.py:202
  16.0 1.8 %collective-permute-start.6 = (bf16[256,2048]{1,0:T(8,128)(2,1)}, bf16[256,2048]{1,0:T(8,128)(2,1)S(1)}, u32[]{:S(2)}, u32[]{:S(2)}) collective-permute-start(bf16[256,2048]{1,0:T(8,128)(2,1)} %shard_map.86), channel_id=1, source_target_pairs={{0,2},{1,5},{2,0},{3,7},{4,6},{5,1},{6,4},{7,3},{8,10},{9,13},{10,... | collective-permute-start | bytes 3145736 | tf_op jit(solution)/shard_map/ppermute | solution.py:20
  17.8 1.2 %shard_map.87 = bf16[256,2048]{1,0:T(8,128)(2,1)} custom-call(bf16[256,8192]{1,0:T(8,128)(2,1)S(1)} %collective-permute-done.7.w_ref.wp_ref), custom_call_target="tpu_custom_call" | custom-call | bytes 2097152 | tf_op jit(solution)/shard_map/pallas_call | solution.py:202
  19.7 6.6 %qlocal.1 = (bf16[512,256]{1,0:T(8,128)(2,1)S(1)}, f32[512,256]{1,0:T(8,128)S(1)}) custom-call(bf16[512,8192]{1,0:T(8,128)(2,1)S(1)} %get-tuple-element.12.x_ref, bf16[3,8192,256]{2,1,0:T(8,128)(2,1)} %w_ref.5, bf16[512,256]{1,0:T(8,128)(2,1)S(1)} %get-tuple-element.13.k_ref, bf16[512,256]{1,0:T(8,128)(2,1)S(1)} %get-tuple-element.14.v_ref), custom_call_target="tpu_custom_call" | custom-call | flops 2147483648 | bytes 4194304 | tf_op jit(solution)/shard_map/qlocal/pallas_call | solution.py:248
  26.3 1.4 %attend.1.own_ref = bf16[576,256]{1,0:T(8,128)(2,1)} custom-call(bf16[512,256]{1,0:T(8,128)(2,1)S(1)} %get-tuple-element.15.refs_0_, f32[512,256]{1,0:T(8,128)S(1)} %get-tuple-element.16.refs_1_, bf16[64,512]{1,0:T(8,128)(2,1)S(1)} %fusion.21.refs_2_.m_ref, bf16[2,128,128]{2,1,0:T(8,128)(2,1)S(1)} %collective-permute-done.refs_3_, ...), custom_call_target="tpu_custom_call" | custom-call | tf_op jit(solution)/shard_map/attend/pallas_call | solution.py:279
  27.8 1.7 %collective-permute-start.3 = (bf16[576,256]{1,0:T(8,128)(2,1)}, bf16[576,256]{1,0:T(8,128)(2,1)S(1)}, u32[]{:S(2)}, u32[]{:S(2)}) collective-permute-start(bf16[576,256]{1,0:T(8,128)(2,1)} %attend.1.own_ref), channel_id=1, source_target_pairs={{0,2},{1,5},{2,0},{3,7},{4,6},{5,1},{6,4},{7,3},{8,10},{9,13},{10,... | collective-permute-start | bytes 884744 | tf_op jit(solution)/shard_map/ppermute | solution.py:20
  29.7 1.7 %collective-permute-start.5 = (bf16[576,256]{1,0:T(8,128)(2,1)}, bf16[576,256]{1,0:T(8,128)(2,1)}, u32[]{:S(2)}, u32[]{:S(2)}) collective-permute-start(bf16[576,256]{1,0:T(8,128)(2,1)} %collective-permute-done.4.peer_ref), channel_id=1, source_target_pairs={{0,2},{1,5},{2,0},{3,7},{4,6},{5,1},{6,4},{7,3},{8,10},{9,13},{10,... | collective-permute-start | bytes 884744 | tf_op jit(solution)/shard_map/ppermute | solution.py:20
  31.4 2.2 %copy-done.2 = bf16[256,8192]{1,0:T(8,128)(2,1)S(1)} copy-done((bf16[256,8192]{1,0:T(8,128)(2,1)S(1)}, bf16[256,8192]{1,0:T(8,128)(2,1)}, u32[]{:S(2)}) %copy-start.2) | copy-done | bytes 4194328
  33.6 4.4 %here.1.refs_4_ = f32[2,576,1024]{2,1,0:T(8,128)S(1)} custom-call(bf16[576,256]{1,0:T(8,128)(2,1)} %attend.1.own_ref, bf16[576,256]{1,0:T(8,128)(2,1)} %collective-permute-done.4.peer_ref, bf16[64,512]{1,0:T(8,128)(2,1)S(1)} %fusion.21.refs_2_.m_ref, bf16[512,8192]{1,0:T(8,128)(2,1)} %x_ref.3, bf16[256,8192]{1,0:T(8,128)(2,1)} %w_ref.7, ...), custom_call_target="tpu_custom_call" | custom-call | flops 1207959552 | bytes 2097152 | tf_op jit(solution)/shard_map/here/pallas_call | solution.py:293
  38.0 7.5 %collective-permute-done.3.refs_0_ = bf16[576,256]{1,0:T(8,128)(2,1)S(1)} collective-permute-done((bf16[576,256]{1,0:T(8,128)(2,1)}, bf16[576,256]{1,0:T(8,128)(2,1)S(1)}, u32[]{:S(2)}, u32[]{:S(2)}) %collective-permute-start.3) | collective-permute-done | bytes 294944 | tf_op jit(solution)/shard_map/ppermute | solution.py:20
  45.5 3.3 %collective-permute-done.5.refs_1_ = bf16[576,256]{1,0:T(8,128)(2,1)} collective-permute-done((bf16[576,256]{1,0:T(8,128)(2,1)}, bf16[576,256]{1,0:T(8,128)(2,1)}, u32[]{:S(2)}, u32[]{:S(2)}) %collective-permute-start.5) | collective-permute-done | bytes 294944 | tf_op jit(solution)/shard_map/ppermute | solution.py:20
  48.8 1.7 %shard_map.89 = (bf16[512,1024]{1,0:T(8,128)(2,1)S(1)}, bf16[64,1024]{1,0:T(8,128)(2,1)S(1)}) custom-call(bf16[576,256]{1,0:T(8,128)(2,1)S(1)} %collective-permute-done.3.refs_0_, bf16[576,256]{1,0:T(8,128)(2,1)} %collective-permute-done.5.refs_1_, bf16[256,2048]{1,0:T(8,128)(2,1)S(1)} %collective-permute-done.6.refs_2_, ...), custom_call_target="tpu_custom_call" | custom-call | flops 603979776 | bytes 1048576 | tf_op jit(solution)/shard_map/pallas_call | solution.py:316
  51.5 1.7 %collective-permute-start.10 = (bf16[64,1024]{1,0:T(8,128)(2,1)S(1)}, bf16[64,1024]{1,0:T(8,128)(2,1)S(1)}, u32[]{:S(2)}, u32[]{:S(2)}) collective-permute-start(bf16[64,1024]{1,0:T(8,128)(2,1)S(1)} %get-tuple-element.21), channel_id=1, source_target_pairs={{0,4},{1,3},{2,6},{3,1},{4,0},{5,7},{6,2},{7,5},{8,12},{9,11},{10,... | collective-permute-start | bytes 393224 | tf_op jit(solution)/shard_map/ppermute | solution.py:20
  53.4 1.7 %shard_map.88 = (f32[512,1024]{1,0:T(8,128)S(1)}, f32[64,1024]{1,0:T(8,128)S(1)}) custom-call(bf16[576,256]{1,0:T(8,128)(2,1)S(1)} %collective-permute-done.3.refs_0_, bf16[576,256]{1,0:T(8,128)(2,1)} %collective-permute-done.5.refs_1_, bf16[256,2048]{1,0:T(8,128)(2,1)S(1)} %collective-permute-done.6.refs_2_, ...), custom_call_target="tpu_custom_call" | custom-call | flops 603979776 | bytes 1048576 | tf_op jit(solution)/shard_map/pallas_call | solution.py:316
  55.2 1.3 %copy-done.3 = f32[512,1024]{1,0:T(8,128)} copy-done((f32[512,1024]{1,0:T(8,128)}, f32[512,1024]{1,0:T(8,128)S(1)}, u32[]{:S(2)}) %copy-start.3) | copy-done | bytes 2097176
  56.9 1.7 %collective-permute-start.9 = (bf16[512,1024]{1,0:T(8,128)(2,1)}, bf16[512,1024]{1,0:T(8,128)(2,1)S(1)}, u32[]{:S(2)}, u32[]{:S(2)}) collective-permute-start(bf16[512,1024]{1,0:T(8,128)(2,1)} %copy-done.5), channel_id=1, source_target_pairs={{0,4},{1,3},{2,6},{3,1},{4,0},{5,7},{6,2},{7,5},{8,12},{9,11},{10,... | collective-permute-start | bytes 3145736 | tf_op jit(solution)/shard_map/ppermute | solution.py:20
  58.8 1.6 %collective-permute-start.12 = (bf16[32,2048]{1,0:T(8,128)(2,1)S(1)}, bf16[32,2048]{1,0:T(8,128)(2,1)S(1)}, u32[]{:S(2)}, u32[]{:S(2)}) collective-permute-start(bf16[32,2048]{1,0:T(8,128)(2,1)S(1)} %convolution_convert_fusion.2), channel_id=1, source_target_pairs={{0,2},{1,3},{2,0},{3,1},{4,6},{5,7},{6,4},{7,5},{8,10},{9,11},{10,... | collective-permute-start | bytes 393224 | tf_op jit(solution)/shard_map/ppermute | solution.py:20
  60.5 1.2 %collective-permute-start.13 = (bf16[32,2048]{1,0:T(8,128)(2,1)S(1)}, bf16[32,2048]{1,0:T(8,128)(2,1)S(1)}, u32[]{:S(2)}, u32[]{:S(2)}) collective-permute-start(bf16[32,2048]{1,0:T(8,128)(2,1)S(1)} %convolution_convert_fusion.1), channel_id=1, source_target_pairs={{0,4},{1,5},{2,6},{3,7},{4,0},{5,1},{6,2},{7,3},{8,12},{9,13},{10,... | collective-permute-start | bytes 393224 | tf_op jit(solution)/shard_map/ppermute | solution.py:20
  61.9 1.0 %collective-permute-start.14 = (bf16[32,2048]{1,0:T(8,128)(2,1)S(1)}, bf16[32,2048]{1,0:T(8,128)(2,1)S(1)}, u32[]{:S(2)}, u32[]{:S(2)}) collective-permute-start(bf16[32,2048]{1,0:T(8,128)(2,1)S(1)} %convolution_convert_fusion), channel_id=1, source_target_pairs={{0,6},{1,7},{2,4},{3,5},{4,2},{5,3},{6,0},{7,1},{8,14},{9,15},{10,... | collective-permute-start | bytes 393224 | tf_op jit(solution)/shard_map/ppermute | solution.py:20
  63.3 13.5 %collective-permute-done.13 = bf16[32,2048]{1,0:T(8,128)(2,1)S(1)} collective-permute-done((bf16[32,2048]{1,0:T(8,128)(2,1)S(1)}, bf16[32,2048]{1,0:T(8,128)(2,1)S(1)}, u32[]{:S(2)}, u32[]{:S(2)}) %collective-permute-start.13) | collective-permute-done | bytes 131104 | tf_op jit(solution)/shard_map/ppermute | solution.py:20
  78.5 1.4 %add_convert_fusion = bf16[512,1024]{1,0:T(8,128)(2,1)} fusion(f32[512,1024]{1,0:T(8,128)S(1)} %copy-done.4, bf16[512,1024]{1,0:T(8,128)(2,1)S(1)} %collective-permute-done.9), kind=kLoop, calls=%fused_computation.4 | loop fusion | flops 1572864 | bytes 4194304 | tf_op jit(solution)/shard_map/convert_element_type | solution.py:369
  (51 shorter events, 5.5 us)
Async XLA Ops:
  0.6 62.4 %copy-start = (bf16[64,8192]{1,0:T(8,128)(2,1)S(1)}, bf16[64,8192]{1,0:T(8,128)(2,1)}, u32[]{:S(2)}) copy-start(bf16[64,8192]{1,0:T(8,128)(2,1)} %param.13) | copy-start | bytes 3145732
  0.6 17.2 %collective-permute-start.7 = (bf16[256,8192]{1,0:T(8,128)(2,1)}, bf16[256,8192]{1,0:T(8,128)(2,1)S(1)}, u32[]{:S(2)}, u32[]{:S(2)}) collective-permute-start(bf16[256,8192]{1,0:T(8,128)(2,1)} %w_ref.7), channel_id=1, source_target_pairs={{0,1},{1,0},{2,3},{3,2},{4,5},{5,4},{6,7},{7,6},{8,9},{9,8},{10,11... | collective-permute-start | bytes 12582920 | tf_op jit(solution)/shard_map/ppermute | solution.py:20
  8.6 10.8 %copy-start.6 = (s32[1,512]{1,0:T(1,128)S(1)}, s32[1,512]{1,0:T(1,128)}, u32[]{:S(2)}) copy-start(s32[1,512]{1,0:T(1,128)} %param.10) | copy-start | bytes 6148
  8.6 10.8 %copy-start.7 = (s32[1,64]{1,0:T(1,128)S(1)}, s32[1,64]{1,0:T(1,128)}, u32[]{:S(2)}) copy-start(s32[1,64]{1,0:T(1,128)} %param.11) | copy-start | bytes 772
  8.6 17.7 %collective-permute-start = (bf16[2,128,128]{2,1,0:T(8,128)(2,1)S(1)}, bf16[2,128,128]{2,1,0:T(8,128)(2,1)S(1)}, u32[]{:S(2)}, u32[]{:S(2)}) collective-permute-start(bf16[2,128,128]{2,1,0:T(8,128)(2,1)S(1)} %get-tuple-element.17), channel_id=1, source_target_pairs={{0,8},{8,0},{16,24},{24,16},{1,9},{9,1},{17,25},{25,17},{2,10},{10... | collective-permute-start | bytes 196616 | tf_op jit(solution)/shard_map/ppermute | solution.py:243
  11.3 15.1 %collective-permute-start.1 = (bf16[2,128,128]{2,1,0:T(8,128)(2,1)S(1)}, bf16[2,128,128]{2,1,0:T(8,128)(2,1)S(1)}, u32[]{:S(2)}, u32[]{:S(2)}) collective-permute-start(bf16[2,128,128]{2,1,0:T(8,128)(2,1)S(1)} %get-tuple-element.17), channel_id=1, source_target_pairs={{0,16},{8,24},{16,0},{24,8},{1,17},{9,25},{17,1},{25,9},{2,18},{10... | collective-permute-start | bytes 196616 | tf_op jit(solution)/shard_map/ppermute | solution.py:243
  13.9 12.5 %collective-permute-start.2 = (bf16[2,128,128]{2,1,0:T(8,128)(2,1)S(1)}, bf16[2,128,128]{2,1,0:T(8,128)(2,1)S(1)}, u32[]{:S(2)}, u32[]{:S(2)}) collective-permute-start(bf16[2,128,128]{2,1,0:T(8,128)(2,1)S(1)} %get-tuple-element.17), channel_id=1, source_target_pairs={{0,24},{8,16},{16,8},{24,0},{1,25},{9,17},{17,9},{25,1},{2,26},{10... | collective-permute-start | bytes 196616 | tf_op jit(solution)/shard_map/ppermute | solution.py:243
  16.0 32.7 %collective-permute-start.6 = (bf16[256,2048]{1,0:T(8,128)(2,1)}, bf16[256,2048]{1,0:T(8,128)(2,1)S(1)}, u32[]{:S(2)}, u32[]{:S(2)}) collective-permute-start(bf16[256,2048]{1,0:T(8,128)(2,1)} %shard_map.86), channel_id=1, source_target_pairs={{0,2},{1,5},{2,0},{3,7},{4,6},{5,1},{6,4},{7,3},{8,10},{9,13},{10,... | collective-permute-start | bytes 3145736 | tf_op jit(solution)/shard_map/ppermute | solution.py:20
  17.8 8.5 %copy-start.1 = (bf16[256,8192]{1,0:T(8,128)(2,1)}, bf16[256,8192]{1,0:T(8,128)(2,1)S(1)}, u32[]{:S(2)}) copy-start(bf16[256,8192]{1,0:T(8,128)(2,1)S(1)} %collective-permute-done.7.w_ref.wp_ref) | copy-start | bytes 12582916
  19.0 29.8 %collective-permute-start.8 = (bf16[256,2048]{1,0:T(8,128)(2,1)}, bf16[256,2048]{1,0:T(8,128)(2,1)S(1)}, u32[]{:S(2)}, u32[]{:S(2)}) collective-permute-start(bf16[256,2048]{1,0:T(8,128)(2,1)} %shard_map.87), channel_id=1, source_target_pairs={{0,2},{1,5},{2,0},{3,7},{4,6},{5,1},{6,4},{7,3},{8,10},{9,13},{10,... | collective-permute-start | bytes 3145736 | tf_op jit(solution)/shard_map/ppermute | solution.py:20
  27.8 1.9 %collective-permute-start.4 = (bf16[576,256]{1,0:T(8,128)(2,1)}, bf16[576,256]{1,0:T(8,128)(2,1)}, u32[]{:S(2)}, u32[]{:S(2)}) collective-permute-start(bf16[576,256]{1,0:T(8,128)(2,1)} %attend.1.own_ref), channel_id=1, source_target_pairs={{0,1},{1,0},{2,3},{3,2},{4,5},{5,4},{6,7},{7,6},{8,9},{9,8},{10,11... | collective-permute-start | bytes 884744 | tf_op jit(solution)/shard_map/ppermute | solution.py:20
  27.8 17.7 %collective-permute-start.3 = (bf16[576,256]{1,0:T(8,128)(2,1)}, bf16[576,256]{1,0:T(8,128)(2,1)S(1)}, u32[]{:S(2)}, u32[]{:S(2)}) collective-permute-start(bf16[576,256]{1,0:T(8,128)(2,1)} %attend.1.own_ref), channel_id=1, source_target_pairs={{0,2},{1,5},{2,0},{3,7},{4,6},{5,1},{6,4},{7,3},{8,10},{9,13},{10,... | collective-permute-start | bytes 884744 | tf_op jit(solution)/shard_map/ppermute | solution.py:20
  29.7 19.1 %collective-permute-start.5 = (bf16[576,256]{1,0:T(8,128)(2,1)}, bf16[576,256]{1,0:T(8,128)(2,1)}, u32[]{:S(2)}, u32[]{:S(2)}) collective-permute-start(bf16[576,256]{1,0:T(8,128)(2,1)} %collective-permute-done.4.peer_ref), channel_id=1, source_target_pairs={{0,2},{1,5},{2,0},{3,7},{4,6},{5,1},{6,4},{7,3},{8,10},{9,13},{10,... | collective-permute-start | bytes 884744 | tf_op jit(solution)/shard_map/ppermute | solution.py:20
  31.4 2.2 %copy-start.2 = (bf16[256,8192]{1,0:T(8,128)(2,1)S(1)}, bf16[256,8192]{1,0:T(8,128)(2,1)}, u32[]{:S(2)}) copy-start(bf16[256,8192]{1,0:T(8,128)(2,1)} %copy-done.1) | copy-start | bytes 12582916
  50.5 1.0 %copy-start.5 = (bf16[512,1024]{1,0:T(8,128)(2,1)}, bf16[512,1024]{1,0:T(8,128)(2,1)S(1)}, u32[]{:S(2)}) copy-start(bf16[512,1024]{1,0:T(8,128)(2,1)S(1)} %get-tuple-element.19) | copy-start | bytes 3145732
  51.5 5.2 %copy-start.8 = (s32[64,1]{0,1:T(1,128)S(1)}, s32[64,1]{0,1:T(1,128)}, u32[]{:S(2)}) copy-start(s32[64,1]{0,1:T(1,128)} %param.12) | copy-start | bytes 772
  51.5 5.0 %collective-permute-start.10 = (bf16[64,1024]{1,0:T(8,128)(2,1)S(1)}, bf16[64,1024]{1,0:T(8,128)(2,1)S(1)}, u32[]{:S(2)}, u32[]{:S(2)}) collective-permute-start(bf16[64,1024]{1,0:T(8,128)(2,1)S(1)} %get-tuple-element.21), channel_id=1, source_target_pairs={{0,4},{1,3},{2,6},{3,1},{4,0},{5,7},{6,2},{7,5},{8,12},{9,11},{10,... | collective-permute-start | bytes 393224 | tf_op jit(solution)/shard_map/ppermute | solution.py:20
  55.2 1.3 %copy-start.3 = (f32[512,1024]{1,0:T(8,128)}, f32[512,1024]{1,0:T(8,128)S(1)}, u32[]{:S(2)}) copy-start(f32[512,1024]{1,0:T(8,128)S(1)} %get-tuple-element.18) | copy-start | bytes 6291460
  56.5 21.9 %copy-start.4 = (f32[512,1024]{1,0:T(8,128)S(1)}, f32[512,1024]{1,0:T(8,128)}, u32[]{:S(2)}) copy-start(f32[512,1024]{1,0:T(8,128)} %copy-done.3) | copy-start | bytes 6291460
  56.6 2.0 %collective-permute-start.11 = (bf16[64,1024]{1,0:T(8,128)(2,1)S(1)}, bf16[64,1024]{1,0:T(8,128)(2,1)S(1)}, u32[]{:S(2)}, u32[]{:S(2)}) collective-permute-start(bf16[64,1024]{1,0:T(8,128)(2,1)S(1)} %divide_convert_fusion), channel_id=1, source_target_pairs={{0,1},{1,0},{2,3},{3,2},{4,5},{5,4},{6,7},{7,6},{8,9},{9,8},{10,11... | collective-permute-start | bytes 393224 | tf_op jit(solution)/shard_map/ppermute | solution.py:20
  56.9 21.5 %collective-permute-start.9 = (bf16[512,1024]{1,0:T(8,128)(2,1)}, bf16[512,1024]{1,0:T(8,128)(2,1)S(1)}, u32[]{:S(2)}, u32[]{:S(2)}) collective-permute-start(bf16[512,1024]{1,0:T(8,128)(2,1)} %copy-done.5), channel_id=1, source_target_pairs={{0,4},{1,3},{2,6},{3,1},{4,0},{5,7},{6,2},{7,5},{8,12},{9,11},{10,... | collective-permute-start | bytes 3145736 | tf_op jit(solution)/shard_map/ppermute | solution.py:20
  58.8 18.7 %collective-permute-start.12 = (bf16[32,2048]{1,0:T(8,128)(2,1)S(1)}, bf16[32,2048]{1,0:T(8,128)(2,1)S(1)}, u32[]{:S(2)}, u32[]{:S(2)}) collective-permute-start(bf16[32,2048]{1,0:T(8,128)(2,1)S(1)} %convolution_convert_fusion.2), channel_id=1, source_target_pairs={{0,2},{1,3},{2,0},{3,1},{4,6},{5,7},{6,4},{7,5},{8,10},{9,11},{10,... | collective-permute-start | bytes 393224 | tf_op jit(solution)/shard_map/ppermute | solution.py:20
  60.5 16.3 %collective-permute-start.13 = (bf16[32,2048]{1,0:T(8,128)(2,1)S(1)}, bf16[32,2048]{1,0:T(8,128)(2,1)S(1)}, u32[]{:S(2)}, u32[]{:S(2)}) collective-permute-start(bf16[32,2048]{1,0:T(8,128)(2,1)S(1)} %convolution_convert_fusion.1), channel_id=1, source_target_pairs={{0,4},{1,5},{2,6},{3,7},{4,0},{5,1},{6,2},{7,3},{8,12},{9,13},{10,... | collective-permute-start | bytes 393224 | tf_op jit(solution)/shard_map/ppermute | solution.py:20
  61.9 15.3 %collective-permute-start.14 = (bf16[32,2048]{1,0:T(8,128)(2,1)S(1)}, bf16[32,2048]{1,0:T(8,128)(2,1)S(1)}, u32[]{:S(2)}, u32[]{:S(2)}) collective-permute-start(bf16[32,2048]{1,0:T(8,128)(2,1)S(1)} %convolution_convert_fusion), channel_id=1, source_target_pairs={{0,6},{1,7},{2,4},{3,5},{4,2},{5,3},{6,0},{7,1},{8,14},{9,15},{10,... | collective-permute-start | bytes 393224 | tf_op jit(solution)/shard_map/ppermute | solution.py:20
where the time goes:
time: 80.5 us; the launch traced here: 79.8 us
  Pallas kernels  26.7 us (33%)
  waiting for transfers between devices  24.5 us (30%)
  starting transfers between devices  18.6 us (23%)
  local copies, waits for them, and re-layouts  4.52 us (6%)
  matrix products  2.72 us (3%)
  other arithmetic  1.92 us (2%)
  between operations  0.96 us (1%)
    ppermute x12, waiting for transfers between devices, move(): lax.ppermute(value, 'head', [(i, i ^ masks[i % 2]) for i in range(n)])  24.5 us
    ppermute x12, starting transfers between devices, move(): lax.ppermute(value, 'head', [(i, i ^ masks[i % 2]) for i in range(n)])  13.3 us
    pallas_call x1, Pallas kernels, per_device(): pl.pallas_call(functools.partial(kv_kernel, steps=steps), out_shape=[jax....  7.38 us
    pallas_call x1, Pallas kernels, per_device(): pl.pallas_call(functools.partial(q_kernel, steps=steps), out_shape=[jax.S...  6.62 us
    ppermute x3, starting transfers between devices, per_device(): lax.ppermute(states, 'seq', [(i, i ^ s) for i in range(n_seq)])  5.24 us
    unnamed x18, local copies, waits for them, and re-layouts  4.52 us
    pallas_call x1, Pallas kernels, per_device(): pl.pallas_call(functools.partial(here_kernel, half_bits=half_bits), out_s...  4.4 us
    pallas_call x2, Pallas kernels, project(): pl.pallas_call(functools.partial(add_kernel, count=len(stacks), r=r, rows...  3.49 us
  transfers between devices with their start and end apart: 15, of which 4 were waited for; matrix products, arithmetic and copies ran while one was open for 4% of the time, Pallas kernels for 31%

commit v1 on v0

--- a/solution.py
+++ b/solution.py
@@ -12,7 +12,6 @@
 BF16 = jnp.bfloat16
 VMEM = pl.BlockSpec(memory_space=pltpu.VMEM)
 HBM = pl.BlockSpec(memory_space=pltpu.HBM)
-ANY = pl.BlockSpec(memory_space=pl.ANY)
 
 
 def move(value, masks):
@@ -28,8 +27,8 @@
     return (m << 1, m << (1 + half_bits))
 
 
-def place(half_bits, m, r):
-    head = lax.axis_index("head")
+def place(half_bits, m, r, head=None):
+    head = lax.axis_index("head") if head is None else head
     a, c = masks_of(half_bits, m), masks_of(half_bits, r)[::-1]
     return head ^ jnp.where(lax.bitwise_and(head, 1) == 0, a[0] ^ c[0], a[1] ^ c[1])
 
@@ -38,7 +37,9 @@
     return pl.ds(pl.multiple_of(index * size, size), size)
 
 
-def kv_kernel(x_ref, w_ref, k_ref, v_ref, s_ref, x_buf, w_buf, acc, sems, *, steps):
+def kv_kernel(
+    x_ref, w_ref, o_ref, k_ref, v_ref, s_ref, x_buf, cut_ref, w_buf, acc, sems, cut_sems, *, steps, half_bits
+):
     depth = x_ref.shape[1] // steps
     copies = []
     for s in range(steps):
@@ -52,6 +53,9 @@
         )
         for copy in copies[-1]:
             copy.start()
+    for_partner = cuts(o_ref, [cut_ref], cut_sems, [(True, 0)], half_bits)
+    for copy in for_partner:
+        copy.start()
     for s in range(steps):
         for copy in copies[s]:
             copy.wait()
@@ -67,6 +71,8 @@
             k_ref[:, of], v_ref[:, of], (((0,), (0,)), ((), ())), preferred_element_type=F32
         )
         s_ref[h] = state.astype(BF16)
+    for copy in for_partner:
+        copy.wait()
 
 
 def q_kernel(x_ref, w_ref, k_ref, v_ref, q_ref, l_ref, w_buf, acc, sems, *, steps):
@@ -121,17 +127,26 @@
     return pltpu.with_memory_space_constraint(x, pltpu.HBM)
 
 
-def cut_kernel(w_ref, out_ref, sems, *, m, half_bits):
-    count = 1 << half_bits
-    cols = out_ref.shape[1] // count
-    copies = [
-        pltpu.make_async_copy(
-            w_ref.at[:, block_of(place(half_bits, m, r), cols)],
-            out_ref.at[:, pl.ds(r * cols, cols)],
-            sems.at[r],
-        )
-        for r in range(count)
-    ]
+def cuts(w_ref, outs, sems, jobs, half_bits):
+    side = 1 << half_bits
+    cols = outs[0].shape[1] // side
+    head = lax.axis_index("head")
+    copies = []
+    for n, (partner, m) in enumerate(jobs):
+        for r in range(side):
+            at = place(half_bits, m, r, head ^ 1 if partner else head)
+            copies.append(
+                pltpu.make_async_copy(
+                    w_ref.at[:, block_of(at, cols)],
+                    outs[n].at[:, pl.ds(r * cols, cols)],
+                    sems.at[n, r],
+                )
+            )
+    return copies
+
+
+def cut_kernel(w_ref, *refs, jobs, half_bits):
+    copies = cuts(w_ref, refs[: len(jobs)], refs[-1], jobs, half_bits)
     for copy in copies:
         copy.start()
     for copy in copies:
@@ -146,20 +161,16 @@
     copies = {}
     for r in order:
         at = block_of(place(half_bits, 0, r), cols)
-        for i, ref in enumerate((w_ref, wp_ref)):
-            copies[r, i] = pltpu.make_async_copy(ref.at[:, at], w_buf.at[r, i], sems.at[r, i])
-            copies[r, i].start()
+        copies[r] = pltpu.make_async_copy(w_ref.at[:, at], w_buf.at[r], sems.at[r])
+        copies[r].start()
     own = pltpu.make_async_copy(
-        x_ref.at[:, block_of(lax.axis_index("head"), cols)], x_buf, sems.at[side, 0]
+        x_ref.at[:, block_of(lax.axis_index("head"), cols)], x_buf, sems.at[side]
     )
     own.start()
     for r in order:
-        total = None
-        for i, ext in enumerate((own_ref, peer_ref)):
-            copies[r, i].wait()
-            part = dot(ext[...], w_buf[r, i])
-            total = part if total is None else total + part
-        out_ref[r] = total
+        part = dot(peer_ref[...], wp_ref[:, pl.ds(r * cols, cols)])
+        copies[r].wait()
+        out_ref[r] = part + dot(own_ref[...], w_buf[r])
     own.wait()
     out_ref[0, pl.ds(0, rows)] += x_buf[...].astype(F32)
     out_ref[0, pl.ds(rows, m_ref.shape[0])] += dot(m_ref[...], x_buf[...])
@@ -167,15 +178,53 @@
 
 def add_kernel(*refs, count, r, rows):
     ext, w, base = refs[:count], refs[count : 2 * count], refs[2 * count]
-    r_ref, p_ref = refs[2 * count + 1 :]
+    r_ref, p_ref, buf, sems = refs[2 * count + 1 :]
     cols = r_ref.shape[1]
     half = cols // 2
-    for c in range(0, cols, half):
-        total = base[r, :, pl.ds(c, half)]
+    copies = []
+    for n, c in enumerate((0, half)):
+        at = pl.ds(c, half)
+        total = base[r, :, at]
         for e, b in zip(ext, w):
             total = total + dot(e[...], b[:, pl.ds(r * cols + c, half)])
-        r_ref[:, pl.ds(c, half)] = total[:rows].astype(r_ref.dtype)
-        p_ref[:, pl.ds(c, half)] = total[rows:].astype(p_ref.dtype)
+        buf[:, at] = total[:rows].astype(buf.dtype)
+        copies.append(pltpu.make_async_copy(buf.at[:, at], r_ref.at[:, at], sems.at[n]))
+        copies[-1].start()
+        p_ref[:, at] = total[rows:].astype(p_ref.dtype)
+    for copy in copies:
+        copy.wait()
+
+
+def mix_kernel(*refs):
+    parts, out_ref, buf, sems = refs[:-3], refs[-3], refs[-2], refs[-1]
+    rows = buf.shape[0] // 4
+    copies = []
+    for n in range(4):
+        at = pl.ds(n * rows, rows)
+        total = parts[0][at]
+        for part in parts[1:]:
+            total = total + part[at].astype(F32)
+        buf[at] = total.astype(BF16)
+        copies.append(pltpu.make_async_copy(buf.at[at], out_ref.at[at], sems.at[n]))
+        copies[-1].start()
+    for copy in copies:
+        copy.wait()
+
+
+def score_kernel(*refs):
+    c_ref, slots, out_ref = refs[0], refs[1:-1], refs[-1]
+    cols = slots[0].shape[1] // 2
+    head = lax.axis_index("head")
+    total = jnp.zeros(out_ref.shape, F32)
+    for j, rows in enumerate(slots):
+        for c in range(2):
+            total = total + lax.dot_general(
+                rows[:, pl.ds(c * cols, cols)],
+                c_ref[:, block_of(head ^ (2 * j + c), cols)],
+                (((1,), (1,)), ((), ())),
+                preferred_element_type=F32,
+            )
+    out_ref[...] = total
 
 
 def per_device(inputs, w_qkv, w_out, turn_ids, picked, owners, candidates):
@@ -198,52 +247,58 @@
     def across(r):
         return along(r)[::-1]
 
-    def for_columns(w, m):
-        return pl.pallas_call(
-            functools.partial(cut_kernel, m=m, half_bits=half_bits),
-            out_shape=jax.ShapeDtypeStruct((width, side * cols), BF16),
-            in_specs=[ANY],
-            out_specs=VMEM,
-            scratch_shapes=[pltpu.SemaphoreType.DMA((side,))],
-            cost_estimate=pl.CostEstimate(
-                flops=0, bytes_accessed=4 * width * side * cols, transcendentals=0
-            ),
-            compiler_params=pltpu.CompilerParams(vmem_limit_bytes=4 << 20),
-        )(w)
-
-    w_in = [move(for_columns(stay(w_out), m), along(m)) for m in range(1, side)]
-    w_peer = move(w_out, (1, 1))
+    def beside(m):
+        return tuple(mask ^ 1 for mask in across(m))
+
+    jobs = [(partner, m) for partner in (False, True) for m in range(1, side)]
+    cut = pl.pallas_call(
+        functools.partial(cut_kernel, jobs=jobs, half_bits=half_bits),
+        out_shape=[jax.ShapeDtypeStruct((width, side * cols), BF16)] * len(jobs),
+        in_specs=[HBM],
+        out_specs=[VMEM] * len(jobs),
+        scratch_shapes=[pltpu.SemaphoreType.DMA((len(jobs), side))],
+        cost_estimate=pl.CostEstimate(
+            flops=0, bytes_accessed=4 * width * side * cols * len(jobs), transcendentals=0
+        ),
+        compiler_params=pltpu.CompilerParams(
+            vmem_limit_bytes=2 * width * side * cols * len(jobs) + (1 << 20)
+        ),
+        name="cut",
+    )(stay(w_out))
+    w_in = [move(cut[m - 1], along(m)) for m in range(1, side)]
+    w_in_peer = [move(cut[side + m - 2], beside(m)) for m in range(1, side)]
 
     scratch = pltpu.VMEM
-    keys, values, states, x_here = pl.pallas_call(
-        functools.partial(kv_kernel, steps=steps),
+    keys, values, states, x_here, w_own = pl.pallas_call(
+        functools.partial(kv_kernel, steps=steps, half_bits=half_bits),
         out_shape=[
             jax.ShapeDtypeStruct((tokens_here, width), BF16),
             jax.ShapeDtypeStruct((tokens_here, width), BF16),
             jax.ShapeDtypeStruct((heads_here, HDIM, HDIM), BF16),
             jax.ShapeDtypeStruct((tokens_here, model_width), BF16),
+            jax.ShapeDtypeStruct((width, side * cols), BF16),
         ],
-        in_specs=[HBM, HBM],
-        out_specs=[VMEM] * 4,
+        in_specs=[HBM] * 3,
+        out_specs=[VMEM] * 5,
         scratch_shapes=[
             scratch((2, model_width, width), BF16),
             scratch((2, tokens_here, width), F32),
             pltpu.SemaphoreType.DMA((3, steps)),
+            pltpu.SemaphoreType.DMA((1, side)),
         ],
         cost_estimate=pl.CostEstimate(
             flops=4 * tokens_here * model_width * width,
             bytes_accessed=2 * model_width * (tokens_here + 2 * width),
             transcendentals=0,
         ),
-        compiler_params=pltpu.CompilerParams(vmem_limit_bytes=24 << 20),
+        compiler_params=pltpu.CompilerParams(vmem_limit_bytes=14 << 20),
         name="kv",
-    )(stay(inputs), stay(w_qkv))
+    )(stay(inputs), stay(w_qkv), stay(w_out))
+    w_peer = move(w_own, (1, 1))
 
     earlier = [
         lax.ppermute(states, "seq", [(i, i ^ s) for i in range(n_seq)]) for s in range(1, n_seq)
     ]
-
-    w_in_peer = [move(for_columns(w_peer, m), along(m)) for m in range(1, side)]
 
     query, local = pl.pallas_call(
         functools.partial(q_kernel, steps=steps),
@@ -281,31 +336,31 @@
         out_shape=jax.ShapeDtypeStruct((tokens_here + r_dev, width), BF16),
         in_specs=[VMEM] * (3 + n_seq - 1),
         out_specs=VMEM,
-        compiler_params=pltpu.CompilerParams(vmem_limit_bytes=8 << 20),
+        compiler_params=pltpu.CompilerParams(vmem_limit_bytes=4 << 20),
         name="attend",
     )(query, local, member, *earlier)
 
+    ext_in = [move(ext, along(m)) for m in range(1, side)]
+    ext_in_peer = [move(ext, beside(m)) for m in range(1, side)]
     ext_peer = move(ext, (1, 1))
-    ext_in = [move(ext, along(m)) for m in range(1, side)]
-    ext_in_peer = [move(ext_peer, along(m)) for m in range(1, side)]
 
     height = tokens_here + r_dev
     base = pl.pallas_call(
         functools.partial(here_kernel, half_bits=half_bits),
         out_shape=jax.ShapeDtypeStruct((side, height, cols), F32),
-        in_specs=[VMEM] * 3 + [HBM, HBM, ANY],
+        in_specs=[VMEM] * 3 + [HBM, HBM, VMEM],
         out_specs=VMEM,
         scratch_shapes=[
             scratch((tokens_here, cols), BF16),
-            scratch((side, 2, width, cols), BF16),
-            pltpu.SemaphoreType.DMA((side + 1, 2)),
+            scratch((side, width, cols), BF16),
+            pltpu.SemaphoreType.DMA((side + 1,)),
         ],
         cost_estimate=pl.CostEstimate(
             flops=4 * height * side * cols * width,
             bytes_accessed=4 * width * side * cols,
             transcendentals=0,
         ),
-        compiler_params=pltpu.CompilerParams(vmem_limit_bytes=24 << 20),
+        compiler_params=pltpu.CompilerParams(vmem_limit_bytes=12 << 20),
         name="here",
     )(ext, ext_peer, member, stay(inputs), stay(w_out), w_peer)
 
@@ -320,7 +375,11 @@
                 jax.ShapeDtypeStruct((r_dev, cols), kind),
             ],
             in_specs=[VMEM] * (2 * len(stacks) + 1),
-            out_specs=[VMEM] * 2,
+            out_specs=[HBM, VMEM],
+            scratch_shapes=[
+                scratch((tokens_here, cols), kind),
+                pltpu.SemaphoreType.DMA((2,)),
+            ],
             cost_estimate=pl.CostEstimate(
                 flops=2 * height * cols * width * len(stacks),
                 bytes_accessed=2 * width * cols * len(stacks),
@@ -348,25 +407,33 @@
     slot_rank = jnp.sum(jnp.dot(before, own_hot) * own_hot, axis=1)
     slots = jnp.arange(cap_rows, dtype=jnp.int32)
     both = jnp.concatenate([summary, summary_peer], axis=1)
-    scores = 0.0
+    found = []
     for j in range(chips):
         wanted = (owner_row == (head ^ (2 * j)))[None, :] & (slot_rank[None, :] == slots[:, None])
         rows = dot(wanted.astype(BF16), both).astype(BF16)
-        if j:
-            rows = move(rows, (2 * j, 2 * j))
-        for c in range(2):
-            cand = lax.dynamic_slice_in_dim(candidates, (head ^ (2 * j) ^ c) * cols, cols, 1)
-            scores = scores + lax.dot_general(
-                rows[:, c * cols : (c + 1) * cols],
-                cand,
-                (((1,), (1,)), ((), ())),
-                preferred_element_type=F32,
-            )
-
-    total = rows_here
-    for b in rows_in:
-        total = total + b.astype(F32)
-    return (total.astype(BF16), scores)
+        found.append(move(rows, (2 * j, 2 * j)) if j else rows)
+
+    mixed = pl.pallas_call(
+        mix_kernel,
+        out_shape=jax.ShapeDtypeStruct((tokens_here, cols), BF16),
+        in_specs=[VMEM] * (1 + len(rows_in)),
+        out_specs=HBM,
+        scratch_shapes=[scratch((tokens_here, cols), BF16), pltpu.SemaphoreType.DMA((4,))],
+        cost_estimate=pl.CostEstimate(
+            flops=tokens_here * cols, bytes_accessed=8 * tokens_here * cols, transcendentals=0
+        ),
+        compiler_params=pltpu.CompilerParams(vmem_limit_bytes=4 << 20),
+        name="mix",
+    )(rows_here, *rows_in)
+    scores = pl.pallas_call(
+        score_kernel,
+        out_shape=jax.ShapeDtypeStruct((cap_rows, candidates.shape[0]), F32),
+        in_specs=[VMEM] * (1 + chips),
+        out_specs=VMEM,
+        compiler_params=pltpu.CompilerParams(vmem_limit_bytes=2 << 20),
+        name="score",
+    )(candidates, *found)
+    return (mixed, scores)
 
 
 def solution(mesh):

time: 80.5 us -> 76 us (0.944)
  waiting for transfers between devices: 24.5 us -> 29.1 us
  local copies, waits for them, and re-layouts: 4.52 us -> 0.02 us
  matrix products: 2.72 us -> 0.79 us
  starting transfers between devices: 18.6 us -> 16.8 us
  other arithmetic: 1.92 us -> 0.56 us
  Pallas kernels: 26.7 us -> 27.8 us
    ppermute x12, waiting for transfers between devices: 24.5 us -> 29 us  [move(): lax.ppermute(value, 'head', [(i, i ^ masks[i % 2]) for i in range(n)])]
    unnamed x18 -> x8, local copies, waits for them, and re-layouts: 4.52 us -> 0.02 us
    pallas_call x3 -> x4, Pallas kernels: 10.7 us -> 13.3 us  [the longest x1 8.38 us: per_device(): pl.pallas_call(functools.partial(kv_kernel, steps=steps, half_bits=half_b...]
    ppermute x12, starting transfers between devices: 13.3 us -> 11.2 us  [move(): lax.ppermute(value, 'head', [(i, i ^ masks[i % 2]) for i in range(n)])]
    dot_general x8 -> x0, matrix products: 1.93 us -> none  [per_device(): lax.dot_general(rows[:, c * cols:(c + 1) * cols], cand, (((1,), (1,)), ((...]
    convert_element_type x1 -> x0, other arithmetic: 1.36 us -> none  [per_device(): return (total.astype(BF16), scores)]
    pallas_call x2, Pallas kernels: 3.49 us -> 2.59 us  [project(): pl.pallas_call(functools.partial(add_kernel, count=len(stacks), r=r, rows...]
  transfers between devices with their start and end apart: 15 -> 15, of which waited for: 4 -> 6; matrix products, arithmetic and copies ran while one was open for 4% -> 2% of each run, Pallas kernels for 31% -> 23%
where the time goes in v1:
time: 76 us; the launch traced here: 75.8 us
  waiting for transfers between devices  29.1 us (38%)
  Pallas kernels  27.8 us (37%)
  starting transfers between devices  16.8 us (22%)
  between operations  0.83 us (1%)
  matrix products  0.79 us (1%)
    ppermute x12, waiting for transfers between devices, move(): lax.ppermute(value, 'head', [(i, i ^ masks[i % 2]) for i in range(n)])  29 us
    ppermute x12, starting transfers between devices, move(): lax.ppermute(value, 'head', [(i, i ^ masks[i % 2]) for i in range(n)])  11.2 us
    pallas_call x1, Pallas kernels, per_device(): pl.pallas_call(functools.partial(kv_kernel, steps=steps, half_bits=half_b...  8.38 us
    pallas_call x1, Pallas kernels, per_device(): pl.pallas_call(functools.partial(q_kernel, steps=steps), out_shape=[jax.S...  6.61 us
    ppermute x3, starting transfers between devices, per_device(): lax.ppermute(states, 'seq', [(i, i ^ s) for i in range(n_seq)])  5.52 us
    pallas_call x1, Pallas kernels, per_device(): pl.pallas_call(functools.partial(here_kernel, half_bits=half_bits), out_s...  4.52 us
    pallas_call x1, Pallas kernels, per_device(): pl.pallas_call(functools.partial(cut_kernel, jobs=jobs, half_bits=half_bi...  2.88 us
    pallas_call x2, Pallas kernels, project(): pl.pallas_call(functools.partial(add_kernel, count=len(stacks), r=r, rows...  2.59 us
  transfers between devices with their start and end apart: 15, of which 6 were waited for; matrix products, arithmetic and copies ran while one was open for 2% of the time, Pallas kernels for 23%

profile of v1, /device:TPU:0, one launch (start us, length us, event | category | flops | bytes accessed | tf_op | source)
XLA Modules:
  0.0 75.8 jit_solution(16596070556777670711)
XLA Ops:
  0.6 8.4 %kv.1 = (bf16[512,256]{1,0:T(8,128)(2,1)S(1)}, bf16[512,256]{1,0:T(8,128)(2,1)S(1)}, bf16[2,128,128]{2,1,0:T(8,128)(2,1)S(1)}, bf16[512,8192]{1,0:T(8,128)(2,1)S(1)}, bf16[256,2048]{1,0:T(8,128)(2,1)}) custom-call(bf16[512,8192]{1,0:T(8,128)(2,1)} %x_ref.3, bf16[3,8192,256]{2,1,0:T(8,128)(2,1)} %w_ref.5, bf16[256,8192]{1,0:T(8,128)(2,1)} %w_ref.7), custom_call_target="tpu_custom_call" | custom-call | flops 4294967296 | bytes 16777216 | tf_op jit(solution)/shard_map/kv/pallas_call | solution.py:272
  9.6 2.6 %collective-permute-start = (bf16[2,128,128]{2,1,0:T(8,128)(2,1)S(1)}, bf16[2,128,128]{2,1,0:T(8,128)(2,1)S(1)}, u32[]{:S(2)}, u32[]{:S(2)}) collective-permute-start(bf16[2,128,128]{2,1,0:T(8,128)(2,1)S(1)} %get-tuple-element.20), channel_id=1, source_target_pairs={{0,8},{8,0},{16,24},{24,16},{1,9},{9,1},{17,25},{25,17},{2,10},{10... | collective-permute-start | bytes 196616 | tf_op jit(solution)/shard_map/ppermute | solution.py:300
  12.2 2.6 %collective-permute-start.1 = (bf16[2,128,128]{2,1,0:T(8,128)(2,1)S(1)}, bf16[2,128,128]{2,1,0:T(8,128)(2,1)S(1)}, u32[]{:S(2)}, u32[]{:S(2)}) collective-permute-start(bf16[2,128,128]{2,1,0:T(8,128)(2,1)S(1)} %get-tuple-element.20), channel_id=1, source_target_pairs={{0,16},{8,24},{16,0},{24,8},{1,17},{9,25},{17,1},{25,9},{2,18},{10... | collective-permute-start | bytes 196616 | tf_op jit(solution)/shard_map/ppermute | solution.py:300
  14.8 2.9 %cut.1 = (bf16[256,2048]{1,0:T(8,128)(2,1)}, bf16[256,2048]{1,0:T(8,128)(2,1)}) custom-call(bf16[256,8192]{1,0:T(8,128)(2,1)} %w_ref.7), custom_call_target="tpu_custom_call" | custom-call | bytes 4194304 | tf_op jit(solution)/shard_map/cut/pallas_call | solution.py:254
  17.7 1.6 %collective-permute-start.5 = (bf16[256,2048]{1,0:T(8,128)(2,1)}, bf16[256,2048]{1,0:T(8,128)(2,1)S(1)}, u32[]{:S(2)}, u32[]{:S(2)}) collective-permute-start(bf16[256,2048]{1,0:T(8,128)(2,1)} %get-tuple-element.21), channel_id=1, source_target_pairs={{0,2},{1,5},{2,0},{3,7},{4,6},{5,1},{6,4},{7,3},{8,10},{9,13},{10,... | collective-permute-start | bytes 3145736 | tf_op jit(solution)/shard_map/ppermute | solution.py:19
  19.9 6.6 %qlocal.1 = (bf16[512,256]{1,0:T(8,128)(2,1)S(1)}, f32[512,256]{1,0:T(8,128)S(1)}) custom-call(bf16[512,8192]{1,0:T(8,128)(2,1)S(1)} %get-tuple-element.15.x_ref, bf16[3,8192,256]{2,1,0:T(8,128)(2,1)} %w_ref.5, bf16[512,256]{1,0:T(8,128)(2,1)S(1)} %get-tuple-element.16.k_ref, bf16[512,256]{1,0:T(8,128)(2,1)S(1)} %get-tuple-element.17.v_ref), custom_call_target="tpu_custom_call" | custom-call | flops 2147483648 | bytes 4194304 | tf_op jit(solution)/shard_map/qlocal/pallas_call | solution.py:303
  26.5 0.7 attend.1.own_ref
  27.8 1.5 %collective-permute-start.3 = (bf16[576,256]{1,0:T(8,128)(2,1)S(1)}, bf16[576,256]{1,0:T(8,128)(2,1)S(1)}, u32[]{:S(2)}, u32[]{:S(2)}) collective-permute-start(bf16[576,256]{1,0:T(8,128)(2,1)S(1)} %attend.1.own_ref), channel_id=1, source_target_pairs={{0,2},{1,5},{2,0},{3,7},{4,6},{5,1},{6,4},{7,3},{8,10},{9,13},{10,... | collective-permute-start | bytes 884744 | tf_op jit(solution)/shard_map/ppermute | solution.py:19
  29.2 1.2 %collective-permute-start.4 = (bf16[576,256]{1,0:T(8,128)(2,1)S(1)}, bf16[576,256]{1,0:T(8,128)(2,1)S(1)}, u32[]{:S(2)}, u32[]{:S(2)}) collective-permute-start(bf16[576,256]{1,0:T(8,128)(2,1)S(1)} %attend.1.own_ref), channel_id=1, source_target_pairs={{0,5},{1,2},{2,7},{3,0},{4,1},{5,6},{6,3},{7,4},{8,13},{9,10},{10,... | collective-permute-start | bytes 884744 | tf_op jit(solution)/shard_map/ppermute | solution.py:19
  30.5 4.5 %here.1.refs_4_ = f32[2,576,1024]{2,1,0:T(8,128)S(1)} custom-call(bf16[576,256]{1,0:T(8,128)(2,1)S(1)} %attend.1.own_ref, bf16[576,256]{1,0:T(8,128)(2,1)S(1)} %collective-permute-done.7.peer_ref, bf16[64,512]{1,0:T(8,128)(2,1)S(1)} %fusion.2.refs_2_.m_ref, bf16[512,8192]{1,0:T(8,128)(2,1)} %x_ref.3, bf16[256,8192]{1,0:T(8,128)(2,1)} %w_ref.7, ...), custom_call_target="tpu_custom_call" | custom-call | flops 1207959552 | bytes 2097152 | tf_op jit(solution)/shard_map/here/pallas_call | solution.py:348
  35.0 14.4 %collective-permute-done.3.refs_0_ = bf16[576,256]{1,0:T(8,128)(2,1)S(1)} collective-permute-done((bf16[576,256]{1,0:T(8,128)(2,1)S(1)}, bf16[576,256]{1,0:T(8,128)(2,1)S(1)}, u32[]{:S(2)}, u32[]{:S(2)}) %collective-permute-start.3) | collective-permute-done | bytes 294944 | tf_op jit(solution)/shard_map/ppermute | solution.py:19
  49.4 0.9 %collective-permute-done.4.refs_1_ = bf16[576,256]{1,0:T(8,128)(2,1)S(1)} collective-permute-done((bf16[576,256]{1,0:T(8,128)(2,1)S(1)}, bf16[576,256]{1,0:T(8,128)(2,1)S(1)}, u32[]{:S(2)}, u32[]{:S(2)}) %collective-permute-start.4) | collective-permute-done | bytes 294944 | tf_op jit(solution)/shard_map/ppermute | solution.py:19
  50.4 1.1 %shard_map.87 = (bf16[512,1024]{1,0:T(8,128)(2,1)S(1)}, bf16[64,1024]{1,0:T(8,128)(2,1)S(1)}) custom-call(bf16[576,256]{1,0:T(8,128)(2,1)S(1)} %collective-permute-done.3.refs_0_, bf16[576,256]{1,0:T(8,128)(2,1)S(1)} %collective-permute-done.4.refs_1_, bf16[256,2048]{1,0:T(8,128)(2,1)S(1)} %collective-permute-done.5.refs_2_, ...), custom_call_target="tpu_custom_call" | custom-call | flops 603979776 | bytes 1048576 | tf_op jit(solution)/shard_map/pallas_call | solution.py:371
  51.5 1.6 %collective-permute-start.10 = (bf16[64,1024]{1,0:T(8,128)(2,1)S(1)}, bf16[64,1024]{1,0:T(8,128)(2,1)S(1)}, u32[]{:S(2)}, u32[]{:S(2)}) collective-permute-start(bf16[64,1024]{1,0:T(8,128)(2,1)S(1)} %get-tuple-element.27), channel_id=1, source_target_pairs={{0,4},{1,3},{2,6},{3,1},{4,0},{5,7},{6,2},{7,5},{8,12},{9,11},{10,... | collective-permute-start | bytes 393224 | tf_op jit(solution)/shard_map/ppermute | solution.py:19
  53.2 0.6 collective-permute-start.9
  53.8 1.5 %shard_map.86 = (f32[512,1024]{1,0:T(8,128)S(1)}, f32[64,1024]{1,0:T(8,128)S(1)}) custom-call(bf16[576,256]{1,0:T(8,128)(2,1)S(1)} %collective-permute-done.3.refs_0_, bf16[576,256]{1,0:T(8,128)(2,1)S(1)} %collective-permute-done.4.refs_1_, bf16[256,2048]{1,0:T(8,128)(2,1)S(1)} %collective-permute-done.5.refs_2_, ...), custom_call_target="tpu_custom_call" | custom-call | flops 603979776 | bytes 1048576 | tf_op jit(solution)/shard_map/pallas_call | solution.py:371
  55.3 1.2 %collective-permute-done.10 = bf16[64,1024]{1,0:T(8,128)(2,1)S(1)} collective-permute-done((bf16[64,1024]{1,0:T(8,128)(2,1)S(1)}, bf16[64,1024]{1,0:T(8,128)(2,1)S(1)}, u32[]{:S(2)}, u32[]{:S(2)}) %collective-permute-start.10) | collective-permute-done | bytes 131104 | tf_op jit(solution)/shard_map/ppermute | solution.py:19
  56.9 1.2 %collective-permute-done.11 = bf16[64,1024]{1,0:T(8,128)(2,1)S(1)} collective-permute-done((bf16[64,1024]{1,0:T(8,128)(2,1)S(1)}, bf16[64,1024]{1,0:T(8,128)(2,1)S(1)}, u32[]{:S(2)}, u32[]{:S(2)}) %collective-permute-start.11) | collective-permute-done | bytes 131104 | tf_op jit(solution)/shard_map/ppermute | solution.py:19
  58.2 2.5 %collective-permute-start.14 = (bf16[32,2048]{1,0:T(8,128)(2,1)S(1)}, bf16[32,2048]{1,0:T(8,128)(2,1)S(1)}, u32[]{:S(2)}, u32[]{:S(2)}) collective-permute-start(bf16[32,2048]{1,0:T(8,128)(2,1)S(1)} %convolution_convert_fusion), channel_id=1, source_target_pairs={{0,6},{1,7},{2,4},{3,5},{4,2},{5,3},{6,0},{7,1},{8,14},{9,15},{10,... | collective-permute-start | bytes 393224 | tf_op jit(solution)/shard_map/ppermute | solution.py:19
  61.6 0.6 collective-permute-start.12
  62.4 3.1 %collective-permute-done.14.refs_4_ = bf16[32,2048]{1,0:T(8,128)(2,1)S(1)} collective-permute-done((bf16[32,2048]{1,0:T(8,128)(2,1)S(1)}, bf16[32,2048]{1,0:T(8,128)(2,1)S(1)}, u32[]{:S(2)}, u32[]{:S(2)}) %collective-permute-start.14) | collective-permute-done | bytes 131104 | tf_op jit(solution)/shard_map/ppermute | solution.py:19
  65.5 8.2 %collective-permute-done.13.refs_3_ = bf16[32,2048]{1,0:T(8,128)(2,1)S(1)} collective-permute-done((bf16[32,2048]{1,0:T(8,128)(2,1)S(1)}, bf16[32,2048]{1,0:T(8,128)(2,1)S(1)}, u32[]{:S(2)}, u32[]{:S(2)}) %collective-permute-start.13) | collective-permute-done | bytes 131104 | tf_op jit(solution)/shard_map/ppermute | solution.py:19
  73.7 1.0 %score.1 = f32[32,64]{1,0:T(8,128)} custom-call(bf16[64,8192]{1,0:T(8,128)(2,1)S(1)} %copy-done, bf16[32,2048]{1,0:T(8,128)(2,1)S(1)} %convolution_convert_fusion.3.refs_1_, bf16[32,2048]{1,0:T(8,128)(2,1)S(1)} %collective-permute-done.12.refs_2_, bf16[32,2048]{1,0:T(8,128)(2,1)S(1)} %collective-permute-done.13.refs_3_, ...), custom_call_target="tpu_custom_call" | custom-call | tf_op jit(solution)/shard_map/score/pallas_call | solution.py:428
  74.8 1.0 %mix.1 = bf16[512,1024]{1,0:T(8,128)(2,1)} custom-call(f32[512,1024]{1,0:T(8,128)S(1)} %get-tuple-element.24.refs_0_, bf16[512,1024]{1,0:T(8,128)(2,1)S(1)} %collective-permute-done.9.refs_1_), custom_call_target="tpu_custom_call" | custom-call | flops 524288 | bytes 4194304 | tf_op jit(solution)/shard_map/mix/pallas_call | solution.py:416
  (33 shorter events, 3.4 us)
Async XLA Ops:
  0.6 18.6 %copy-start.1 = (s32[1,512]{1,0:T(1,128)S(1)}, s32[1,512]{1,0:T(1,128)}, u32[]{:S(2)}) copy-start(s32[1,512]{1,0:T(1,128)} %param.10) | copy-start | bytes 6148
  0.6 18.6 %copy-start.2 = (s32[1,64]{1,0:T(1,128)S(1)}, s32[1,64]{1,0:T(1,128)}, u32[]{:S(2)}) copy-start(s32[1,64]{1,0:T(1,128)} %param.11) | copy-start | bytes 772
  9.0 21.4 %collective-permute-start.8 = (bf16[256,2048]{1,0:T(8,128)(2,1)}, bf16[256,2048]{1,0:T(8,128)(2,1)}, u32[]{:S(2)}, u32[]{:S(2)}) collective-permute-start(bf16[256,2048]{1,0:T(8,128)(2,1)} %get-tuple-element.23), channel_id=1, source_target_pairs={{0,1},{1,0},{2,3},{3,2},{4,5},{5,4},{6,7},{7,6},{8,9},{9,8},{10,11... | collective-permute-start | bytes 3145736 | tf_op jit(solution)/shard_map/ppermute | solution.py:19
  9.6 10.0 %collective-permute-start = (bf16[2,128,128]{2,1,0:T(8,128)(2,1)S(1)}, bf16[2,128,128]{2,1,0:T(8,128)(2,1)S(1)}, u32[]{:S(2)}, u32[]{:S(2)}) collective-permute-start(bf16[2,128,128]{2,1,0:T(8,128)(2,1)S(1)} %get-tuple-element.20), channel_id=1, source_target_pairs={{0,8},{8,0},{16,24},{24,16},{1,9},{9,1},{17,25},{25,17},{2,10},{10... | collective-permute-start | bytes 196616 | tf_op jit(solution)/shard_map/ppermute | solution.py:300
  12.2 14.3 %collective-permute-start.1 = (bf16[2,128,128]{2,1,0:T(8,128)(2,1)S(1)}, bf16[2,128,128]{2,1,0:T(8,128)(2,1)S(1)}, u32[]{:S(2)}, u32[]{:S(2)}) collective-permute-start(bf16[2,128,128]{2,1,0:T(8,128)(2,1)S(1)} %get-tuple-element.20), channel_id=1, source_target_pairs={{0,16},{8,24},{16,0},{24,8},{1,17},{9,25},{17,1},{25,9},{2,18},{10... | collective-permute-start | bytes 196616 | tf_op jit(solution)/shard_map/ppermute | solution.py:300
  17.7 32.6 %collective-permute-start.5 = (bf16[256,2048]{1,0:T(8,128)(2,1)}, bf16[256,2048]{1,0:T(8,128)(2,1)S(1)}, u32[]{:S(2)}, u32[]{:S(2)}) collective-permute-start(bf16[256,2048]{1,0:T(8,128)(2,1)} %get-tuple-element.21), channel_id=1, source_target_pairs={{0,2},{1,5},{2,0},{3,7},{4,6},{5,1},{6,4},{7,3},{8,10},{9,13},{10,... | collective-permute-start | bytes 3145736 | tf_op jit(solution)/shard_map/ppermute | solution.py:19
  19.3 31.1 %collective-permute-start.6 = (bf16[256,2048]{1,0:T(8,128)(2,1)}, bf16[256,2048]{1,0:T(8,128)(2,1)S(1)}, u32[]{:S(2)}, u32[]{:S(2)}) collective-permute-start(bf16[256,2048]{1,0:T(8,128)(2,1)} %get-tuple-element.22), channel_id=1, source_target_pairs={{0,5},{1,2},{2,7},{3,0},{4,1},{5,6},{6,3},{7,4},{8,13},{9,10},{10,... | collective-permute-start | bytes 3145736 | tf_op jit(solution)/shard_map/ppermute | solution.py:19
  19.6 6.9 %collective-permute-start.2 = (bf16[2,128,128]{2,1,0:T(8,128)(2,1)S(1)}, bf16[2,128,128]{2,1,0:T(8,128)(2,1)S(1)}, u32[]{:S(2)}, u32[]{:S(2)}) collective-permute-start(bf16[2,128,128]{2,1,0:T(8,128)(2,1)S(1)} %get-tuple-element.20), channel_id=1, source_target_pairs={{0,24},{8,16},{16,8},{24,0},{1,25},{9,17},{17,9},{25,1},{2,26},{10... | collective-permute-start | bytes 196616 | tf_op jit(solution)/shard_map/ppermute | solution.py:300
  27.2 2.0 %collective-permute-start.7 = (bf16[576,256]{1,0:T(8,128)(2,1)S(1)}, bf16[576,256]{1,0:T(8,128)(2,1)S(1)}, u32[]{:S(2)}, u32[]{:S(2)}) collective-permute-start(bf16[576,256]{1,0:T(8,128)(2,1)S(1)} %attend.1.own_ref), channel_id=1, source_target_pairs={{0,1},{1,0},{2,3},{3,2},{4,5},{5,4},{6,7},{7,6},{8,9},{9,8},{10,11... | collective-permute-start | bytes 884744 | tf_op jit(solution)/shard_map/ppermute | solution.py:19
  27.8 21.7 %collective-permute-start.3 = (bf16[576,256]{1,0:T(8,128)(2,1)S(1)}, bf16[576,256]{1,0:T(8,128)(2,1)S(1)}, u32[]{:S(2)}, u32[]{:S(2)}) collective-permute-start(bf16[576,256]{1,0:T(8,128)(2,1)S(1)} %attend.1.own_ref), channel_id=1, source_target_pairs={{0,2},{1,5},{2,0},{3,7},{4,6},{5,1},{6,4},{7,3},{8,10},{9,13},{10,... | collective-permute-start | bytes 884744 | tf_op jit(solution)/shard_map/ppermute | solution.py:19
  29.2 21.1 %collective-permute-start.4 = (bf16[576,256]{1,0:T(8,128)(2,1)S(1)}, bf16[576,256]{1,0:T(8,128)(2,1)S(1)}, u32[]{:S(2)}, u32[]{:S(2)}) collective-permute-start(bf16[576,256]{1,0:T(8,128)(2,1)S(1)} %attend.1.own_ref), channel_id=1, source_target_pairs={{0,5},{1,2},{2,7},{3,0},{4,1},{5,6},{6,3},{7,4},{8,13},{9,10},{10,... | collective-permute-start | bytes 884744 | tf_op jit(solution)/shard_map/ppermute | solution.py:19
  35.0 21.7 %copy-start.3 = (s32[64,1]{0,1:T(1,128)S(1)}, s32[64,1]{0,1:T(1,128)}, u32[]{:S(2)}) copy-start(s32[64,1]{0,1:T(1,128)} %param.12) | copy-start | bytes 772
  35.0 38.7 %copy-start = (bf16[64,8192]{1,0:T(8,128)(2,1)S(1)}, bf16[64,8192]{1,0:T(8,128)(2,1)}, u32[]{:S(2)}) copy-start(bf16[64,8192]{1,0:T(8,128)(2,1)} %refs_0_.1) | copy-start | bytes 3145732
  51.5 5.0 %collective-permute-start.10 = (bf16[64,1024]{1,0:T(8,128)(2,1)S(1)}, bf16[64,1024]{1,0:T(8,128)(2,1)S(1)}, u32[]{:S(2)}, u32[]{:S(2)}) collective-permute-start(bf16[64,1024]{1,0:T(8,128)(2,1)S(1)} %get-tuple-element.27), channel_id=1, source_target_pairs={{0,4},{1,3},{2,6},{3,1},{4,0},{5,7},{6,2},{7,5},{8,12},{9,11},{10,... | collective-permute-start | bytes 393224 | tf_op jit(solution)/shard_map/ppermute | solution.py:19
  53.2 21.5 %collective-permute-start.9 = (bf16[512,1024]{1,0:T(8,128)(2,1)S(1)}, bf16[512,1024]{1,0:T(8,128)(2,1)S(1)}, u32[]{:S(2)}, u32[]{:S(2)}) collective-permute-start(bf16[512,1024]{1,0:T(8,128)(2,1)S(1)} %get-tuple-element.25), channel_id=1, source_target_pairs={{0,4},{1,3},{2,6},{3,1},{4,0},{5,7},{6,2},{7,5},{8,12},{9,11},{10,... | collective-permute-start | bytes 3145736 | tf_op jit(solution)/shard_map/ppermute | solution.py:19
  56.6 1.4 %collective-permute-start.11 = (bf16[64,1024]{1,0:T(8,128)(2,1)S(1)}, bf16[64,1024]{1,0:T(8,128)(2,1)S(1)}, u32[]{:S(2)}, u32[]{:S(2)}) collective-permute-start(bf16[64,1024]{1,0:T(8,128)(2,1)S(1)} %divide_convert_fusion), channel_id=1, source_target_pairs={{0,1},{1,0},{2,3},{3,2},{4,5},{5,4},{6,7},{7,6},{8,9},{9,8},{10,11... | collective-permute-start | bytes 393224 | tf_op jit(solution)/shard_map/ppermute | solution.py:19
  58.2 7.3 %collective-permute-start.14 = (bf16[32,2048]{1,0:T(8,128)(2,1)S(1)}, bf16[32,2048]{1,0:T(8,128)(2,1)S(1)}, u32[]{:S(2)}, u32[]{:S(2)}) collective-permute-start(bf16[32,2048]{1,0:T(8,128)(2,1)S(1)} %convolution_convert_fusion), channel_id=1, source_target_pairs={{0,6},{1,7},{2,4},{3,5},{4,2},{5,3},{6,0},{7,1},{8,14},{9,15},{10,... | collective-permute-start | bytes 393224 | tf_op jit(solution)/shard_map/ppermute | solution.py:19
  60.8 12.9 %collective-permute-start.13 = (bf16[32,2048]{1,0:T(8,128)(2,1)S(1)}, bf16[32,2048]{1,0:T(8,128)(2,1)S(1)}, u32[]{:S(2)}, u32[]{:S(2)}) collective-permute-start(bf16[32,2048]{1,0:T(8,128)(2,1)S(1)} %convolution_convert_fusion.1), channel_id=1, source_target_pairs={{0,4},{1,5},{2,6},{3,7},{4,0},{5,1},{6,2},{7,3},{8,12},{9,13},{10,... | collective-permute-start | bytes 393224 | tf_op jit(solution)/shard_map/ppermute | solution.py:19
  61.6 12.2 %collective-permute-start.12 = (bf16[32,2048]{1,0:T(8,128)(2,1)S(1)}, bf16[32,2048]{1,0:T(8,128)(2,1)S(1)}, u32[]{:S(2)}, u32[]{:S(2)}) collective-permute-start(bf16[32,2048]{1,0:T(8,128)(2,1)S(1)} %convolution_convert_fusion.2), channel_id=1, source_target_pairs={{0,2},{1,3},{2,0},{3,1},{4,6},{5,7},{6,4},{7,5},{8,10},{9,11},{10,... | collective-permute-start | bytes 393224 | tf_op jit(solution)/shard_map/ppermute | solution.py:19

commit v2 on v1

--- a/solution.py
+++ b/solution.py
@@ -12,6 +12,7 @@
 BF16 = jnp.bfloat16
 VMEM = pl.BlockSpec(memory_space=pltpu.VMEM)
 HBM = pl.BlockSpec(memory_space=pltpu.HBM)
+ANY = pl.BlockSpec(memory_space=pl.ANY)
 
 
 def move(value, masks):
@@ -38,8 +39,11 @@
 
 
 def kv_kernel(
-    x_ref, w_ref, o_ref, k_ref, v_ref, s_ref, x_buf, cut_ref, w_buf, acc, sems, cut_sems, *, steps, half_bits
+    x_ref, w_ref, o_ref, k_ref, v_ref, s_ref, x_buf, own_ref, *refs, steps, half_bits
 ):
+    side = 1 << half_bits
+    mains, lates = refs[: side - 1], refs[side - 1 : 2 * side - 2]
+    w_buf, acc, sems, cut_sems = refs[2 * side - 2 :]
     depth = x_ref.shape[1] // steps
     copies = []
     for s in range(steps):
@@ -51,11 +55,31 @@
                 for i in range(2)
             ]
         )
-        for copy in copies[-1]:
+    cols = own_ref.shape[1] // side
+    half = cols // 2
+    partner = lax.bitwise_xor(lax.axis_index("head"), 1)
+    cut = []
+
+    def take(m, r, first, size, out, to):
+        start = pl.multiple_of(place(half_bits, m, r, partner) * cols + first, half)
+        cut.append(
+            pltpu.make_async_copy(
+                o_ref.at[:, pl.ds(start, size)], out.at[:, pl.ds(to, size)], cut_sems.at[len(cut)]
+            )
+        )
+
+    for m in range(1, side):
+        for r in range(1, side):
+            take(m, r, 0, cols, mains[m - 1], (r - 1) * cols)
+        take(m, 0, 0, half, mains[m - 1], (side - 1) * cols)
+        take(m, 0, half, half, lates[m - 1], 0)
+    for r in range(side):
+        take(0, r, 0, cols, own_ref, r * cols)
+    for copy in [*copies[0], *copies[1], *cut]:
+        copy.start()
+    for group in copies[2:]:
+        for copy in group:
             copy.start()
-    for_partner = cuts(o_ref, [cut_ref], cut_sems, [(True, 0)], half_bits)
-    for copy in for_partner:
-        copy.start()
     for s in range(steps):
         for copy in copies[s]:
             copy.wait()
@@ -71,12 +95,14 @@
             k_ref[:, of], v_ref[:, of], (((0,), (0,)), ((), ())), preferred_element_type=F32
         )
         s_ref[h] = state.astype(BF16)
-    for copy in for_partner:
+    for copy in cut:
         copy.wait()
 
 
 def q_kernel(x_ref, w_ref, k_ref, v_ref, q_ref, l_ref, w_buf, acc, sems, *, steps):
     depth = x_ref.shape[1] // steps
+    rows = q_ref.shape[0]
+    block = min(rows, 256)
     copies = []
     for s in range(steps):
         at = pl.ds(s * depth, depth)
@@ -85,11 +111,10 @@
     for s in range(steps):
         copies[s].wait()
         at = pl.ds(s * depth, depth)
-        part = dot(x_ref[:, at], w_buf[at])
-        acc[...] = part if s == 0 else acc[...] + part
+        for b in range(0, rows, block):
+            part = dot(x_ref[pl.ds(b, block), at], w_buf[at])
+            acc[pl.ds(b, block)] = part if s == 0 else acc[pl.ds(b, block)] + part
     q_ref[...] = acc[...].astype(BF16)
-    rows = q_ref.shape[0]
-    block = min(rows, 256)
     for h in range(q_ref.shape[1] // HDIM):
         of = pl.ds(h * HDIM, HDIM)
         for b in range(0, rows, block):
@@ -127,66 +152,77 @@
     return pltpu.with_memory_space_constraint(x, pltpu.HBM)
 
 
-def cuts(w_ref, outs, sems, jobs, half_bits):
+def cut_kernel(w_ref, *refs, half_bits):
+    outs, sems = refs[:-1], refs[-1]
     side = 1 << half_bits
     cols = outs[0].shape[1] // side
-    head = lax.axis_index("head")
-    copies = []
-    for n, (partner, m) in enumerate(jobs):
-        for r in range(side):
-            at = place(half_bits, m, r, head ^ 1 if partner else head)
-            copies.append(
-                pltpu.make_async_copy(
-                    w_ref.at[:, block_of(at, cols)],
-                    outs[n].at[:, pl.ds(r * cols, cols)],
-                    sems.at[n, r],
-                )
-            )
-    return copies
-
-
-def cut_kernel(w_ref, *refs, jobs, half_bits):
-    copies = cuts(w_ref, refs[: len(jobs)], refs[-1], jobs, half_bits)
+    copies = [
+        pltpu.make_async_copy(
+            w_ref.at[:, block_of(place(half_bits, m + 1, r), cols)],
+            out.at[:, pl.ds(r * cols, cols)],
+            sems.at[m, r],
+        )
+        for m, out in enumerate(outs)
+        for r in range(side)
+    ]
     for copy in copies:
         copy.start()
     for copy in copies:
         copy.wait()
 
 
-def here_kernel(own_ref, peer_ref, m_ref, x_ref, w_ref, wp_ref, out_ref, x_buf, w_buf, sems, *, half_bits):
+def here_kernel(own_ref, peer_ref, m_ref, x_ref, w_ref, wp_ref, out_ref, e_buf, x_buf, w_buf, sems, *, half_bits):
     side = 1 << half_bits
     cols = out_ref.shape[2]
-    rows = m_ref.shape[1]
+    rows, width = m_ref.shape[1], own_ref.shape[1]
     order = list(range(1, side)) + [0]
     copies = {}
     for r in order:
         at = block_of(place(half_bits, 0, r), cols)
-        copies[r] = pltpu.make_async_copy(w_ref.at[:, at], w_buf.at[r], sems.at[r])
-        copies[r].start()
+        copies[r] = (
+            pltpu.make_async_copy(w_ref.at[:, at], w_buf.at[r, pl.ds(0, width)], sems.at[r, 0]),
+            pltpu.make_async_copy(
+                wp_ref.at[:, pl.ds(r * cols, cols)], w_buf.at[r, pl.ds(width, width)], sems.at[r, 1]
+            ),
+        )
+        for copy in copies[r]:
+            copy.start()
     own = pltpu.make_async_copy(
-        x_ref.at[:, block_of(lax.axis_index("head"), cols)], x_buf, sems.at[side]
+        x_ref.at[:, block_of(lax.axis_index("head"), cols)], x_buf, sems.at[side, 0]
     )
     own.start()
+    e_buf[:, pl.ds(0, width)] = own_ref[...]
+    e_buf[:, pl.ds(width, width)] = peer_ref[...]
+    block = e_buf.shape[0] // 2
     for r in order:
-        part = dot(peer_ref[...], wp_ref[:, pl.ds(r * cols, cols)])
-        copies[r].wait()
-        out_ref[r] = part + dot(own_ref[...], w_buf[r])
+        for copy in copies[r]:
+            copy.wait()
+        for b in range(0, e_buf.shape[0], block):
+            out_ref[r, pl.ds(b, block)] = dot(e_buf[pl.ds(b, block)], w_buf[r])
     own.wait()
     out_ref[0, pl.ds(0, rows)] += x_buf[...].astype(F32)
     out_ref[0, pl.ds(rows, m_ref.shape[0])] += dot(m_ref[...], x_buf[...])
 
 
 def add_kernel(*refs, count, r, rows):
-    ext, w, base = refs[:count], refs[count : 2 * count], refs[2 * count]
-    r_ref, p_ref, buf, sems = refs[2 * count + 1 :]
+    ext, w = refs[: 2 * count], refs[2 * count : 4 * count]
+    late, base = refs[4 * count : -5], refs[-5]
+    r_ref, p_ref, buf, sems = refs[-4:]
     cols = r_ref.shape[1]
     half = cols // 2
     copies = []
     for n, c in enumerate((0, half)):
         at = pl.ds(c, half)
         total = base[r, :, at]
-        for e, b in zip(ext, w):
-            total = total + dot(e[...], b[:, pl.ds(r * cols + c, half)])
+        for i in range(count):
+            total = total + dot(ext[i][...], w[i][:, pl.ds(r * cols + c, half)])
+            if r:
+                part = w[count + i][:, pl.ds((r - 1) * cols + c, half)]
+            elif n:
+                part = late[i][...]
+            else:
+                part = w[count + i][:, pl.ds(w[count + i].shape[1] - half, half)]
+            total = total + dot(ext[count + i][...], part)
         buf[:, at] = total[:rows].astype(buf.dtype)
         copies.append(pltpu.make_async_copy(buf.at[:, at], r_ref.at[:, at], sems.at[n]))
         copies[-1].start()
@@ -250,26 +286,24 @@
     def beside(m):
         return tuple(mask ^ 1 for mask in across(m))
 
-    jobs = [(partner, m) for partner in (False, True) for m in range(1, side)]
     cut = pl.pallas_call(
-        functools.partial(cut_kernel, jobs=jobs, half_bits=half_bits),
-        out_shape=[jax.ShapeDtypeStruct((width, side * cols), BF16)] * len(jobs),
+        functools.partial(cut_kernel, half_bits=half_bits),
+        out_shape=[jax.ShapeDtypeStruct((width, side * cols), BF16)] * (side - 1),
         in_specs=[HBM],
-        out_specs=[VMEM] * len(jobs),
-        scratch_shapes=[pltpu.SemaphoreType.DMA((len(jobs), side))],
+        out_specs=[VMEM] * (side - 1),
+        scratch_shapes=[pltpu.SemaphoreType.DMA((side - 1, side))],
         cost_estimate=pl.CostEstimate(
-            flops=0, bytes_accessed=4 * width * side * cols * len(jobs), transcendentals=0
+            flops=0, bytes_accessed=4 * width * side * cols * (side - 1), transcendentals=0
         ),
         compiler_params=pltpu.CompilerParams(
-            vmem_limit_bytes=2 * width * side * cols * len(jobs) + (1 << 20)
+            vmem_limit_bytes=2 * width * side * cols * (side - 1) + (1 << 20)
         ),
         name="cut",
     )(stay(w_out))
-    w_in = [move(cut[m - 1], along(m)) for m in range(1, side)]
-    w_in_peer = [move(cut[side + m - 2], beside(m)) for m in range(1, side)]
+    w_in = [move(c, along(m + 1)) for m, c in enumerate(cut)]
 
     scratch = pltpu.VMEM
-    keys, values, states, x_here, w_own = pl.pallas_call(
+    keys, values, states, x_here, w_own, *w_beside = pl.pallas_call(
         functools.partial(kv_kernel, steps=steps, half_bits=half_bits),
         out_shape=[
             jax.ShapeDtypeStruct((tokens_here, width), BF16),
@@ -277,14 +311,16 @@
             jax.ShapeDtypeStruct((heads_here, HDIM, HDIM), BF16),
             jax.ShapeDtypeStruct((tokens_here, model_width), BF16),
             jax.ShapeDtypeStruct((width, side * cols), BF16),
+            *[jax.ShapeDtypeStruct((width, side * cols - cols // 2), BF16)] * (side - 1),
+            *[jax.ShapeDtypeStruct((width, cols // 2), BF16)] * (side - 1),
         ],
         in_specs=[HBM] * 3,
-        out_specs=[VMEM] * 5,
+        out_specs=[VMEM] * (2 * side + 3),
         scratch_shapes=[
             scratch((2, model_width, width), BF16),
             scratch((2, tokens_here, width), F32),
             pltpu.SemaphoreType.DMA((3, steps)),
-            pltpu.SemaphoreType.DMA((1, side)),
+            pltpu.SemaphoreType.DMA(((side - 1) * (side + 1) + side,)),
         ],
         cost_estimate=pl.CostEstimate(
             flops=4 * tokens_here * model_width * width,
@@ -294,6 +330,8 @@
         compiler_params=pltpu.CompilerParams(vmem_limit_bytes=14 << 20),
         name="kv",
     )(stay(inputs), stay(w_qkv), stay(w_out))
+    w_main = [move(w, beside(m + 1)) for m, w in enumerate(w_beside[: side - 1])]
+    w_late = [move(w, beside(m + 1)) for m, w in enumerate(w_beside[side - 1 :])]
     w_peer = move(w_own, (1, 1))
 
     earlier = [
@@ -301,7 +339,7 @@
     ]
 
     query, local = pl.pallas_call(
-        functools.partial(q_kernel, steps=steps),
+        functools.partial(q_kernel, steps=4),
         out_shape=[
             jax.ShapeDtypeStruct((tokens_here, width), BF16),
             jax.ShapeDtypeStruct((tokens_here, width), F32),
@@ -311,7 +349,7 @@
         scratch_shapes=[
             scratch((model_width, width), BF16),
             scratch((tokens_here, width), F32),
-            pltpu.SemaphoreType.DMA((steps,)),
+            pltpu.SemaphoreType.DMA((4,)),
         ],
         cost_estimate=pl.CostEstimate(
             flops=2 * tokens_here * model_width * width,
@@ -348,12 +386,13 @@
     base = pl.pallas_call(
         functools.partial(here_kernel, half_bits=half_bits),
         out_shape=jax.ShapeDtypeStruct((side, height, cols), F32),
-        in_specs=[VMEM] * 3 + [HBM, HBM, VMEM],
+        in_specs=[VMEM] * 3 + [HBM, HBM, ANY],
         out_specs=VMEM,
         scratch_shapes=[
+            scratch((height, 2 * width), BF16),
             scratch((tokens_here, cols), BF16),
-            scratch((side, width, cols), BF16),
-            pltpu.SemaphoreType.DMA((side + 1,)),
+            scratch((side, 2 * width, cols), BF16),
+            pltpu.SemaphoreType.DMA((side + 1, 2)),
         ],
         cost_estimate=pl.CostEstimate(
             flops=4 * height * side * cols * width,
@@ -365,16 +404,17 @@
     )(ext, ext_peer, member, stay(inputs), stay(w_out), w_peer)
 
     stacks = [*ext_in, *ext_in_peer]
-    weights = [*w_in, *w_in_peer]
+    weights = [*w_in, *w_main]
 
     def project(r, kind):
+        late = [] if r else w_late
         return pl.pallas_call(
-            functools.partial(add_kernel, count=len(stacks), r=r, rows=tokens_here),
+            functools.partial(add_kernel, count=side - 1, r=r, rows=tokens_here),
             out_shape=[
                 jax.ShapeDtypeStruct((tokens_here, cols), kind),
                 jax.ShapeDtypeStruct((r_dev, cols), kind),
             ],
-            in_specs=[VMEM] * (2 * len(stacks) + 1),
+            in_specs=[VMEM] * (2 * len(stacks) + len(late) + 1),
             out_specs=[HBM, VMEM],
             scratch_shapes=[
                 scratch((tokens_here, cols), kind),
@@ -386,7 +426,7 @@
                 transcendentals=0,
             ),
             compiler_params=pltpu.CompilerParams(vmem_limit_bytes=12 << 20),
-        )(*stacks, *weights, base)
+        )(*stacks, *weights, *late, base)
 
     given = [project(r, BF16) for r in range(1, side)]
     pool_in = [move(p, across(r + 1)) for r, (_, p) in enumerate(given)]

time: 76 us -> 74.8 us (0.984)
  Pallas kernels: 27.8 us -> 24.5 us
  starting transfers between devices: 16.8 us -> 18.6 us
    pallas_call x4, Pallas kernels: 12.1 us -> 9.25 us  [the longest x1 4.47 us: per_device(): pl.pallas_call(functools.partial(q_kernel, steps=4), out_shape=[jax.Shape...]
    ppermute x12 -> x13, starting transfers between devices: 11.2 us -> 13.5 us  [move(): lax.ppermute(value, 'head', [(i, i ^ masks[i % 2]) for i in range(n)])]
    pallas_call x1, Pallas kernels: 4.52 us -> 3.44 us  [per_device(): pl.pallas_call(functools.partial(here_kernel, half_bits=half_bits), out_s...]
    ppermute x12 -> x13, waiting for transfers between devices: 29 us -> 29.3 us  [move(): lax.ppermute(value, 'head', [(i, i ^ masks[i % 2]) for i in range(n)])]
  transfers between devices with their start and end apart: 15 -> 16, of which waited for: 6 -> 5; matrix products, arithmetic and copies ran while one was open for 2% -> 2% of each run, Pallas kernels for 23% -> 19%
where the time goes in v2:
time: 74.8 us; the launch traced here: 74.7 us
  waiting for transfers between devices  29.3 us (39%)
  Pallas kernels  24.5 us (33%)
  starting transfers between devices  18.6 us (25%)
  between operations  0.85 us (1%)
  matrix products  0.8 us (1%)
    ppermute x13, waiting for transfers between devices, move(): lax.ppermute(value, 'head', [(i, i ^ masks[i % 2]) for i in range(n)])  29.3 us
    ppermute x13, starting transfers between devices, move(): lax.ppermute(value, 'head', [(i, i ^ masks[i % 2]) for i in range(n)])  13.5 us
    pallas_call x1, Pallas kernels, per_device(): pl.pallas_call(functools.partial(kv_kernel, steps=steps, half_bits=half_b...  9 us
    ppermute x3, starting transfers between devices, per_device(): lax.ppermute(states, 'seq', [(i, i ^ s) for i in range(n_seq)])  5.1 us
    pallas_call x1, Pallas kernels, per_device(): pl.pallas_call(functools.partial(q_kernel, steps=4), out_shape=[jax.Shape...  4.47 us
    pallas_call x1, Pallas kernels, per_device(): pl.pallas_call(functools.partial(here_kernel, half_bits=half_bits), out_s...  3.44 us
    pallas_call x2, Pallas kernels, project(): pl.pallas_call(functools.partial(add_kernel, count=side - 1, r=r, rows=to...  2.59 us
    pallas_call x1, Pallas kernels, per_device(): pl.pallas_call(functools.partial(cut_kernel, half_bits=half_bits), out_sh...  2.19 us
  transfers between devices with their start and end apart: 16, of which 5 were waited for; matrix products, arithmetic and copies ran while one was open for 2% of the time, Pallas kernels for 19%

profile of v2, /device:TPU:0, one launch (start us, length us, event | category | flops | bytes accessed | tf_op | source)
XLA Modules:
  0.0 74.7 jit_solution(4364191473198144732)
XLA Ops:
  0.6 9.0 %kv.1 = (bf16[512,256]{1,0:T(8,128)(2,1)S(1)}, bf16[512,256]{1,0:T(8,128)(2,1)S(1)}, bf16[2,128,128]{2,1,0:T(8,128)(2,1)S(1)}, bf16[512,8192]{1,0:T(8,128)(2,1)S...) custom-call(bf16[512,8192]{1,0:T(8,128)(2,1)} %x_ref.3, ...), custom_call_target="tpu_custom_call" | custom-call | flops 4294967296 | bytes 16777216 | tf_op jit(solution)/shard_map/kv/pallas_call | solution.py:306
  10.3 2.5 %collective-permute-start = (bf16[2,128,128]{2,1,0:T(8,128)(2,1)S(1)}, bf16[2,128,128]{2,1,0:T(8,128)(2,1)S(1)}, u32[]{:S(2)}, u32[]{:S(2)}) collective-permute-start(bf16[2,128,128]{2,1,0:T(8,128)(2,1)S(1)} %get-tuple-element.20), channel_id=1, source_target_pairs={{0,8},{8,0},{16,24},{24,16},{1,9},{9,1},{17,25},{25,17},{2,10},{10... | collective-permute-start | bytes 196616 | tf_op jit(solution)/shard_map/ppermute | solution.py:338
  12.9 2.6 %collective-permute-start.1 = (bf16[2,128,128]{2,1,0:T(8,128)(2,1)S(1)}, bf16[2,128,128]{2,1,0:T(8,128)(2,1)S(1)}, u32[]{:S(2)}, u32[]{:S(2)}) collective-permute-start(bf16[2,128,128]{2,1,0:T(8,128)(2,1)S(1)} %get-tuple-element.20), channel_id=1, source_target_pairs={{0,16},{8,24},{16,0},{24,8},{1,17},{9,25},{17,1},{25,9},{2,18},{10... | collective-permute-start | bytes 196616 | tf_op jit(solution)/shard_map/ppermute | solution.py:338
  15.4 2.2 %cut.1 = bf16[256,2048]{1,0:T(8,128)(2,1)} custom-call(bf16[256,8192]{1,0:T(8,128)(2,1)} %w_ref.7), custom_call_target="tpu_custom_call" | custom-call | bytes 2097152 | tf_op jit(solution)/shard_map/cut/pallas_call | solution.py:289
  17.6 1.8 %collective-permute-start.5 = (bf16[256,2048]{1,0:T(8,128)(2,1)}, bf16[256,2048]{1,0:T(8,128)(2,1)S(1)}, u32[]{:S(2)}, u32[]{:S(2)}) collective-permute-start(bf16[256,2048]{1,0:T(8,128)(2,1)} %cut.1), channel_id=1, source_target_pairs={{0,2},{1,5},{2,0},{3,7},{4,6},{5,1},{6,4},{7,3},{8,10},{9,13},{10,... | collective-permute-start | bytes 3145736 | tf_op jit(solution)/shard_map/ppermute | solution.py:20
  19.8 4.5 %qlocal.1 = (bf16[512,256]{1,0:T(8,128)(2,1)S(1)}, f32[512,256]{1,0:T(8,128)S(1)}) custom-call(bf16[512,8192]{1,0:T(8,128)(2,1)S(1)} %get-tuple-element.15.x_ref, bf16[3,8192,256]{2,1,0:T(8,128)(2,1)} %w_ref.5, bf16[512,256]{1,0:T(8,128)(2,1)S(1)} %get-tuple-element.16.k_ref, bf16[512,256]{1,0:T(8,128)(2,1)S(1)} %get-tuple-element.17.v_ref), custom_call_target="tpu_custom_call" | custom-call | flops 2147483648 | bytes 4194304 | tf_op jit(solution)/shard_map/qlocal/pallas_call | solution.py:341
  24.3 0.7 attend.1.own_ref
  25.5 1.7 %collective-permute-start.3 = (bf16[576,256]{1,0:T(8,128)(2,1)S(1)}, bf16[576,256]{1,0:T(8,128)(2,1)S(1)}, u32[]{:S(2)}, u32[]{:S(2)}) collective-permute-start(bf16[576,256]{1,0:T(8,128)(2,1)S(1)} %attend.1.own_ref), channel_id=1, source_target_pairs={{0,2},{1,5},{2,0},{3,7},{4,6},{5,1},{6,4},{7,3},{8,10},{9,13},{10,... | collective-permute-start | bytes 884744 | tf_op jit(solution)/shard_map/ppermute | solution.py:20
  27.2 1.2 %collective-permute-start.4 = (bf16[576,256]{1,0:T(8,128)(2,1)S(1)}, bf16[576,256]{1,0:T(8,128)(2,1)S(1)}, u32[]{:S(2)}, u32[]{:S(2)}) collective-permute-start(bf16[576,256]{1,0:T(8,128)(2,1)S(1)} %attend.1.own_ref), channel_id=1, source_target_pairs={{0,5},{1,2},{2,7},{3,0},{4,1},{5,6},{6,3},{7,4},{8,13},{9,10},{10,... | collective-permute-start | bytes 884744 | tf_op jit(solution)/shard_map/ppermute | solution.py:20
  28.4 1.2 %collective-permute-start.7 = (bf16[256,512]{1,0:T(8,128)(2,1)S(1)}, bf16[256,512]{1,0:T(8,128)(2,1)S(1)}, u32[]{:S(2)}, u32[]{:S(2)}) collective-permute-start(bf16[256,512]{1,0:T(8,128)(2,1)S(1)} %get-tuple-element.22), channel_id=1, source_target_pairs={{0,5},{1,2},{2,7},{3,0},{4,1},{5,6},{6,3},{7,4},{8,13},{9,10},{10,... | collective-permute-start | bytes 786440 | tf_op jit(solution)/shard_map/ppermute | solution.py:20
  29.7 3.4 %here.1.refs_5_.refs_4_ = f32[2,576,1024]{2,1,0:T(8,128)S(1)} custom-call(bf16[576,256]{1,0:T(8,128)(2,1)S(1)} %attend.1.own_ref, bf16[576,256]{1,0:T(8,128)(2,1)S(1)} %collective-permute-done.8.peer_ref, bf16[64,512]{1,0:T(8,128)(2,1)S(1)} %fusion.2.refs_2_.m_ref, bf16[512,8192]{1,0:T(8,128)(2,1)} %x_ref.3, bf16[256,8192]{1,0:T(8,128)(2,1)} %w_ref.7, ...), custom_call_target="tpu_custom_call" | custom-call | flops 1207959552 | bytes 2097152 | tf_op jit(solution)/shard_map/here/pallas_call | solution.py:386
  33.1 16.3 %collective-permute-done.3.refs_0_ = bf16[576,256]{1,0:T(8,128)(2,1)S(1)} collective-permute-done((bf16[576,256]{1,0:T(8,128)(2,1)S(1)}, bf16[576,256]{1,0:T(8,128)(2,1)S(1)}, u32[]{:S(2)}, u32[]{:S(2)}) %collective-permute-start.3) | collective-permute-done | bytes 294944 | tf_op jit(solution)/shard_map/ppermute | solution.py:20
  49.4 1.1 %shard_map.87 = (bf16[512,1024]{1,0:T(8,128)(2,1)S(1)}, bf16[64,1024]{1,0:T(8,128)(2,1)S(1)}) custom-call(bf16[576,256]{1,0:T(8,128)(2,1)S(1)} %collective-permute-done.3.refs_0_, bf16[576,256]{1,0:T(8,128)(2,1)S(1)} %collective-permute-done.4.refs_1_, bf16[256,2048]{1,0:T(8,128)(2,1)S(1)} %collective-permute-done.5.refs_2_, ...), custom_call_target="tpu_custom_call" | custom-call | flops 603979776 | bytes 1048576 | tf_op jit(solution)/shard_map/pallas_call | solution.py:411
  50.5 1.4 %collective-permute-start.11 = (bf16[64,1024]{1,0:T(8,128)(2,1)S(1)}, bf16[64,1024]{1,0:T(8,128)(2,1)S(1)}, u32[]{:S(2)}, u32[]{:S(2)}) collective-permute-start(bf16[64,1024]{1,0:T(8,128)(2,1)S(1)} %get-tuple-element.27), channel_id=1, source_target_pairs={{0,4},{1,3},{2,6},{3,1},{4,0},{5,7},{6,2},{7,5},{8,12},{9,11},{10,... | collective-permute-start | bytes 393224 | tf_op jit(solution)/shard_map/ppermute | solution.py:20
  52.1 0.8 %collective-permute-start.10 = (bf16[512,1024]{1,0:T(8,128)(2,1)S(1)}, bf16[512,1024]{1,0:T(8,128)(2,1)S(1)}, u32[]{:S(2)}, u32[]{:S(2)}) collective-permute-start(bf16[512,1024]{1,0:T(8,128)(2,1)S(1)} %get-tuple-element.25), channel_id=1, source_target_pairs={{0,4},{1,3},{2,6},{3,1},{4,0},{5,7},{6,2},{7,5},{8,12},{9,11},{10,... | collective-permute-start | bytes 3145736 | tf_op jit(solution)/shard_map/ppermute | solution.py:20
  52.9 1.5 %shard_map.86 = (f32[512,1024]{1,0:T(8,128)S(1)}, f32[64,1024]{1,0:T(8,128)S(1)}) custom-call(bf16[576,256]{1,0:T(8,128)(2,1)S(1)} %collective-permute-done.3.refs_0_, bf16[576,256]{1,0:T(8,128)(2,1)S(1)} %collective-permute-done.4.refs_1_, bf16[256,2048]{1,0:T(8,128)(2,1)S(1)} %collective-permute-done.5.refs_2_, ...), custom_call_target="tpu_custom_call" | custom-call | flops 603979776 | bytes 1048576 | tf_op jit(solution)/shard_map/pallas_call | solution.py:411
  54.4 1.2 %collective-permute-done.11 = bf16[64,1024]{1,0:T(8,128)(2,1)S(1)} collective-permute-done((bf16[64,1024]{1,0:T(8,128)(2,1)S(1)}, bf16[64,1024]{1,0:T(8,128)(2,1)S(1)}, u32[]{:S(2)}, u32[]{:S(2)}) %collective-permute-start.11) | collective-permute-done | bytes 131104 | tf_op jit(solution)/shard_map/ppermute | solution.py:20
  55.9 1.2 %collective-permute-done.12 = bf16[64,1024]{1,0:T(8,128)(2,1)S(1)} collective-permute-done((bf16[64,1024]{1,0:T(8,128)(2,1)S(1)}, bf16[64,1024]{1,0:T(8,128)(2,1)S(1)}, u32[]{:S(2)}, u32[]{:S(2)}) %collective-permute-start.12) | collective-permute-done | bytes 131104 | tf_op jit(solution)/shard_map/ppermute | solution.py:20
  57.2 3.3 %collective-permute-start.15 = (bf16[32,2048]{1,0:T(8,128)(2,1)S(1)}, bf16[32,2048]{1,0:T(8,128)(2,1)S(1)}, u32[]{:S(2)}, u32[]{:S(2)}) collective-permute-start(bf16[32,2048]{1,0:T(8,128)(2,1)S(1)} %convolution_convert_fusion), channel_id=1, source_target_pairs={{0,6},{1,7},{2,4},{3,5},{4,2},{5,3},{6,0},{7,1},{8,14},{9,15},{10,... | collective-permute-start | bytes 393224 | tf_op jit(solution)/shard_map/ppermute | solution.py:20
  60.7 0.8 %collective-permute-start.14 = (bf16[32,2048]{1,0:T(8,128)(2,1)S(1)}, bf16[32,2048]{1,0:T(8,128)(2,1)S(1)}, u32[]{:S(2)}, u32[]{:S(2)}) collective-permute-start(bf16[32,2048]{1,0:T(8,128)(2,1)S(1)} %convolution_convert_fusion.1), channel_id=1, source_target_pairs={{0,4},{1,5},{2,6},{3,7},{4,0},{5,1},{6,2},{7,3},{8,12},{9,13},{10,... | collective-permute-start | bytes 393224 | tf_op jit(solution)/shard_map/ppermute | solution.py:20
  61.9 3.0 %collective-permute-done.15.refs_4_ = bf16[32,2048]{1,0:T(8,128)(2,1)S(1)} collective-permute-done((bf16[32,2048]{1,0:T(8,128)(2,1)S(1)}, bf16[32,2048]{1,0:T(8,128)(2,1)S(1)}, u32[]{:S(2)}, u32[]{:S(2)}) %collective-permute-start.15) | collective-permute-done | bytes 131104 | tf_op jit(solution)/shard_map/ppermute | solution.py:20
  64.9 7.7 %collective-permute-done.14.refs_3_ = bf16[32,2048]{1,0:T(8,128)(2,1)S(1)} collective-permute-done((bf16[32,2048]{1,0:T(8,128)(2,1)S(1)}, bf16[32,2048]{1,0:T(8,128)(2,1)S(1)}, u32[]{:S(2)}, u32[]{:S(2)}) %collective-permute-start.14) | collective-permute-done | bytes 131104 | tf_op jit(solution)/shard_map/ppermute | solution.py:20
  72.6 1.0 %score.1 = f32[32,64]{1,0:T(8,128)} custom-call(bf16[64,8192]{1,0:T(8,128)(2,1)S(1)} %copy-done, bf16[32,2048]{1,0:T(8,128)(2,1)S(1)} %convolution_convert_fusion.3.refs_1_, bf16[32,2048]{1,0:T(8,128)(2,1)S(1)} %collective-permute-done.13.refs_2_, bf16[32,2048]{1,0:T(8,128)(2,1)S(1)} %collective-permute-done.14.refs_3_, ...), custom_call_target="tpu_custom_call" | custom-call | tf_op jit(solution)/shard_map/score/pallas_call | solution.py:468
  73.6 1.0 %mix.1 = bf16[512,1024]{1,0:T(8,128)(2,1)} custom-call(f32[512,1024]{1,0:T(8,128)S(1)} %get-tuple-element.24.refs_0_, bf16[512,1024]{1,0:T(8,128)(2,1)S(1)} %collective-permute-done.10.refs_1_), custom_call_target="tpu_custom_call" | custom-call | flops 524288 | bytes 4194304 | tf_op jit(solution)/shard_map/mix/pallas_call | solution.py:456
  (35 shorter events, 2.8 us)
Async XLA Ops:
  0.6 18.8 %copy-start.1 = (s32[1,512]{1,0:T(1,128)S(1)}, s32[1,512]{1,0:T(1,128)}, u32[]{:S(2)}) copy-start(s32[1,512]{1,0:T(1,128)} %param.10) | copy-start | bytes 6148
  0.6 18.8 %copy-start.2 = (s32[1,64]{1,0:T(1,128)S(1)}, s32[1,64]{1,0:T(1,128)}, u32[]{:S(2)}) copy-start(s32[1,64]{1,0:T(1,128)} %param.11) | copy-start | bytes 772
  9.7 18.8 %collective-permute-start.9 = (bf16[256,2048]{1,0:T(8,128)(2,1)}, bf16[256,2048]{1,0:T(8,128)(2,1)}, u32[]{:S(2)}, u32[]{:S(2)}) collective-permute-start(bf16[256,2048]{1,0:T(8,128)(2,1)} %get-tuple-element.23), channel_id=1, source_target_pairs={{0,1},{1,0},{2,3},{3,2},{4,5},{5,4},{6,7},{7,6},{8,9},{9,8},{10,11... | collective-permute-start | bytes 3145736 | tf_op jit(solution)/shard_map/ppermute | solution.py:20
  10.3 9.4 %collective-permute-start = (bf16[2,128,128]{2,1,0:T(8,128)(2,1)S(1)}, bf16[2,128,128]{2,1,0:T(8,128)(2,1)S(1)}, u32[]{:S(2)}, u32[]{:S(2)}) collective-permute-start(bf16[2,128,128]{2,1,0:T(8,128)(2,1)S(1)} %get-tuple-element.20), channel_id=1, source_target_pairs={{0,8},{8,0},{16,24},{24,16},{1,9},{9,1},{17,25},{25,17},{2,10},{10... | collective-permute-start | bytes 196616 | tf_op jit(solution)/shard_map/ppermute | solution.py:338
  12.9 11.4 %collective-permute-start.1 = (bf16[2,128,128]{2,1,0:T(8,128)(2,1)S(1)}, bf16[2,128,128]{2,1,0:T(8,128)(2,1)S(1)}, u32[]{:S(2)}, u32[]{:S(2)}) collective-permute-start(bf16[2,128,128]{2,1,0:T(8,128)(2,1)S(1)} %get-tuple-element.20), channel_id=1, source_target_pairs={{0,16},{8,24},{16,0},{24,8},{1,17},{9,25},{17,1},{25,9},{2,18},{10... | collective-permute-start | bytes 196616 | tf_op jit(solution)/shard_map/ppermute | solution.py:338
  15.4 8.8 %collective-permute-start.2 = (bf16[2,128,128]{2,1,0:T(8,128)(2,1)S(1)}, bf16[2,128,128]{2,1,0:T(8,128)(2,1)S(1)}, u32[]{:S(2)}, u32[]{:S(2)}) collective-permute-start(bf16[2,128,128]{2,1,0:T(8,128)(2,1)S(1)} %get-tuple-element.20), channel_id=1, source_target_pairs={{0,24},{8,16},{16,8},{24,0},{1,25},{9,17},{17,9},{25,1},{2,26},{10... | collective-permute-start | bytes 196616 | tf_op jit(solution)/shard_map/ppermute | solution.py:338
  17.6 31.8 %collective-permute-start.5 = (bf16[256,2048]{1,0:T(8,128)(2,1)}, bf16[256,2048]{1,0:T(8,128)(2,1)S(1)}, u32[]{:S(2)}, u32[]{:S(2)}) collective-permute-start(bf16[256,2048]{1,0:T(8,128)(2,1)} %cut.1), channel_id=1, source_target_pairs={{0,2},{1,5},{2,0},{3,7},{4,6},{5,1},{6,4},{7,3},{8,10},{9,13},{10,... | collective-permute-start | bytes 3145736 | tf_op jit(solution)/shard_map/ppermute | solution.py:20
  19.7 29.7 %collective-permute-start.6 = (bf16[256,1536]{1,0:T(8,128)(2,1)}, bf16[256,1536]{1,0:T(8,128)(2,1)S(1)}, u32[]{:S(2)}, u32[]{:S(2)}) collective-permute-start(bf16[256,1536]{1,0:T(8,128)(2,1)} %get-tuple-element.21), channel_id=1, source_target_pairs={{0,5},{1,2},{2,7},{3,0},{4,1},{5,6},{6,3},{7,4},{8,13},{9,10},{10,... | collective-permute-start | bytes 2359304 | tf_op jit(solution)/shard_map/ppermute | solution.py:20
  25.0 2.2 %collective-permute-start.8 = (bf16[576,256]{1,0:T(8,128)(2,1)S(1)}, bf16[576,256]{1,0:T(8,128)(2,1)S(1)}, u32[]{:S(2)}, u32[]{:S(2)}) collective-permute-start(bf16[576,256]{1,0:T(8,128)(2,1)S(1)} %attend.1.own_ref), channel_id=1, source_target_pairs={{0,1},{1,0},{2,3},{3,2},{4,5},{5,4},{6,7},{7,6},{8,9},{9,8},{10,11... | collective-permute-start | bytes 884744 | tf_op jit(solution)/shard_map/ppermute | solution.py:20
  25.5 23.9 %collective-permute-start.3 = (bf16[576,256]{1,0:T(8,128)(2,1)S(1)}, bf16[576,256]{1,0:T(8,128)(2,1)S(1)}, u32[]{:S(2)}, u32[]{:S(2)}) collective-permute-start(bf16[576,256]{1,0:T(8,128)(2,1)S(1)} %attend.1.own_ref), channel_id=1, source_target_pairs={{0,2},{1,5},{2,0},{3,7},{4,6},{5,1},{6,4},{7,3},{8,10},{9,13},{10,... | collective-permute-start | bytes 884744 | tf_op jit(solution)/shard_map/ppermute | solution.py:20
  27.2 22.2 %collective-permute-start.4 = (bf16[576,256]{1,0:T(8,128)(2,1)S(1)}, bf16[576,256]{1,0:T(8,128)(2,1)S(1)}, u32[]{:S(2)}, u32[]{:S(2)}) collective-permute-start(bf16[576,256]{1,0:T(8,128)(2,1)S(1)} %attend.1.own_ref), channel_id=1, source_target_pairs={{0,5},{1,2},{2,7},{3,0},{4,1},{5,6},{6,3},{7,4},{8,13},{9,10},{10,... | collective-permute-start | bytes 884744 | tf_op jit(solution)/shard_map/ppermute | solution.py:20
  28.4 24.4 %collective-permute-start.7 = (bf16[256,512]{1,0:T(8,128)(2,1)S(1)}, bf16[256,512]{1,0:T(8,128)(2,1)S(1)}, u32[]{:S(2)}, u32[]{:S(2)}) collective-permute-start(bf16[256,512]{1,0:T(8,128)(2,1)S(1)} %get-tuple-element.22), channel_id=1, source_target_pairs={{0,5},{1,2},{2,7},{3,0},{4,1},{5,6},{6,3},{7,4},{8,13},{9,10},{10,... | collective-permute-start | bytes 786440 | tf_op jit(solution)/shard_map/ppermute | solution.py:20
  33.1 22.6 %copy-start.3 = (s32[64,1]{0,1:T(1,128)S(1)}, s32[64,1]{0,1:T(1,128)}, u32[]{:S(2)}) copy-start(s32[64,1]{0,1:T(1,128)} %param.12) | copy-start | bytes 772
  33.1 39.5 %copy-start = (bf16[64,8192]{1,0:T(8,128)(2,1)S(1)}, bf16[64,8192]{1,0:T(8,128)(2,1)}, u32[]{:S(2)}) copy-start(bf16[64,8192]{1,0:T(8,128)(2,1)} %refs_0_.1) | copy-start | bytes 3145732
  50.5 5.0 %collective-permute-start.11 = (bf16[64,1024]{1,0:T(8,128)(2,1)S(1)}, bf16[64,1024]{1,0:T(8,128)(2,1)S(1)}, u32[]{:S(2)}, u32[]{:S(2)}) collective-permute-start(bf16[64,1024]{1,0:T(8,128)(2,1)S(1)} %get-tuple-element.27), channel_id=1, source_target_pairs={{0,4},{1,3},{2,6},{3,1},{4,0},{5,7},{6,2},{7,5},{8,12},{9,11},{10,... | collective-permute-start | bytes 393224 | tf_op jit(solution)/shard_map/ppermute | solution.py:20
  52.1 21.5 %collective-permute-start.10 = (bf16[512,1024]{1,0:T(8,128)(2,1)S(1)}, bf16[512,1024]{1,0:T(8,128)(2,1)S(1)}, u32[]{:S(2)}, u32[]{:S(2)}) collective-permute-start(bf16[512,1024]{1,0:T(8,128)(2,1)S(1)} %get-tuple-element.25), channel_id=1, source_target_pairs={{0,4},{1,3},{2,6},{3,1},{4,0},{5,7},{6,2},{7,5},{8,12},{9,11},{10,... | collective-permute-start | bytes 3145736 | tf_op jit(solution)/shard_map/ppermute | solution.py:20
  55.7 1.4 %collective-permute-start.12 = (bf16[64,1024]{1,0:T(8,128)(2,1)S(1)}, bf16[64,1024]{1,0:T(8,128)(2,1)S(1)}, u32[]{:S(2)}, u32[]{:S(2)}) collective-permute-start(bf16[64,1024]{1,0:T(8,128)(2,1)S(1)} %divide_convert_fusion), channel_id=1, source_target_pairs={{0,1},{1,0},{2,3},{3,2},{4,5},{5,4},{6,7},{7,6},{8,9},{9,8},{10,11... | collective-permute-start | bytes 393224 | tf_op jit(solution)/shard_map/ppermute | solution.py:20
  57.2 7.6 %collective-permute-start.15 = (bf16[32,2048]{1,0:T(8,128)(2,1)S(1)}, bf16[32,2048]{1,0:T(8,128)(2,1)S(1)}, u32[]{:S(2)}, u32[]{:S(2)}) collective-permute-start(bf16[32,2048]{1,0:T(8,128)(2,1)S(1)} %convolution_convert_fusion), channel_id=1, source_target_pairs={{0,6},{1,7},{2,4},{3,5},{4,2},{5,3},{6,0},{7,1},{8,14},{9,15},{10,... | collective-permute-start | bytes 393224 | tf_op jit(solution)/shard_map/ppermute | solution.py:20
  60.7 11.9 %collective-permute-start.14 = (bf16[32,2048]{1,0:T(8,128)(2,1)S(1)}, bf16[32,2048]{1,0:T(8,128)(2,1)S(1)}, u32[]{:S(2)}, u32[]{:S(2)}) collective-permute-start(bf16[32,2048]{1,0:T(8,128)(2,1)S(1)} %convolution_convert_fusion.1), channel_id=1, source_target_pairs={{0,4},{1,5},{2,6},{3,7},{4,0},{5,1},{6,2},{7,3},{8,12},{9,13},{10,... | collective-permute-start | bytes 393224 | tf_op jit(solution)/shard_map/ppermute | solution.py:20
  61.7 10.9 %collective-permute-start.13 = (bf16[32,2048]{1,0:T(8,128)(2,1)S(1)}, bf16[32,2048]{1,0:T(8,128)(2,1)S(1)}, u32[]{:S(2)}, u32[]{:S(2)}) collective-permute-start(bf16[32,2048]{1,0:T(8,128)(2,1)S(1)} %convolution_convert_fusion.2), channel_id=1, source_target_pairs={{0,2},{1,3},{2,0},{3,1},{4,6},{5,7},{6,4},{7,5},{8,10},{9,11},{10,... | collective-permute-start | bytes 393224 | tf_op jit(solution)/shard_map/ppermute | solution.py:20

commit v3 on v2

--- a/solution.py
+++ b/solution.py
@@ -38,12 +38,29 @@
     return pl.ds(pl.multiple_of(index * size, size), size)
 
 
+def cutter(w_ref, sems, cols, half_bits, partner):
+    head = lax.axis_index("head")
+    head = lax.bitwise_xor(head, 1) if partner else head
+    copies = []
+
+    def take(m, r, first, size, out, to):
+        start = place(half_bits, m, r, head) * cols + first
+        start = pl.multiple_of(start, cols // 2)
+        copies.append(
+            pltpu.make_async_copy(
+                w_ref.at[:, pl.ds(start, size)], out.at[:, pl.ds(to, size)], sems.at[len(copies)]
+            )
+        )
+
+    return copies, take
+
+
 def kv_kernel(
-    x_ref, w_ref, o_ref, k_ref, v_ref, s_ref, x_buf, own_ref, *refs, steps, half_bits
+    x_ref, w_ref, o_ref, k_ref, v_ref, s_ref, x_buf, *refs, steps, half_bits, cols
 ):
     side = 1 << half_bits
-    mains, lates = refs[: side - 1], refs[side - 1 : 2 * side - 2]
-    w_buf, acc, sems, cut_sems = refs[2 * side - 2 :]
+    mains = refs[: side - 1]
+    w_buf, acc, sems, cut_sems = refs[side - 1 :]
     depth = x_ref.shape[1] // steps
     copies = []
     for s in range(steps):
@@ -55,29 +72,12 @@
                 for i in range(2)
             ]
         )
-    cols = own_ref.shape[1] // side
-    half = cols // 2
-    partner = lax.bitwise_xor(lax.axis_index("head"), 1)
-    cut = []
-
-    def take(m, r, first, size, out, to):
-        start = pl.multiple_of(place(half_bits, m, r, partner) * cols + first, half)
-        cut.append(
-            pltpu.make_async_copy(
-                o_ref.at[:, pl.ds(start, size)], out.at[:, pl.ds(to, size)], cut_sems.at[len(cut)]
-            )
-        )
-
+    cut, take = cutter(o_ref, cut_sems, cols, half_bits, True)
     for m in range(1, side):
         for r in range(1, side):
             take(m, r, 0, cols, mains[m - 1], (r - 1) * cols)
-        take(m, 0, 0, half, mains[m - 1], (side - 1) * cols)
-        take(m, 0, half, half, lates[m - 1], 0)
-    for r in range(side):
-        take(0, r, 0, cols, own_ref, r * cols)
-    for copy in [*copies[0], *copies[1], *cut]:
-        copy.start()
-    for group in copies[2:]:
+        take(m, 0, 0, cols // 2, mains[m - 1], (side - 1) * cols)
+    for group in (*copies[:-2], cut, *copies[-2:]):
         for copy in group:
             copy.start()
     for s in range(steps):
@@ -99,7 +99,12 @@
         copy.wait()
 
 
-def q_kernel(x_ref, w_ref, k_ref, v_ref, q_ref, l_ref, w_buf, acc, sems, *, steps):
+def q_kernel(
+    x_ref, w_ref, k_ref, v_ref, o_ref, q_ref, l_ref, own_ref, *refs, steps, half_bits, cols
+):
+    side = 1 << half_bits
+    lates = refs[: side - 1]
+    w_buf, acc, sems, cut_sems = refs[side - 1 :]
     depth = x_ref.shape[1] // steps
     rows = q_ref.shape[0]
     block = min(rows, 256)
@@ -108,6 +113,13 @@
         at = pl.ds(s * depth, depth)
         copies.append(pltpu.make_async_copy(w_ref.at[0, at], w_buf.at[at], sems.at[s]))
         copies[-1].start()
+    cut, take = cutter(o_ref, cut_sems, cols, half_bits, True)
+    for r in range(side):
+        take(0, r, 0, cols, own_ref, r * cols)
+    for m in range(1, side):
+        take(m, 0, cols // 2, cols // 2, lates[m - 1], 0)
+    for copy in cut:
+        copy.start()
     for s in range(steps):
         copies[s].wait()
         at = pl.ds(s * depth, depth)
@@ -129,12 +141,13 @@
             s = lax.broadcasted_iota(jnp.int32, sc.shape, 1)
             sc = jnp.where(t >= s, sc, 0.0).astype(BF16)
             l_ref[pl.ds(b, block), of] = dot(sc, v_ref[pl.ds(0, seen), of])
+    for copy in cut:
+        copy.wait()
 
 
 def attend_kernel(*refs, others):
-    q_ref, l_ref, m_ref = refs[:3]
-    states, out_ref = refs[3 : 3 + others], refs[3 + others]
-    rows = q_ref.shape[0]
+    q_ref, l_ref = refs[:2]
+    states, out_ref = refs[2 : 2 + others], refs[2 + others]
     seq = lax.axis_index("seq")
     for h in range(q_ref.shape[1] // HDIM):
         of = pl.ds(h * HDIM, HDIM)
@@ -143,9 +156,7 @@
             prefix = prefix + jnp.where((seq ^ (i + 1)) < seq, state[h].astype(F32), 0.0)
         summed = l_ref[:, of] + dot(q_ref[:, of], prefix.astype(BF16))
         scale = lax.rsqrt(jnp.mean(summed * summed, axis=-1, keepdims=True) + 1e-05)
-        attn = (summed * scale).astype(BF16)
-        out_ref[pl.ds(0, rows), of] = attn
-        out_ref[pl.ds(rows, m_ref.shape[0]), of] = dot(m_ref[...], attn).astype(BF16)
+        out_ref[:, of] = (summed * scale).astype(BF16)
 
 
 def stay(x):
@@ -191,8 +202,10 @@
         x_ref.at[:, block_of(lax.axis_index("head"), cols)], x_buf, sems.at[side, 0]
     )
     own.start()
-    e_buf[:, pl.ds(0, width)] = own_ref[...]
-    e_buf[:, pl.ds(width, width)] = peer_ref[...]
+    for i, ref in enumerate((own_ref, peer_ref)):
+        at = pl.ds(i * width, width)
+        e_buf[pl.ds(0, rows), at] = ref[...]
+        e_buf[pl.ds(rows, m_ref.shape[0]), at] = dot(m_ref[...], ref[...]).astype(BF16)
     block = e_buf.shape[0] // 2
     for r in order:
         for copy in copies[r]:
@@ -206,27 +219,30 @@
 
 def add_kernel(*refs, count, r, rows):
     ext, w = refs[: 2 * count], refs[2 * count : 4 * count]
-    late, base = refs[4 * count : -5], refs[-5]
+    late, m_ref, base = refs[4 * count : -6], refs[-6], refs[-5]
     r_ref, p_ref, buf, sems = refs[-4:]
     cols = r_ref.shape[1]
     half = cols // 2
+    pooled = [dot(m_ref[...], e[...]).astype(BF16) for e in ext]
     copies = []
     for n, c in enumerate((0, half)):
         at = pl.ds(c, half)
-        total = base[r, :, at]
-        for i in range(count):
-            total = total + dot(ext[i][...], w[i][:, pl.ds(r * cols + c, half)])
-            if r:
-                part = w[count + i][:, pl.ds((r - 1) * cols + c, half)]
+        total, few = base[r, pl.ds(0, rows), at], base[r, pl.ds(rows, m_ref.shape[0]), at]
+        for i in range(2 * count):
+            if i < count:
+                part = w[i][:, pl.ds(r * cols + c, half)]
+            elif r:
+                part = w[i][:, pl.ds((r - 1) * cols + c, half)]
             elif n:
-                part = late[i][...]
+                part = late[i - count][...]
             else:
-                part = w[count + i][:, pl.ds(w[count + i].shape[1] - half, half)]
-            total = total + dot(ext[count + i][...], part)
-        buf[:, at] = total[:rows].astype(buf.dtype)
+                part = w[i][:, pl.ds(w[i].shape[1] - half, half)]
+            total = total + dot(ext[i][...], part)
+            few = few + dot(pooled[i], part)
+        p_ref[:, at] = few.astype(p_ref.dtype)
+        buf[:, at] = total.astype(buf.dtype)
         copies.append(pltpu.make_async_copy(buf.at[:, at], r_ref.at[:, at], sems.at[n]))
         copies[-1].start()
-        p_ref[:, at] = total[rows:].astype(p_ref.dtype)
     for copy in copies:
         copy.wait()
 
@@ -247,12 +263,12 @@
         copy.wait()
 
 
-def score_kernel(*refs):
-    c_ref, slots, out_ref = refs[0], refs[1:-1], refs[-1]
+def score_kernel(c_ref, *refs, steps, add):
+    slots, out_ref = refs[: len(steps)], refs[-1]
     cols = slots[0].shape[1] // 2
     head = lax.axis_index("head")
-    total = jnp.zeros(out_ref.shape, F32)
-    for j, rows in enumerate(slots):
+    total = refs[-2][...] if add else jnp.zeros(out_ref.shape, F32)
+    for j, rows in zip(steps, slots):
         for c in range(2):
             total = total + lax.dot_general(
                 rows[:, pl.ds(c * cols, cols)],
@@ -303,24 +319,22 @@
     w_in = [move(c, along(m + 1)) for m, c in enumerate(cut)]
 
     scratch = pltpu.VMEM
-    keys, values, states, x_here, w_own, *w_beside = pl.pallas_call(
-        functools.partial(kv_kernel, steps=steps, half_bits=half_bits),
+    keys, values, states, x_here, *w_beside = pl.pallas_call(
+        functools.partial(kv_kernel, steps=steps, half_bits=half_bits, cols=cols),
         out_shape=[
             jax.ShapeDtypeStruct((tokens_here, width), BF16),
             jax.ShapeDtypeStruct((tokens_here, width), BF16),
             jax.ShapeDtypeStruct((heads_here, HDIM, HDIM), BF16),
             jax.ShapeDtypeStruct((tokens_here, model_width), BF16),
-            jax.ShapeDtypeStruct((width, side * cols), BF16),
             *[jax.ShapeDtypeStruct((width, side * cols - cols // 2), BF16)] * (side - 1),
-            *[jax.ShapeDtypeStruct((width, cols // 2), BF16)] * (side - 1),
         ],
         in_specs=[HBM] * 3,
-        out_specs=[VMEM] * (2 * side + 3),
+        out_specs=[VMEM] * (side + 3),
         scratch_shapes=[
             scratch((2, model_width, width), BF16),
             scratch((2, tokens_here, width), F32),
             pltpu.SemaphoreType.DMA((3, steps)),
-            pltpu.SemaphoreType.DMA(((side - 1) * (side + 1) + side,)),
+            pltpu.SemaphoreType.DMA(((side - 1) * side,)),
         ],
         cost_estimate=pl.CostEstimate(
             flops=4 * tokens_here * model_width * width,
@@ -330,26 +344,27 @@
         compiler_params=pltpu.CompilerParams(vmem_limit_bytes=14 << 20),
         name="kv",
     )(stay(inputs), stay(w_qkv), stay(w_out))
-    w_main = [move(w, beside(m + 1)) for m, w in enumerate(w_beside[: side - 1])]
-    w_late = [move(w, beside(m + 1)) for m, w in enumerate(w_beside[side - 1 :])]
-    w_peer = move(w_own, (1, 1))
+    w_main = [move(w, beside(m + 1)) for m, w in enumerate(w_beside)]
 
     earlier = [
         lax.ppermute(states, "seq", [(i, i ^ s) for i in range(n_seq)]) for s in range(1, n_seq)
     ]
 
-    query, local = pl.pallas_call(
-        functools.partial(q_kernel, steps=4),
+    query, local, w_own, *w_rest = pl.pallas_call(
+        functools.partial(q_kernel, steps=4, half_bits=half_bits, cols=cols),
         out_shape=[
             jax.ShapeDtypeStruct((tokens_here, width), BF16),
             jax.ShapeDtypeStruct((tokens_here, width), F32),
+            jax.ShapeDtypeStruct((width, side * cols), BF16),
+            *[jax.ShapeDtypeStruct((width, cols // 2), BF16)] * (side - 1),
         ],
-        in_specs=[VMEM, HBM, VMEM, VMEM],
-        out_specs=[VMEM] * 2,
+        in_specs=[VMEM, HBM, VMEM, VMEM, HBM],
+        out_specs=[VMEM] * (side + 2),
         scratch_shapes=[
             scratch((model_width, width), BF16),
             scratch((tokens_here, width), F32),
             pltpu.SemaphoreType.DMA((4,)),
+            pltpu.SemaphoreType.DMA((2 * side - 1,)),
         ],
         cost_estimate=pl.CostEstimate(
             flops=2 * tokens_here * model_width * width,
@@ -358,7 +373,9 @@
         ),
         compiler_params=pltpu.CompilerParams(vmem_limit_bytes=10 << 20),
         name="qlocal",
-    )(x_here, stay(w_qkv), keys, values)
+    )(x_here, stay(w_qkv), keys, values, stay(w_out))
+    w_late = [move(w, beside(m + 1)) for m, w in enumerate(w_rest)]
+    w_peer = move(w_own, (1, 1))
 
     turn_row = turn_ids[0]
     pick_row = picked[0]
@@ -371,12 +388,12 @@
 
     ext = pl.pallas_call(
         functools.partial(attend_kernel, others=n_seq - 1),
-        out_shape=jax.ShapeDtypeStruct((tokens_here + r_dev, width), BF16),
-        in_specs=[VMEM] * (3 + n_seq - 1),
+        out_shape=jax.ShapeDtypeStruct((tokens_here, width), BF16),
+        in_specs=[VMEM] * (2 + n_seq - 1),
         out_specs=VMEM,
         compiler_params=pltpu.CompilerParams(vmem_limit_bytes=4 << 20),
         name="attend",
-    )(query, local, member, *earlier)
+    )(query, local, *earlier)
 
     ext_in = [move(ext, along(m)) for m in range(1, side)]
     ext_in_peer = [move(ext, beside(m)) for m in range(1, side)]
@@ -414,7 +431,7 @@
                 jax.ShapeDtypeStruct((tokens_here, cols), kind),
                 jax.ShapeDtypeStruct((r_dev, cols), kind),
             ],
-            in_specs=[VMEM] * (2 * len(stacks) + len(late) + 1),
+            in_specs=[VMEM] * (2 * len(stacks) + len(late) + 2),
             out_specs=[HBM, VMEM],
             scratch_shapes=[
                 scratch((tokens_here, cols), kind),
@@ -426,7 +443,7 @@
                 transcendentals=0,
             ),
             compiler_params=pltpu.CompilerParams(vmem_limit_bytes=12 << 20),
-        )(*stacks, *weights, *late, base)
+        )(*stacks, *weights, *late, member, base)
 
     given = [project(r, BF16) for r in range(1, side)]
     pool_in = [move(p, across(r + 1)) for r, (_, p) in enumerate(given)]
@@ -465,14 +482,18 @@
         compiler_params=pltpu.CompilerParams(vmem_limit_bytes=4 << 20),
         name="mix",
     )(rows_here, *rows_in)
-    scores = pl.pallas_call(
-        score_kernel,
-        out_shape=jax.ShapeDtypeStruct((cap_rows, candidates.shape[0]), F32),
-        in_specs=[VMEM] * (1 + chips),
-        out_specs=VMEM,
-        compiler_params=pltpu.CompilerParams(vmem_limit_bytes=2 << 20),
-        name="score",
-    )(candidates, *found)
+
+    def score(steps, *before):
+        return pl.pallas_call(
+            functools.partial(score_kernel, steps=steps, add=bool(before)),
+            out_shape=jax.ShapeDtypeStruct((cap_rows, candidates.shape[0]), F32),
+            in_specs=[VMEM] * (1 + len(steps) + len(before)),
+            out_specs=VMEM,
+            compiler_params=pltpu.CompilerParams(vmem_limit_bytes=2 << 20),
+            name="score" if before else "score_first",
+        )(candidates, *[found[j] for j in steps], *before)
+
+    scores = score(range(1, chips), score(range(1)))
     return (mixed, scores)
 
 

time: 74.8 us -> 73.6 us (0.984)
  waiting for transfers between devices: 29.3 us -> 24.3 us
  starting transfers between devices: 18.6 us -> 22.9 us
    ppermute x13, waiting for transfers between devices: 29.3 us -> 22.1 us  [move(): lax.ppermute(value, 'head', [(i, i ^ masks[i % 2]) for i in range(n)])]
    ppermute x3, starting transfers between devices: 5.1 us -> 8.94 us  [per_device(): lax.ppermute(states, 'seq', [(i, i ^ s) for i in range(n_seq)])]
    ppermute x3, waiting for transfers between devices: 0.01 us -> 2.24 us  [per_device(): lax.ppermute(states, 'seq', [(i, i ^ s) for i in range(n_seq)])]
    pallas_call x2 -> x3, Pallas kernels: 5.49 us -> 6.64 us  [the longest x1 5.48 us: per_device(): pl.pallas_call(functools.partial(q_kernel, steps=4, half_bits=half_bits,...]
    pallas_call x1, Pallas kernels: 2.19 us -> 1.22 us  [per_device(): pl.pallas_call(functools.partial(cut_kernel, half_bits=half_bits), out_sh...]
  transfers between devices with their start and end apart: 16 -> 16, of which waited for: 5 -> 6; matrix products, arithmetic and copies ran while one was open for 2% -> 2% of each run, Pallas kernels for 19% -> 12%
where the time goes in v3:
time: 73.6 us; the launch traced here: 73.4 us
  waiting for transfers between devices  24.3 us (33%)
  Pallas kernels  24 us (33%)
  starting transfers between devices  22.9 us (31%)
  between operations  0.87 us (1%)
  matrix products  0.79 us (1%)
    ppermute x13, waiting for transfers between devices, move(): lax.ppermute(value, 'head', [(i, i ^ masks[i % 2]) for i in range(n)])  22.1 us
    ppermute x13, starting transfers between devices, move(): lax.ppermute(value, 'head', [(i, i ^ masks[i % 2]) for i in range(n)])  14 us
    ppermute x3, starting transfers between devices, per_device(): lax.ppermute(states, 'seq', [(i, i ^ s) for i in range(n_seq)])  8.94 us
    pallas_call x1, Pallas kernels, per_device(): pl.pallas_call(functools.partial(kv_kernel, steps=steps, half_bits=half_b...  8.34 us
    pallas_call x1, Pallas kernels, per_device(): pl.pallas_call(functools.partial(q_kernel, steps=4, half_bits=half_bits,...  5.48 us
    pallas_call x1, Pallas kernels, per_device(): pl.pallas_call(functools.partial(here_kernel, half_bits=half_bits), out_s...  3.44 us
    pallas_call x2, Pallas kernels, project(): pl.pallas_call(functools.partial(add_kernel, count=side - 1, r=r, rows=to...  2.89 us
    ppermute x3, waiting for transfers between devices, per_device(): lax.ppermute(states, 'seq', [(i, i ^ s) for i in range(n_seq)])  2.24 us
  transfers between devices with their start and end apart: 16, of which 6 were waited for; matrix products, arithmetic and copies ran while one was open for 2% of the time, Pallas kernels for 12%

profile of v3, /device:TPU:0, one launch (start us, length us, event | category | flops | bytes accessed | tf_op | source)
XLA Modules:
  0.0 73.4 jit_solution(487159089830044439)
XLA Ops:
  0.6 8.3 %kv.1 = (bf16[512,256]{1,0:T(8,128)(2,1)S(1)}, bf16[512,256]{1,0:T(8,128)(2,1)S(1)}, bf16[2,128,128]{2,1,0:T(8,128)(2,1)S(1)}, bf16[512,8192]{1,0:T(8,128)(2,1)S(1)}, bf16[256,1536]{1,0:T(8,128)(2,1)}) custom-call(bf16[512,8192]{1,0:T(8,128)(2,1)} %x_ref.3, bf16[3,8192,256]{2,1,0:T(8,128)(2,1)} %w_ref.5, bf16[256,8192]{1,0:T(8,128)(2,1)} %w_ref.7), custom_call_target="tpu_custom_call" | custom-call | flops 4294967296 | bytes 16777216 | tf_op jit(solution)/shard_map/kv/pallas_call | solution.py:322
  9.0 5.5 %qlocal.1 = (bf16[512,256]{1,0:T(8,128)(2,1)S(1)}, f32[512,256]{1,0:T(8,128)S(1)}, bf16[256,2048]{1,0:T(8,128)(2,1)}, bf16[256,512]{1,0:T(8,128)(2,1)S(1)}) custom-call(bf16[512,8192]{1,0:T(8,128)(2,1)S(1)} %get-tuple-element.15.x_ref, bf16[3,8192,256]{2,1,0:T(8,128)(2,1)} %w_ref.5, bf16[512,256]{1,0:T(8,128)(2,1)S(1)} %get-tuple-element.16.k_ref, ...), custom_call_target="tpu_custom_call" | custom-call | flops 2147483648 | bytes 4194304 | tf_op jit(solution)/shard_map/qlocal/pallas_call | solution.py:353
  14.5 0.5 collective-permute-start.9
  15.1 1.2 %cut.1 = bf16[256,2048]{1,0:T(8,128)(2,1)S(1)} custom-call(bf16[256,8192]{1,0:T(8,128)(2,1)} %w_ref.7), custom_call_target="tpu_custom_call" | custom-call | bytes 2097152 | tf_op jit(solution)/shard_map/cut/pallas_call | solution.py:305
  16.3 2.6 %collective-permute-start.5 = (bf16[256,2048]{1,0:T(8,128)(2,1)S(1)}, bf16[256,2048]{1,0:T(8,128)(2,1)S(1)}, u32[]{:S(2)}, u32[]{:S(2)}) collective-permute-start(bf16[256,2048]{1,0:T(8,128)(2,1)S(1)} %cut.1), channel_id=1, source_target_pairs={{0,2},{1,5},{2,0},{3,7},{4,6},{5,1},{6,4},{7,3},{8,10},{9,13},{10,... | collective-permute-start | bytes 3145736 | tf_op jit(solution)/shard_map/ppermute | solution.py:20
  19.0 1.8 %collective-permute-start = (bf16[2,128,128]{2,1,0:T(8,128)(2,1)S(1)}, bf16[2,128,128]{2,1,0:T(8,128)(2,1)S(1)}, u32[]{:S(2)}, u32[]{:S(2)}) collective-permute-start(bf16[2,128,128]{2,1,0:T(8,128)(2,1)S(1)} %get-tuple-element.20), channel_id=1, source_target_pairs={{0,8},{8,0},{16,24},{24,16},{1,9},{9,1},{17,25},{25,17},{2,10},{10... | collective-permute-start | bytes 196616 | tf_op jit(solution)/shard_map/ppermute | solution.py:350
  20.8 2.6 %collective-permute-start.1 = (bf16[2,128,128]{2,1,0:T(8,128)(2,1)S(1)}, bf16[2,128,128]{2,1,0:T(8,128)(2,1)S(1)}, u32[]{:S(2)}, u32[]{:S(2)}) collective-permute-start(bf16[2,128,128]{2,1,0:T(8,128)(2,1)S(1)} %get-tuple-element.20), channel_id=1, source_target_pairs={{0,16},{8,24},{16,0},{24,8},{1,17},{9,25},{17,1},{25,9},{2,18},{10... | collective-permute-start | bytes 196616 | tf_op jit(solution)/shard_map/ppermute | solution.py:350
  23.4 4.6 %collective-permute-start.2 = (bf16[2,128,128]{2,1,0:T(8,128)(2,1)S(1)}, bf16[2,128,128]{2,1,0:T(8,128)(2,1)S(1)}, u32[]{:S(2)}, u32[]{:S(2)}) collective-permute-start(bf16[2,128,128]{2,1,0:T(8,128)(2,1)S(1)} %get-tuple-element.20), channel_id=1, source_target_pairs={{0,24},{8,16},{16,8},{24,0},{1,25},{9,17},{17,9},{25,1},{2,26},{10... | collective-permute-start | bytes 196616 | tf_op jit(solution)/shard_map/ppermute | solution.py:350
  28.0 2.2 %collective-permute-done.2.refs_4_ = bf16[2,128,128]{2,1,0:T(8,128)(2,1)S(1)} collective-permute-done((bf16[2,128,128]{2,1,0:T(8,128)(2,1)S(1)}, bf16[2,128,128]{2,1,0:T(8,128)(2,1)S(1)}, u32[]{:S(2)}, u32[]{:S(2)}) %collective-permute-start.2) | collective-permute-done | bytes 65568 | tf_op jit(solution)/shard_map/ppermute | solution.py:350
  30.9 1.6 %collective-permute-start.3 = (bf16[512,256]{1,0:T(8,128)(2,1)S(1)}, bf16[512,256]{1,0:T(8,128)(2,1)S(1)}, u32[]{:S(2)}, u32[]{:S(2)}) collective-permute-start(bf16[512,256]{1,0:T(8,128)(2,1)S(1)} %attend.1.own_ref), channel_id=1, source_target_pairs={{0,2},{1,5},{2,0},{3,7},{4,6},{5,1},{6,4},{7,3},{8,10},{9,13},{10,... | collective-permute-start | bytes 786440 | tf_op jit(solution)/shard_map/ppermute | solution.py:20
  32.5 1.0 %collective-permute-start.4 = (bf16[512,256]{1,0:T(8,128)(2,1)S(1)}, bf16[512,256]{1,0:T(8,128)(2,1)S(1)}, u32[]{:S(2)}, u32[]{:S(2)}) collective-permute-start(bf16[512,256]{1,0:T(8,128)(2,1)S(1)} %attend.1.own_ref), channel_id=1, source_target_pairs={{0,5},{1,2},{2,7},{3,0},{4,1},{5,6},{6,3},{7,4},{8,13},{9,10},{10,... | collective-permute-start | bytes 786440 | tf_op jit(solution)/shard_map/ppermute | solution.py:20
  33.6 1.5 %collective-permute-start.7 = (bf16[256,512]{1,0:T(8,128)(2,1)}, bf16[256,512]{1,0:T(8,128)(2,1)S(1)}, u32[]{:S(2)}, u32[]{:S(2)}) collective-permute-start(bf16[256,512]{1,0:T(8,128)(2,1)} %copy-done.1), channel_id=1, source_target_pairs={{0,5},{1,2},{2,7},{3,0},{4,1},{5,6},{6,3},{7,4},{8,13},{9,10},{10,... | collective-permute-start | bytes 786440 | tf_op jit(solution)/shard_map/ppermute | solution.py:20
  35.1 3.4 %here.1.refs_6_.refs_5_ = f32[2,576,1024]{2,1,0:T(8,128)S(1)} custom-call(bf16[512,256]{1,0:T(8,128)(2,1)S(1)} %attend.1.own_ref, bf16[512,256]{1,0:T(8,128)(2,1)S(1)} %collective-permute-done.8.peer_ref, bf16[64,512]{1,0:T(8,128)(2,1)S(1)} %fusion.2.m_ref.refs_5_.refs_4_, bf16[512,8192]{1,0:T(8,128)(2,1)} %x_ref.3, bf16[256,8192]{1,0:T(8,128)(2,1)} %w_ref.7, ...), custom_call_target="tpu_custom_call" | custom-call | flops 1207959552 | bytes 2097152 | tf_op jit(solution)/shard_map/here/pallas_call | solution.py:403
  38.6 9.2 %collective-permute-done.3.refs_0_ = bf16[512,256]{1,0:T(8,128)(2,1)S(1)} collective-permute-done((bf16[512,256]{1,0:T(8,128)(2,1)S(1)}, bf16[512,256]{1,0:T(8,128)(2,1)S(1)}, u32[]{:S(2)}, u32[]{:S(2)}) %collective-permute-start.3) | collective-permute-done | bytes 262176 | tf_op jit(solution)/shard_map/ppermute | solution.py:20
  47.8 1.3 %shard_map.87 = (bf16[512,1024]{1,0:T(8,128)(2,1)S(1)}, bf16[64,1024]{1,0:T(8,128)(2,1)S(1)}) custom-call(bf16[512,256]{1,0:T(8,128)(2,1)S(1)} %collective-permute-done.3.refs_0_, bf16[512,256]{1,0:T(8,128)(2,1)S(1)} %collective-permute-done.4.refs_1_, bf16[256,2048]{1,0:T(8,128)(2,1)S(1)} %collective-permute-done.5.refs_2_, ...), custom_call_target="tpu_custom_call" | custom-call | flops 603979776 | bytes 1048576 | tf_op jit(solution)/shard_map/pallas_call | solution.py:428
  49.1 1.7 %collective-permute-start.11 = (bf16[64,1024]{1,0:T(8,128)(2,1)S(1)}, bf16[64,1024]{1,0:T(8,128)(2,1)S(1)}, u32[]{:S(2)}, u32[]{:S(2)}) collective-permute-start(bf16[64,1024]{1,0:T(8,128)(2,1)S(1)} %get-tuple-element.27), channel_id=1, source_target_pairs={{0,4},{1,3},{2,6},{3,1},{4,0},{5,7},{6,2},{7,5},{8,12},{9,11},{10,... | collective-permute-start | bytes 393224 | tf_op jit(solution)/shard_map/ppermute | solution.py:20
  51.4 1.6 %shard_map.86 = (f32[512,1024]{1,0:T(8,128)S(1)}, f32[64,1024]{1,0:T(8,128)S(1)}) custom-call(bf16[512,256]{1,0:T(8,128)(2,1)S(1)} %collective-permute-done.3.refs_0_, bf16[512,256]{1,0:T(8,128)(2,1)S(1)} %collective-permute-done.4.refs_1_, bf16[256,2048]{1,0:T(8,128)(2,1)S(1)} %collective-permute-done.5.refs_2_, ...), custom_call_target="tpu_custom_call" | custom-call | flops 603979776 | bytes 1048576 | tf_op jit(solution)/shard_map/pallas_call | solution.py:428
  53.0 1.1 %collective-permute-done.11 = bf16[64,1024]{1,0:T(8,128)(2,1)S(1)} collective-permute-done((bf16[64,1024]{1,0:T(8,128)(2,1)S(1)}, bf16[64,1024]{1,0:T(8,128)(2,1)S(1)}, u32[]{:S(2)}, u32[]{:S(2)}) %collective-permute-start.11) | collective-permute-done | bytes 131104 | tf_op jit(solution)/shard_map/ppermute | solution.py:20
  54.4 1.2 %collective-permute-done.12 = bf16[64,1024]{1,0:T(8,128)(2,1)S(1)} collective-permute-done((bf16[64,1024]{1,0:T(8,128)(2,1)S(1)}, bf16[64,1024]{1,0:T(8,128)(2,1)S(1)}, u32[]{:S(2)}, u32[]{:S(2)}) %collective-permute-start.12) | collective-permute-done | bytes 131104 | tf_op jit(solution)/shard_map/ppermute | solution.py:20
  55.8 3.6 %collective-permute-start.15 = (bf16[32,2048]{1,0:T(8,128)(2,1)S(1)}, bf16[32,2048]{1,0:T(8,128)(2,1)S(1)}, u32[]{:S(2)}, u32[]{:S(2)}) collective-permute-start(bf16[32,2048]{1,0:T(8,128)(2,1)S(1)} %convolution_convert_fusion.1), channel_id=1, source_target_pairs={{0,6},{1,7},{2,4},{3,5},{4,2},{5,3},{6,0},{7,1},{8,14},{9,15},{10,... | collective-permute-start | bytes 393224 | tf_op jit(solution)/shard_map/ppermute | solution.py:20
  60.8 2.9 %collective-permute-done.15.refs_2_ = bf16[32,2048]{1,0:T(8,128)(2,1)S(1)} collective-permute-done((bf16[32,2048]{1,0:T(8,128)(2,1)S(1)}, bf16[32,2048]{1,0:T(8,128)(2,1)S(1)}, u32[]{:S(2)}, u32[]{:S(2)}) %collective-permute-start.15) | collective-permute-done | bytes 131104 | tf_op jit(solution)/shard_map/ppermute | solution.py:20
  63.7 7.7 %collective-permute-done.14.refs_1_ = bf16[32,2048]{1,0:T(8,128)(2,1)S(1)} collective-permute-done((bf16[32,2048]{1,0:T(8,128)(2,1)S(1)}, bf16[32,2048]{1,0:T(8,128)(2,1)S(1)}, u32[]{:S(2)}, u32[]{:S(2)}) %collective-permute-start.14) | collective-permute-done | bytes 131104 | tf_op jit(solution)/shard_map/ppermute | solution.py:20
  71.4 1.0 %score.1 = f32[32,64]{1,0:T(8,128)} custom-call(bf16[64,8192]{1,0:T(8,128)(2,1)S(1)} %copy-done, bf16[32,2048]{1,0:T(8,128)(2,1)S(1)} %collective-permute-done.13.refs_0_, bf16[32,2048]{1,0:T(8,128)(2,1)S(1)} %collective-permute-done.14.refs_1_, bf16[32,2048]{1,0:T(8,128)(2,1)S(1)} %collective-permute-done.15.refs_2_, f32[32,64]{1,0:T(8,128)S(1)} %score_first.1.refs_3_), custom_call_target="tpu_custom_call" | custom-call | tf_op jit(solution)/shard_map/score/pallas_call | solution.py:487
  72.4 1.0 %mix.1 = bf16[512,1024]{1,0:T(8,128)(2,1)} custom-call(f32[512,1024]{1,0:T(8,128)S(1)} %get-tuple-element.24.refs_0_, bf16[512,1024]{1,0:T(8,128)(2,1)S(1)} %collective-permute-done.10.refs_1_), custom_call_target="tpu_custom_call" | custom-call | flops 524288 | bytes 4194304 | tf_op jit(solution)/shard_map/mix/pallas_call | solution.py:473
  (38 shorter events, 3.5 us)
Async XLA Ops:
  9.0 21.7 %copy-start.2 = (s32[1,512]{1,0:T(1,128)S(1)}, s32[1,512]{1,0:T(1,128)}, u32[]{:S(2)}) copy-start(s32[1,512]{1,0:T(1,128)} %param.10) | copy-start | bytes 6148
  9.0 21.7 %copy-start.3 = (s32[1,64]{1,0:T(1,128)S(1)}, s32[1,64]{1,0:T(1,128)}, u32[]{:S(2)}) copy-start(s32[1,64]{1,0:T(1,128)} %param.11) | copy-start | bytes 772
  14.5 16.1 %copy-start.1 = (bf16[256,512]{1,0:T(8,128)(2,1)}, bf16[256,512]{1,0:T(8,128)(2,1)S(1)}, u32[]{:S(2)}) copy-start(bf16[256,512]{1,0:T(8,128)(2,1)S(1)} %get-tuple-element.22) | copy-start | bytes 786436
  14.5 19.1 %collective-permute-start.9 = (bf16[256,2048]{1,0:T(8,128)(2,1)}, bf16[256,2048]{1,0:T(8,128)(2,1)}, u32[]{:S(2)}, u32[]{:S(2)}) collective-permute-start(bf16[256,2048]{1,0:T(8,128)(2,1)} %get-tuple-element.23), channel_id=1, source_target_pairs={{0,1},{1,0},{2,3},{3,2},{4,5},{5,4},{6,7},{7,6},{8,9},{9,8},{10,11... | collective-permute-start | bytes 3145736 | tf_op jit(solution)/shard_map/ppermute | solution.py:20
  16.3 31.5 %collective-permute-start.5 = (bf16[256,2048]{1,0:T(8,128)(2,1)S(1)}, bf16[256,2048]{1,0:T(8,128)(2,1)S(1)}, u32[]{:S(2)}, u32[]{:S(2)}) collective-permute-start(bf16[256,2048]{1,0:T(8,128)(2,1)S(1)} %cut.1), channel_id=1, source_target_pairs={{0,2},{1,5},{2,0},{3,7},{4,6},{5,1},{6,4},{7,3},{8,10},{9,13},{10,... | collective-permute-start | bytes 3145736 | tf_op jit(solution)/shard_map/ppermute | solution.py:20
  18.8 28.9 %collective-permute-start.6 = (bf16[256,1536]{1,0:T(8,128)(2,1)}, bf16[256,1536]{1,0:T(8,128)(2,1)S(1)}, u32[]{:S(2)}, u32[]{:S(2)}) collective-permute-start(bf16[256,1536]{1,0:T(8,128)(2,1)} %get-tuple-element.21), channel_id=1, source_target_pairs={{0,5},{1,2},{2,7},{3,0},{4,1},{5,6},{6,3},{7,4},{8,13},{9,10},{10,... | collective-permute-start | bytes 2359304 | tf_op jit(solution)/shard_map/ppermute | solution.py:20
  19.0 4.3 %collective-permute-start = (bf16[2,128,128]{2,1,0:T(8,128)(2,1)S(1)}, bf16[2,128,128]{2,1,0:T(8,128)(2,1)S(1)}, u32[]{:S(2)}, u32[]{:S(2)}) collective-permute-start(bf16[2,128,128]{2,1,0:T(8,128)(2,1)S(1)} %get-tuple-element.20), channel_id=1, source_target_pairs={{0,8},{8,0},{16,24},{24,16},{1,9},{9,1},{17,25},{25,17},{2,10},{10... | collective-permute-start | bytes 196616 | tf_op jit(solution)/shard_map/ppermute | solution.py:350
  20.8 7.2 %collective-permute-start.1 = (bf16[2,128,128]{2,1,0:T(8,128)(2,1)S(1)}, bf16[2,128,128]{2,1,0:T(8,128)(2,1)S(1)}, u32[]{:S(2)}, u32[]{:S(2)}) collective-permute-start(bf16[2,128,128]{2,1,0:T(8,128)(2,1)S(1)} %get-tuple-element.20), channel_id=1, source_target_pairs={{0,16},{8,24},{16,0},{24,8},{1,17},{9,25},{17,1},{25,9},{2,18},{10... | collective-permute-start | bytes 196616 | tf_op jit(solution)/shard_map/ppermute | solution.py:350
  23.4 6.9 %collective-permute-start.2 = (bf16[2,128,128]{2,1,0:T(8,128)(2,1)S(1)}, bf16[2,128,128]{2,1,0:T(8,128)(2,1)S(1)}, u32[]{:S(2)}, u32[]{:S(2)}) collective-permute-start(bf16[2,128,128]{2,1,0:T(8,128)(2,1)S(1)} %get-tuple-element.20), channel_id=1, source_target_pairs={{0,24},{8,16},{16,8},{24,0},{1,25},{9,17},{17,9},{25,1},{2,26},{10... | collective-permute-start | bytes 196616 | tf_op jit(solution)/shard_map/ppermute | solution.py:350
  30.6 1.9 %collective-permute-start.8 = (bf16[512,256]{1,0:T(8,128)(2,1)S(1)}, bf16[512,256]{1,0:T(8,128)(2,1)S(1)}, u32[]{:S(2)}, u32[]{:S(2)}) collective-permute-start(bf16[512,256]{1,0:T(8,128)(2,1)S(1)} %attend.1.own_ref), channel_id=1, source_target_pairs={{0,1},{1,0},{2,3},{3,2},{4,5},{5,4},{6,7},{7,6},{8,9},{9,8},{10,11... | collective-permute-start | bytes 786440 | tf_op jit(solution)/shard_map/ppermute | solution.py:20
  30.9 16.9 %collective-permute-start.3 = (bf16[512,256]{1,0:T(8,128)(2,1)S(1)}, bf16[512,256]{1,0:T(8,128)(2,1)S(1)}, u32[]{:S(2)}, u32[]{:S(2)}) collective-permute-start(bf16[512,256]{1,0:T(8,128)(2,1)S(1)} %attend.1.own_ref), channel_id=1, source_target_pairs={{0,2},{1,5},{2,0},{3,7},{4,6},{5,1},{6,4},{7,3},{8,10},{9,13},{10,... | collective-permute-start | bytes 786440 | tf_op jit(solution)/shard_map/ppermute | solution.py:20
  32.5 15.3 %collective-permute-start.4 = (bf16[512,256]{1,0:T(8,128)(2,1)S(1)}, bf16[512,256]{1,0:T(8,128)(2,1)S(1)}, u32[]{:S(2)}, u32[]{:S(2)}) collective-permute-start(bf16[512,256]{1,0:T(8,128)(2,1)S(1)} %attend.1.own_ref), channel_id=1, source_target_pairs={{0,5},{1,2},{2,7},{3,0},{4,1},{5,6},{6,3},{7,4},{8,13},{9,10},{10,... | collective-permute-start | bytes 786440 | tf_op jit(solution)/shard_map/ppermute | solution.py:20
  33.6 17.8 %collective-permute-start.7 = (bf16[256,512]{1,0:T(8,128)(2,1)}, bf16[256,512]{1,0:T(8,128)(2,1)S(1)}, u32[]{:S(2)}, u32[]{:S(2)}) collective-permute-start(bf16[256,512]{1,0:T(8,128)(2,1)} %copy-done.1), channel_id=1, source_target_pairs={{0,5},{1,2},{2,7},{3,0},{4,1},{5,6},{6,3},{7,4},{8,13},{9,10},{10,... | collective-permute-start | bytes 786440 | tf_op jit(solution)/shard_map/ppermute | solution.py:20
  38.6 15.7 %copy-start.4 = (s32[64,1]{0,1:T(1,128)S(1)}, s32[64,1]{0,1:T(1,128)}, u32[]{:S(2)}) copy-start(s32[64,1]{0,1:T(1,128)} %param.12) | copy-start | bytes 772
  38.6 22.0 %copy-start = (bf16[64,8192]{1,0:T(8,128)(2,1)S(1)}, bf16[64,8192]{1,0:T(8,128)(2,1)}, u32[]{:S(2)}) copy-start(bf16[64,8192]{1,0:T(8,128)(2,1)} %c_ref.3) | copy-start | bytes 3145732
  49.1 5.0 %collective-permute-start.11 = (bf16[64,1024]{1,0:T(8,128)(2,1)S(1)}, bf16[64,1024]{1,0:T(8,128)(2,1)S(1)}, u32[]{:S(2)}, u32[]{:S(2)}) collective-permute-start(bf16[64,1024]{1,0:T(8,128)(2,1)S(1)} %get-tuple-element.27), channel_id=1, source_target_pairs={{0,4},{1,3},{2,6},{3,1},{4,0},{5,7},{6,2},{7,5},{8,12},{9,11},{10,... | collective-permute-start | bytes 393224 | tf_op jit(solution)/shard_map/ppermute | solution.py:20
  50.9 21.4 %collective-permute-start.10 = (bf16[512,1024]{1,0:T(8,128)(2,1)S(1)}, bf16[512,1024]{1,0:T(8,128)(2,1)S(1)}, u32[]{:S(2)}, u32[]{:S(2)}) collective-permute-start(bf16[512,1024]{1,0:T(8,128)(2,1)S(1)} %get-tuple-element.25), channel_id=1, source_target_pairs={{0,4},{1,3},{2,6},{3,1},{4,0},{5,7},{6,2},{7,5},{8,12},{9,11},{10,... | collective-permute-start | bytes 3145736 | tf_op jit(solution)/shard_map/ppermute | solution.py:20
  54.2 1.4 %collective-permute-start.12 = (bf16[64,1024]{1,0:T(8,128)(2,1)S(1)}, bf16[64,1024]{1,0:T(8,128)(2,1)S(1)}, u32[]{:S(2)}, u32[]{:S(2)}) collective-permute-start(bf16[64,1024]{1,0:T(8,128)(2,1)S(1)} %divide_convert_fusion), channel_id=1, source_target_pairs={{0,1},{1,0},{2,3},{3,2},{4,5},{5,4},{6,7},{7,6},{8,9},{9,8},{10,11... | collective-permute-start | bytes 393224 | tf_op jit(solution)/shard_map/ppermute | solution.py:20
  55.8 7.9 %collective-permute-start.15 = (bf16[32,2048]{1,0:T(8,128)(2,1)S(1)}, bf16[32,2048]{1,0:T(8,128)(2,1)S(1)}, u32[]{:S(2)}, u32[]{:S(2)}) collective-permute-start(bf16[32,2048]{1,0:T(8,128)(2,1)S(1)} %convolution_convert_fusion.1), channel_id=1, source_target_pairs={{0,6},{1,7},{2,4},{3,5},{4,2},{5,3},{6,0},{7,1},{8,14},{9,15},{10,... | collective-permute-start | bytes 393224 | tf_op jit(solution)/shard_map/ppermute | solution.py:20
  59.5 11.9 %collective-permute-start.14 = (bf16[32,2048]{1,0:T(8,128)(2,1)S(1)}, bf16[32,2048]{1,0:T(8,128)(2,1)S(1)}, u32[]{:S(2)}, u32[]{:S(2)}) collective-permute-start(bf16[32,2048]{1,0:T(8,128)(2,1)S(1)} %convolution_convert_fusion.2), channel_id=1, source_target_pairs={{0,4},{1,5},{2,6},{3,7},{4,0},{5,1},{6,2},{7,3},{8,12},{9,13},{10,... | collective-permute-start | bytes 393224 | tf_op jit(solution)/shard_map/ppermute | solution.py:20
  60.2 11.2 %collective-permute-start.13 = (bf16[32,2048]{1,0:T(8,128)(2,1)S(1)}, bf16[32,2048]{1,0:T(8,128)(2,1)S(1)}, u32[]{:S(2)}, u32[]{:S(2)}) collective-permute-start(bf16[32,2048]{1,0:T(8,128)(2,1)S(1)} %convolution_convert_fusion.3), channel_id=1, source_target_pairs={{0,2},{1,3},{2,0},{3,1},{4,6},{5,7},{6,4},{7,5},{8,10},{9,11},{10,... | collective-permute-start | bytes 393224 | tf_op jit(solution)/shard_map/ppermute | solution.py:20

commit v4 on v3

--- a/solution.py
+++ b/solution.py
@@ -38,6 +38,10 @@
     return pl.ds(pl.multiple_of(index * size, size), size)
 
 
+def early_of(cols):
+    return max(HDIM, cols // 4)
+
+
 def cutter(w_ref, sems, cols, half_bits, partner):
     head = lax.axis_index("head")
     head = lax.bitwise_xor(head, 1) if partner else head
@@ -45,7 +49,7 @@
 
     def take(m, r, first, size, out, to):
         start = place(half_bits, m, r, head) * cols + first
-        start = pl.multiple_of(start, cols // 2)
+        start = pl.multiple_of(start, early_of(cols))
         copies.append(
             pltpu.make_async_copy(
                 w_ref.at[:, pl.ds(start, size)], out.at[:, pl.ds(to, size)], sems.at[len(copies)]
@@ -76,7 +80,7 @@
     for m in range(1, side):
         for r in range(1, side):
             take(m, r, 0, cols, mains[m - 1], (r - 1) * cols)
-        take(m, 0, 0, cols // 2, mains[m - 1], (side - 1) * cols)
+        take(m, 0, 0, early_of(cols), mains[m - 1], (side - 1) * cols)
     for group in (*copies[:-2], cut, *copies[-2:]):
         for copy in group:
             copy.start()
@@ -117,7 +121,7 @@
     for r in range(side):
         take(0, r, 0, cols, own_ref, r * cols)
     for m in range(1, side):
-        take(m, 0, cols // 2, cols // 2, lates[m - 1], 0)
+        take(m, 0, early_of(cols), cols - early_of(cols), lates[m - 1], 0)
     for copy in cut:
         copy.start()
     for s in range(steps):
@@ -219,32 +223,27 @@
 
 def add_kernel(*refs, count, r, rows):
     ext, w = refs[: 2 * count], refs[2 * count : 4 * count]
-    late, m_ref, base = refs[4 * count : -6], refs[-6], refs[-5]
-    r_ref, p_ref, buf, sems = refs[-4:]
+    late, m_ref, base = refs[4 * count : -4], refs[-4], refs[-3]
+    r_ref, p_ref = refs[-2:]
     cols = r_ref.shape[1]
-    half = cols // 2
     pooled = [dot(m_ref[...], e[...]).astype(BF16) for e in ext]
-    copies = []
-    for n, c in enumerate((0, half)):
-        at = pl.ds(c, half)
+    split = cols // 2 if r else early_of(cols)
+    for first, size in ((0, split), (split, cols - split)):
+        at = pl.ds(first, size)
         total, few = base[r, pl.ds(0, rows), at], base[r, pl.ds(rows, m_ref.shape[0]), at]
         for i in range(2 * count):
             if i < count:
-                part = w[i][:, pl.ds(r * cols + c, half)]
+                part = w[i][:, pl.ds(r * cols + first, size)]
             elif r:
-                part = w[i][:, pl.ds((r - 1) * cols + c, half)]
-            elif n:
+                part = w[i][:, pl.ds((r - 1) * cols + first, size)]
+            elif first:
                 part = late[i - count][...]
             else:
-                part = w[i][:, pl.ds(w[i].shape[1] - half, half)]
+                part = w[i][:, pl.ds(w[i].shape[1] - size, size)]
             total = total + dot(ext[i][...], part)
             few = few + dot(pooled[i], part)
         p_ref[:, at] = few.astype(p_ref.dtype)
-        buf[:, at] = total.astype(buf.dtype)
-        copies.append(pltpu.make_async_copy(buf.at[:, at], r_ref.at[:, at], sems.at[n]))
-        copies[-1].start()
-    for copy in copies:
-        copy.wait()
+        r_ref[:, at] = total.astype(r_ref.dtype)
 
 
 def mix_kernel(*refs):
@@ -326,7 +325,7 @@
             jax.ShapeDtypeStruct((tokens_here, width), BF16),
             jax.ShapeDtypeStruct((heads_here, HDIM, HDIM), BF16),
             jax.ShapeDtypeStruct((tokens_here, model_width), BF16),
-            *[jax.ShapeDtypeStruct((width, side * cols - cols // 2), BF16)] * (side - 1),
+            *[jax.ShapeDtypeStruct((width, (side - 1) * cols + early_of(cols)), BF16)] * (side - 1),
         ],
         in_specs=[HBM] * 3,
         out_specs=[VMEM] * (side + 3),
@@ -346,9 +345,9 @@
     )(stay(inputs), stay(w_qkv), stay(w_out))
     w_main = [move(w, beside(m + 1)) for m, w in enumerate(w_beside)]
 
-    earlier = [
-        lax.ppermute(states, "seq", [(i, i ^ s) for i in range(n_seq)]) for s in range(1, n_seq)
-    ]
+    earlier = []
+    for s in range(1, n_seq):
+        earlier.append(lax.ppermute(states, "seq", [(i, i ^ s) for i in range(n_seq)]))
 
     query, local, w_own, *w_rest = pl.pallas_call(
         functools.partial(q_kernel, steps=4, half_bits=half_bits, cols=cols),
@@ -356,7 +355,7 @@
             jax.ShapeDtypeStruct((tokens_here, width), BF16),
             jax.ShapeDtypeStruct((tokens_here, width), F32),
             jax.ShapeDtypeStruct((width, side * cols), BF16),
-            *[jax.ShapeDtypeStruct((width, cols // 2), BF16)] * (side - 1),
+            *[jax.ShapeDtypeStruct((width, cols - early_of(cols)), BF16)] * (side - 1),
         ],
         in_specs=[VMEM, HBM, VMEM, VMEM, HBM],
         out_specs=[VMEM] * (side + 2),
@@ -383,7 +382,6 @@
     pick_hot = tok_pos[None, :] == pick_row[:, None]
     sel_turn = jnp.sum(jnp.where(pick_hot, turn_row[None, :], 0), axis=1)
     member = (turn_row[None, :] == sel_turn[:, None]) & (tok_pos[None, :] <= pick_row[:, None])
-    row_count = jnp.sum(member.astype(F32), axis=1)
     member = member.astype(BF16)
 
     ext = pl.pallas_call(
@@ -432,11 +430,7 @@
                 jax.ShapeDtypeStruct((r_dev, cols), kind),
             ],
             in_specs=[VMEM] * (2 * len(stacks) + len(late) + 2),
-            out_specs=[HBM, VMEM],
-            scratch_shapes=[
-                scratch((tokens_here, cols), kind),
-                pltpu.SemaphoreType.DMA((2,)),
-            ],
+            out_specs=[VMEM, VMEM],
             cost_estimate=pl.CostEstimate(
                 flops=2 * height * cols * width * len(stacks),
                 bytes_accessed=2 * width * cols * len(stacks),
@@ -450,6 +444,8 @@
     rows_in = [move(b, across(r + 1)) for r, (b, _) in enumerate(given)]
     rows_here, pooled = project(0, F32)
 
+    counted, pooled = lax.optimization_barrier((member, pooled))
+    row_count = jnp.sum(counted.astype(F32), axis=1)
     for p in pool_in:
         pooled = pooled + p.astype(F32)
     summary = (pooled / row_count[:, None]).astype(BF16)

time: 73.6 us -> 75.4 us (1.024)
  waiting for transfers between devices: 24.3 us -> 32.4 us
  starting transfers between devices: 22.9 us -> 16.5 us
    ppermute x3, starting transfers between devices: 8.94 us -> 4.39 us  [per_device(): lax.ppermute(states, 'seq', [(i, i ^ s) for i in range(n_seq)])]
    ppermute x13, waiting for transfers between devices: 22.1 us -> 26.4 us  [move(): lax.ppermute(value, 'head', [(i, i ^ masks[i % 2]) for i in range(n)])]
    ppermute x3, waiting for transfers between devices: 2.24 us -> 5.95 us  [per_device(): lax.ppermute(states, 'seq', [(i, i ^ s) for i in range(n_seq)])]
    ppermute x13, starting transfers between devices: 14 us -> 12.1 us  [move(): lax.ppermute(value, 'head', [(i, i ^ masks[i % 2]) for i in range(n)])]
    pallas_call x1, Pallas kernels: 3.44 us -> 4.45 us  [per_device(): pl.pallas_call(functools.partial(here_kernel, half_bits=half_bits), out_s...]
    pallas_call x2, Pallas kernels: 2.89 us -> 1.99 us  [project(): pl.pallas_call(functools.partial(add_kernel, count=side - 1, r=r, rows=to...]
  transfers between devices with their start and end apart: 16 -> 16, of which waited for: 6 -> 8; matrix products, arithmetic and copies ran while one was open for 2% -> 2% of each run, Pallas kernels for 12% -> 12%
where the time goes in v4:
time: 75.4 us; the launch traced here: 75.2 us
  waiting for transfers between devices  32.4 us (43%)
  Pallas kernels  24.2 us (32%)
  starting transfers between devices  16.5 us (22%)
  between operations  0.83 us (1%)
  matrix products  0.79 us (1%)
    ppermute x13, waiting for transfers between devices, move(): lax.ppermute(value, 'head', [(i, i ^ masks[i % 2]) for i in range(n)])  26.4 us
    ppermute x13, starting transfers between devices, move(): lax.ppermute(value, 'head', [(i, i ^ masks[i % 2]) for i in range(n)])  12.1 us
    pallas_call x1, Pallas kernels, per_device(): pl.pallas_call(functools.partial(kv_kernel, steps=steps, half_bits=half_b...  8.27 us
    ppermute x3, waiting for transfers between devices, per_device(): lax.ppermute(states, 'seq', [(i, i ^ s) for i in range(n_seq)])  5.95 us
    pallas_call x1, Pallas kernels, per_device(): pl.pallas_call(functools.partial(q_kernel, steps=4, half_bits=half_bits,...  5.63 us
    pallas_call x1, Pallas kernels, per_device(): pl.pallas_call(functools.partial(here_kernel, half_bits=half_bits), out_s...  4.45 us
    ppermute x3, starting transfers between devices, per_device(): lax.ppermute(states, 'seq', [(i, i ^ s) for i in range(n_seq)])  4.39 us
    pallas_call x2, Pallas kernels, project(): pl.pallas_call(functools.partial(add_kernel, count=side - 1, r=r, rows=to...  1.99 us
  transfers between devices with their start and end apart: 16, of which 8 were waited for; matrix products, arithmetic and copies ran while one was open for 2% of the time, Pallas kernels for 12%

profile of v4, /device:TPU:0, one launch (start us, length us, event | category | flops | bytes accessed | tf_op | source)
XLA Modules:
  0.0 75.2 jit_solution(9002573937168687595)
XLA Ops:
  0.6 8.3 %kv.1 = (bf16[512,256]{1,0:T(8,128)(2,1)S(1)}, bf16[512,256]{1,0:T(8,128)(2,1)S(1)}, bf16[2,128,128]{2,1,0:T(8,128)(2,1)S(1)}, bf16[512,8192]{1,0:T(8,128)(2,1)S(1)}, bf16[256,1280]{1,0:T(8,128)(2,1)}) custom-call(bf16[512,8192]{1,0:T(8,128)(2,1)} %x_ref.3, bf16[3,8192,256]{2,1,0:T(8,128)(2,1)} %w_ref.5, bf16[256,8192]{1,0:T(8,128)(2,1)} %w_ref.7), custom_call_target="tpu_custom_call" | custom-call | flops 4294967296 | bytes 16777216 | tf_op jit(solution)/shard_map/kv/pallas_call | solution.py:321
  8.9 5.6 %qlocal.1 = (bf16[512,256]{1,0:T(8,128)(2,1)S(1)}, f32[512,256]{1,0:T(8,128)S(1)}, bf16[256,2048]{1,0:T(8,128)(2,1)}, bf16[256,768]{1,0:T(8,128)(2,1)}) custom-call(bf16[512,8192]{1,0:T(8,128)(2,1)S(1)} %get-tuple-element.17.x_ref, bf16[3,8192,256]{2,1,0:T(8,128)(2,1)} %w_ref.5, bf16[512,256]{1,0:T(8,128)(2,1)S(1)} %get-tuple-element.18.k_ref, ...), custom_call_target="tpu_custom_call" | custom-call | flops 2147483648 | bytes 4194304 | tf_op jit(solution)/shard_map/qlocal/pallas_call | solution.py:352
  15.1 1.2 %cut.1 = bf16[256,2048]{1,0:T(8,128)(2,1)S(1)} custom-call(bf16[256,8192]{1,0:T(8,128)(2,1)} %w_ref.7), custom_call_target="tpu_custom_call" | custom-call | bytes 2097152 | tf_op jit(solution)/shard_map/cut/pallas_call | solution.py:304
  16.4 2.6 %collective-permute-start.5 = (bf16[256,2048]{1,0:T(8,128)(2,1)S(1)}, bf16[256,2048]{1,0:T(8,128)(2,1)S(1)}, u32[]{:S(2)}, u32[]{:S(2)}) collective-permute-start(bf16[256,2048]{1,0:T(8,128)(2,1)S(1)} %cut.1), channel_id=1, source_target_pairs={{0,2},{1,5},{2,0},{3,7},{4,6},{5,1},{6,4},{7,3},{8,10},{9,13},{10,... | collective-permute-start | bytes 3145736 | tf_op jit(solution)/shard_map/ppermute | solution.py:20
  18.9 1.6 %collective-permute-start = (bf16[2,128,128]{2,1,0:T(8,128)(2,1)S(1)}, bf16[2,128,128]{2,1,0:T(8,128)(2,1)S(1)}, u32[]{:S(2)}, u32[]{:S(2)}) collective-permute-start(bf16[2,128,128]{2,1,0:T(8,128)(2,1)S(1)} %get-tuple-element.22), channel_id=1, source_target_pairs={{0,8},{8,0},{16,24},{24,16},{1,9},{9,1},{17,25},{25,17},{2,10},{10... | collective-permute-start | bytes 196616 | tf_op jit(solution)/shard_map/ppermute | solution.py:350
  20.5 2.6 %collective-permute-start.1 = (bf16[2,128,128]{2,1,0:T(8,128)(2,1)S(1)}, bf16[2,128,128]{2,1,0:T(8,128)(2,1)S(1)}, u32[]{:S(2)}, u32[]{:S(2)}) collective-permute-start(bf16[2,128,128]{2,1,0:T(8,128)(2,1)S(1)} %get-tuple-element.22), channel_id=1, source_target_pairs={{0,16},{8,24},{16,0},{24,8},{1,17},{9,25},{17,1},{25,9},{2,18},{10... | collective-permute-start | bytes 196616 | tf_op jit(solution)/shard_map/ppermute | solution.py:350
  23.3 4.8 %collective-permute-done.1.refs_3_ = bf16[2,128,128]{2,1,0:T(8,128)(2,1)S(1)} collective-permute-done((bf16[2,128,128]{2,1,0:T(8,128)(2,1)S(1)}, bf16[2,128,128]{2,1,0:T(8,128)(2,1)S(1)}, u32[]{:S(2)}, u32[]{:S(2)}) %collective-permute-start.1) | collective-permute-done | bytes 65568 | tf_op jit(solution)/shard_map/ppermute | solution.py:350
  28.1 1.2 %collective-permute-done.2.refs_4_ = bf16[2,128,128]{2,1,0:T(8,128)(2,1)S(1)} collective-permute-done((bf16[2,128,128]{2,1,0:T(8,128)(2,1)S(1)}, bf16[2,128,128]{2,1,0:T(8,128)(2,1)S(1)}, u32[]{:S(2)}, u32[]{:S(2)}) %collective-permute-start.2) | collective-permute-done | bytes 65568 | tf_op jit(solution)/shard_map/ppermute | solution.py:350
  29.7 1.5 %collective-permute-start.7 = (bf16[256,768]{1,0:T(8,128)(2,1)}, bf16[256,768]{1,0:T(8,128)(2,1)S(1)}, u32[]{:S(2)}, u32[]{:S(2)}) collective-permute-start(bf16[256,768]{1,0:T(8,128)(2,1)} %get-tuple-element.24), channel_id=1, source_target_pairs={{0,5},{1,2},{2,7},{3,0},{4,1},{5,6},{6,3},{7,4},{8,13},{9,10},{10,... | collective-permute-start | bytes 1179656 | tf_op jit(solution)/shard_map/ppermute | solution.py:20
  31.5 0.8 %collective-permute-start.3 = (bf16[512,256]{1,0:T(8,128)(2,1)S(1)}, bf16[512,256]{1,0:T(8,128)(2,1)S(1)}, u32[]{:S(2)}, u32[]{:S(2)}) collective-permute-start(bf16[512,256]{1,0:T(8,128)(2,1)S(1)} %attend.1.own_ref), channel_id=1, source_target_pairs={{0,2},{1,5},{2,0},{3,7},{4,6},{5,1},{6,4},{7,3},{8,10},{9,13},{10,... | collective-permute-start | bytes 786440 | tf_op jit(solution)/shard_map/ppermute | solution.py:20
  32.3 0.6 collective-permute-start.4
  33.0 4.4 %here.1.refs_6_.refs_5_ = f32[2,576,1024]{2,1,0:T(8,128)S(1)} custom-call(bf16[512,256]{1,0:T(8,128)(2,1)S(1)} %attend.1.own_ref, bf16[512,256]{1,0:T(8,128)(2,1)} %collective-permute-done.8.peer_ref, bf16[64,512]{1,0:T(8,128)(2,1)S(1)} %fusion.2.m_ref.refs_5_.refs_4_, bf16[512,8192]{1,0:T(8,128)(2,1)} %x_ref.3, bf16[256,8192]{1,0:T(8,128)(2,1)} %w_ref.7, ...), custom_call_target="tpu_custom_call" | custom-call | flops 1207959552 | bytes 2097152 | tf_op jit(solution)/shard_map/here/pallas_call | solution.py:401
  37.5 6.3 %collective-permute-done.3.refs_0_ = bf16[512,256]{1,0:T(8,128)(2,1)S(1)} collective-permute-done((bf16[512,256]{1,0:T(8,128)(2,1)S(1)}, bf16[512,256]{1,0:T(8,128)(2,1)S(1)}, u32[]{:S(2)}, u32[]{:S(2)}) %collective-permute-start.3) | collective-permute-done | bytes 262176 | tf_op jit(solution)/shard_map/ppermute | solution.py:20
  43.7 4.8 %collective-permute-done.4.refs_1_ = bf16[512,256]{1,0:T(8,128)(2,1)S(1)} collective-permute-done((bf16[512,256]{1,0:T(8,128)(2,1)S(1)}, bf16[512,256]{1,0:T(8,128)(2,1)S(1)}, u32[]{:S(2)}, u32[]{:S(2)}) %collective-permute-start.4) | collective-permute-done | bytes 262176 | tf_op jit(solution)/shard_map/ppermute | solution.py:20
  48.6 1.0 %shard_map.87 = (bf16[512,1024]{1,0:T(8,128)(2,1)S(1)}, bf16[64,1024]{1,0:T(8,128)(2,1)S(1)}) custom-call(bf16[512,256]{1,0:T(8,128)(2,1)S(1)} %collective-permute-done.3.refs_0_, bf16[512,256]{1,0:T(8,128)(2,1)S(1)} %collective-permute-done.4.refs_1_, bf16[256,2048]{1,0:T(8,128)(2,1)S(1)} %collective-permute-done.5.refs_2_, ...), custom_call_target="tpu_custom_call" | custom-call | flops 603979776 | bytes 1048576 | tf_op jit(solution)/shard_map/pallas_call | solution.py:426
  49.6 2.1 %collective-permute-start.11 = (bf16[64,1024]{1,0:T(8,128)(2,1)S(1)}, bf16[64,1024]{1,0:T(8,128)(2,1)S(1)}, u32[]{:S(2)}, u32[]{:S(2)}) collective-permute-start(bf16[64,1024]{1,0:T(8,128)(2,1)S(1)} %get-tuple-element.30), channel_id=1, source_target_pairs={{0,4},{1,3},{2,6},{3,1},{4,0},{5,7},{6,2},{7,5},{8,12},{9,11},{10,... | collective-permute-start | bytes 393224 | tf_op jit(solution)/shard_map/ppermute | solution.py:20
  51.7 1.0 %shard_map.86 = (f32[512,1024]{1,0:T(8,128)S(1)}, f32[64,1024]{1,0:T(8,128)S(1)}) custom-call(bf16[512,256]{1,0:T(8,128)(2,1)S(1)} %collective-permute-done.3.refs_0_, bf16[512,256]{1,0:T(8,128)(2,1)S(1)} %collective-permute-done.4.refs_1_, bf16[256,2048]{1,0:T(8,128)(2,1)S(1)} %collective-permute-done.5.refs_2_, ...), custom_call_target="tpu_custom_call" | custom-call | flops 603979776 | bytes 1048576 | tf_op jit(solution)/shard_map/pallas_call | solution.py:426
  52.9 1.7 %collective-permute-done.11 = bf16[64,1024]{1,0:T(8,128)(2,1)S(1)} collective-permute-done((bf16[64,1024]{1,0:T(8,128)(2,1)S(1)}, bf16[64,1024]{1,0:T(8,128)(2,1)S(1)}, u32[]{:S(2)}, u32[]{:S(2)}) %collective-permute-start.11) | collective-permute-done | bytes 131104 | tf_op jit(solution)/shard_map/ppermute | solution.py:20
  55.0 1.2 %collective-permute-done.12 = bf16[64,1024]{1,0:T(8,128)(2,1)S(1)} collective-permute-done((bf16[64,1024]{1,0:T(8,128)(2,1)S(1)}, bf16[64,1024]{1,0:T(8,128)(2,1)S(1)}, u32[]{:S(2)}, u32[]{:S(2)}) %collective-permute-start.12) | collective-permute-done | bytes 131104 | tf_op jit(solution)/shard_map/ppermute | solution.py:20
  56.3 3.0 %collective-permute-start.15 = (bf16[32,2048]{1,0:T(8,128)(2,1)S(1)}, bf16[32,2048]{1,0:T(8,128)(2,1)S(1)}, u32[]{:S(2)}, u32[]{:S(2)}) collective-permute-start(bf16[32,2048]{1,0:T(8,128)(2,1)S(1)} %convolution_convert_fusion.1), channel_id=1, source_target_pairs={{0,6},{1,7},{2,4},{3,5},{4,2},{5,3},{6,0},{7,1},{8,14},{9,15},{10,... | collective-permute-start | bytes 393224 | tf_op jit(solution)/shard_map/ppermute | solution.py:20
  60.7 2.9 %collective-permute-done.15.refs_2_ = bf16[32,2048]{1,0:T(8,128)(2,1)S(1)} collective-permute-done((bf16[32,2048]{1,0:T(8,128)(2,1)S(1)}, bf16[32,2048]{1,0:T(8,128)(2,1)S(1)}, u32[]{:S(2)}, u32[]{:S(2)}) %collective-permute-start.15) | collective-permute-done | bytes 131104 | tf_op jit(solution)/shard_map/ppermute | solution.py:20
  63.7 9.5 %collective-permute-done.14.refs_1_ = bf16[32,2048]{1,0:T(8,128)(2,1)S(1)} collective-permute-done((bf16[32,2048]{1,0:T(8,128)(2,1)S(1)}, bf16[32,2048]{1,0:T(8,128)(2,1)S(1)}, u32[]{:S(2)}, u32[]{:S(2)}) %collective-permute-start.14) | collective-permute-done | bytes 131104 | tf_op jit(solution)/shard_map/ppermute | solution.py:20
  73.2 1.0 %score.1 = f32[32,64]{1,0:T(8,128)} custom-call(bf16[64,8192]{1,0:T(8,128)(2,1)S(1)} %copy-done, bf16[32,2048]{1,0:T(8,128)(2,1)S(1)} %collective-permute-done.13.refs_0_, bf16[32,2048]{1,0:T(8,128)(2,1)S(1)} %collective-permute-done.14.refs_1_, bf16[32,2048]{1,0:T(8,128)(2,1)S(1)} %collective-permute-done.15.refs_2_, f32[32,64]{1,0:T(8,128)S(1)} %score_first.1.refs_3_), custom_call_target="tpu_custom_call" | custom-call | tf_op jit(solution)/shard_map/score/pallas_call | solution.py:483
  74.1 1.1 %mix.1 = bf16[512,1024]{1,0:T(8,128)(2,1)} custom-call(f32[512,1024]{1,0:T(8,128)S(1)} %get-tuple-element.26.refs_0_, bf16[512,1024]{1,0:T(8,128)(2,1)S(1)} %collective-permute-done.10.refs_1_), custom_call_target="tpu_custom_call" | custom-call | flops 524288 | bytes 4194304 | tf_op jit(solution)/shard_map/mix/pallas_call | solution.py:469
  (36 shorter events, 3.6 us)
Async XLA Ops:
  8.9 22.4 %copy-start.1 = (s32[1,512]{1,0:T(1,128)S(1)}, s32[1,512]{1,0:T(1,128)}, u32[]{:S(2)}) copy-start(s32[1,512]{1,0:T(1,128)} %param.10) | copy-start | bytes 6148
  8.9 22.3 %copy-start.2 = (s32[1,64]{1,0:T(1,128)S(1)}, s32[1,64]{1,0:T(1,128)}, u32[]{:S(2)}) copy-start(s32[1,64]{1,0:T(1,128)} %param.11) | copy-start | bytes 772
  14.6 17.7 %collective-permute-start.9 = (bf16[256,2048]{1,0:T(8,128)(2,1)}, bf16[256,2048]{1,0:T(8,128)(2,1)}, u32[]{:S(2)}, u32[]{:S(2)}) collective-permute-start(bf16[256,2048]{1,0:T(8,128)(2,1)} %get-tuple-element.25), channel_id=1, source_target_pairs={{0,1},{1,0},{2,3},{3,2},{4,5},{5,4},{6,7},{7,6},{8,9},{9,8},{10,11... | collective-permute-start | bytes 3145736 | tf_op jit(solution)/shard_map/ppermute | solution.py:20
  16.4 32.2 %collective-permute-start.5 = (bf16[256,2048]{1,0:T(8,128)(2,1)S(1)}, bf16[256,2048]{1,0:T(8,128)(2,1)S(1)}, u32[]{:S(2)}, u32[]{:S(2)}) collective-permute-start(bf16[256,2048]{1,0:T(8,128)(2,1)S(1)} %cut.1), channel_id=1, source_target_pairs={{0,2},{1,5},{2,0},{3,7},{4,6},{5,1},{6,4},{7,3},{8,10},{9,13},{10,... | collective-permute-start | bytes 3145736 | tf_op jit(solution)/shard_map/ppermute | solution.py:20
  18.9 4.4 %collective-permute-start = (bf16[2,128,128]{2,1,0:T(8,128)(2,1)S(1)}, bf16[2,128,128]{2,1,0:T(8,128)(2,1)S(1)}, u32[]{:S(2)}, u32[]{:S(2)}) collective-permute-start(bf16[2,128,128]{2,1,0:T(8,128)(2,1)S(1)} %get-tuple-element.22), channel_id=1, source_target_pairs={{0,8},{8,0},{16,24},{24,16},{1,9},{9,1},{17,25},{25,17},{2,10},{10... | collective-permute-start | bytes 196616 | tf_op jit(solution)/shard_map/ppermute | solution.py:350
  20.5 7.6 %collective-permute-start.1 = (bf16[2,128,128]{2,1,0:T(8,128)(2,1)S(1)}, bf16[2,128,128]{2,1,0:T(8,128)(2,1)S(1)}, u32[]{:S(2)}, u32[]{:S(2)}) collective-permute-start(bf16[2,128,128]{2,1,0:T(8,128)(2,1)S(1)} %get-tuple-element.22), channel_id=1, source_target_pairs={{0,16},{8,24},{16,0},{24,8},{1,17},{9,25},{17,1},{25,9},{2,18},{10... | collective-permute-start | bytes 196616 | tf_op jit(solution)/shard_map/ppermute | solution.py:350
  23.1 6.2 %collective-permute-start.2 = (bf16[2,128,128]{2,1,0:T(8,128)(2,1)S(1)}, bf16[2,128,128]{2,1,0:T(8,128)(2,1)S(1)}, u32[]{:S(2)}, u32[]{:S(2)}) collective-permute-start(bf16[2,128,128]{2,1,0:T(8,128)(2,1)S(1)} %get-tuple-element.22), channel_id=1, source_target_pairs={{0,24},{8,16},{16,8},{24,0},{1,25},{9,17},{17,9},{25,1},{2,26},{10... | collective-permute-start | bytes 196616 | tf_op jit(solution)/shard_map/ppermute | solution.py:350
  23.3 25.2 %collective-permute-start.6 = (bf16[256,1280]{1,0:T(8,128)(2,1)}, bf16[256,1280]{1,0:T(8,128)(2,1)S(1)}, u32[]{:S(2)}, u32[]{:S(2)}) collective-permute-start(bf16[256,1280]{1,0:T(8,128)(2,1)} %get-tuple-element.23), channel_id=1, source_target_pairs={{0,5},{1,2},{2,7},{3,0},{4,1},{5,6},{6,3},{7,4},{8,13},{9,10},{10,... | collective-permute-start | bytes 1966088 | tf_op jit(solution)/shard_map/ppermute | solution.py:20
  29.7 1.8 %collective-permute-start.8 = (bf16[512,256]{1,0:T(8,128)(2,1)S(1)}, bf16[512,256]{1,0:T(8,128)(2,1)}, u32[]{:S(2)}, u32[]{:S(2)}) collective-permute-start(bf16[512,256]{1,0:T(8,128)(2,1)S(1)} %attend.1.own_ref), channel_id=1, source_target_pairs={{0,1},{1,0},{2,3},{3,2},{4,5},{5,4},{6,7},{7,6},{8,9},{9,8},{10,11... | collective-permute-start | bytes 786440 | tf_op jit(solution)/shard_map/ppermute | solution.py:20
  29.7 21.9 %collective-permute-start.7 = (bf16[256,768]{1,0:T(8,128)(2,1)}, bf16[256,768]{1,0:T(8,128)(2,1)S(1)}, u32[]{:S(2)}, u32[]{:S(2)}) collective-permute-start(bf16[256,768]{1,0:T(8,128)(2,1)} %get-tuple-element.24), channel_id=1, source_target_pairs={{0,5},{1,2},{2,7},{3,0},{4,1},{5,6},{6,3},{7,4},{8,13},{9,10},{10,... | collective-permute-start | bytes 1179656 | tf_op jit(solution)/shard_map/ppermute | solution.py:20
  31.5 12.3 %collective-permute-start.3 = (bf16[512,256]{1,0:T(8,128)(2,1)S(1)}, bf16[512,256]{1,0:T(8,128)(2,1)S(1)}, u32[]{:S(2)}, u32[]{:S(2)}) collective-permute-start(bf16[512,256]{1,0:T(8,128)(2,1)S(1)} %attend.1.own_ref), channel_id=1, source_target_pairs={{0,2},{1,5},{2,0},{3,7},{4,6},{5,1},{6,4},{7,3},{8,10},{9,13},{10,... | collective-permute-start | bytes 786440 | tf_op jit(solution)/shard_map/ppermute | solution.py:20
  32.3 16.3 %collective-permute-start.4 = (bf16[512,256]{1,0:T(8,128)(2,1)S(1)}, bf16[512,256]{1,0:T(8,128)(2,1)S(1)}, u32[]{:S(2)}, u32[]{:S(2)}) collective-permute-start(bf16[512,256]{1,0:T(8,128)(2,1)S(1)} %attend.1.own_ref), channel_id=1, source_target_pairs={{0,5},{1,2},{2,7},{3,0},{4,1},{5,6},{6,3},{7,4},{8,13},{9,10},{10,... | collective-permute-start | bytes 786440 | tf_op jit(solution)/shard_map/ppermute | solution.py:20
  37.4 17.4 %copy-start.3 = (s32[64,1]{0,1:T(1,128)S(1)}, s32[64,1]{0,1:T(1,128)}, u32[]{:S(2)}) copy-start(s32[64,1]{0,1:T(1,128)} %param.12) | copy-start | bytes 772
  37.5 23.1 %copy-start = (bf16[64,8192]{1,0:T(8,128)(2,1)S(1)}, bf16[64,8192]{1,0:T(8,128)(2,1)}, u32[]{:S(2)}) copy-start(bf16[64,8192]{1,0:T(8,128)(2,1)} %c_ref.3) | copy-start | bytes 3145732
  49.6 5.1 %collective-permute-start.11 = (bf16[64,1024]{1,0:T(8,128)(2,1)S(1)}, bf16[64,1024]{1,0:T(8,128)(2,1)S(1)}, u32[]{:S(2)}, u32[]{:S(2)}) collective-permute-start(bf16[64,1024]{1,0:T(8,128)(2,1)S(1)} %get-tuple-element.30), channel_id=1, source_target_pairs={{0,4},{1,3},{2,6},{3,1},{4,0},{5,7},{6,2},{7,5},{8,12},{9,11},{10,... | collective-permute-start | bytes 393224 | tf_op jit(solution)/shard_map/ppermute | solution.py:20
  52.7 21.4 %collective-permute-start.10 = (bf16[512,1024]{1,0:T(8,128)(2,1)S(1)}, bf16[512,1024]{1,0:T(8,128)(2,1)S(1)}, u32[]{:S(2)}, u32[]{:S(2)}) collective-permute-start(bf16[512,1024]{1,0:T(8,128)(2,1)S(1)} %get-tuple-element.27), channel_id=1, source_target_pairs={{0,4},{1,3},{2,6},{3,1},{4,0},{5,7},{6,2},{7,5},{8,12},{9,11},{10,... | collective-permute-start | bytes 3145736 | tf_op jit(solution)/shard_map/ppermute | solution.py:20
  54.7 1.4 %collective-permute-start.12 = (bf16[64,1024]{1,0:T(8,128)(2,1)S(1)}, bf16[64,1024]{1,0:T(8,128)(2,1)S(1)}, u32[]{:S(2)}, u32[]{:S(2)}) collective-permute-start(bf16[64,1024]{1,0:T(8,128)(2,1)S(1)} %divide_convert_fusion), channel_id=1, source_target_pairs={{0,1},{1,0},{2,3},{3,2},{4,5},{5,4},{6,7},{7,6},{8,9},{9,8},{10,11... | collective-permute-start | bytes 393224 | tf_op jit(solution)/shard_map/ppermute | solution.py:20
  56.3 7.4 %collective-permute-start.15 = (bf16[32,2048]{1,0:T(8,128)(2,1)S(1)}, bf16[32,2048]{1,0:T(8,128)(2,1)S(1)}, u32[]{:S(2)}, u32[]{:S(2)}) collective-permute-start(bf16[32,2048]{1,0:T(8,128)(2,1)S(1)} %convolution_convert_fusion.1), channel_id=1, source_target_pairs={{0,6},{1,7},{2,4},{3,5},{4,2},{5,3},{6,0},{7,1},{8,14},{9,15},{10,... | collective-permute-start | bytes 393224 | tf_op jit(solution)/shard_map/ppermute | solution.py:20
  59.5 13.7 %collective-permute-start.14 = (bf16[32,2048]{1,0:T(8,128)(2,1)S(1)}, bf16[32,2048]{1,0:T(8,128)(2,1)S(1)}, u32[]{:S(2)}, u32[]{:S(2)}) collective-permute-start(bf16[32,2048]{1,0:T(8,128)(2,1)S(1)} %convolution_convert_fusion.2), channel_id=1, source_target_pairs={{0,4},{1,5},{2,6},{3,7},{4,0},{5,1},{6,2},{7,3},{8,12},{9,13},{10,... | collective-permute-start | bytes 393224 | tf_op jit(solution)/shard_map/ppermute | solution.py:20
  60.2 12.9 %collective-permute-start.13 = (bf16[32,2048]{1,0:T(8,128)(2,1)S(1)}, bf16[32,2048]{1,0:T(8,128)(2,1)S(1)}, u32[]{:S(2)}, u32[]{:S(2)}) collective-permute-start(bf16[32,2048]{1,0:T(8,128)(2,1)S(1)} %convolution_convert_fusion.3), channel_id=1, source_target_pairs={{0,2},{1,3},{2,0},{3,1},{4,6},{5,7},{6,4},{7,5},{8,10},{9,11},{10,... | collective-permute-start | bytes 393224 | tf_op jit(solution)/shard_map/ppermute | solution.py:20

commit v5 on v4

--- a/solution.py
+++ b/solution.py
@@ -223,13 +223,21 @@
 
 def add_kernel(*refs, count, r, rows):
     ext, w = refs[: 2 * count], refs[2 * count : 4 * count]
-    late, m_ref, base = refs[4 * count : -4], refs[-4], refs[-3]
-    r_ref, p_ref = refs[-2:]
+    late, m_ref, base = refs[4 * count : -6], refs[-6], refs[-5]
+    r_ref, p_ref, l_buf, l_sems = refs[-4:]
     cols = r_ref.shape[1]
+    copies = [
+        pltpu.make_async_copy(ref, l_buf.at[i], l_sems.at[i]) for i, ref in enumerate(late)
+    ]
+    for copy in copies:
+        copy.start()
     pooled = [dot(m_ref[...], e[...]).astype(BF16) for e in ext]
     split = cols // 2 if r else early_of(cols)
     for first, size in ((0, split), (split, cols - split)):
         at = pl.ds(first, size)
+        if first:
+            for copy in copies:
+                copy.wait()
         total, few = base[r, pl.ds(0, rows), at], base[r, pl.ds(rows, m_ref.shape[0]), at]
         for i in range(2 * count):
             if i < count:
@@ -237,7 +245,7 @@
             elif r:
                 part = w[i][:, pl.ds((r - 1) * cols + first, size)]
             elif first:
-                part = late[i - count][...]
+                part = l_buf[i - count]
             else:
                 part = w[i][:, pl.ds(w[i].shape[1] - size, size)]
             total = total + dot(ext[i][...], part)
@@ -429,15 +437,19 @@
                 jax.ShapeDtypeStruct((tokens_here, cols), kind),
                 jax.ShapeDtypeStruct((r_dev, cols), kind),
             ],
-            in_specs=[VMEM] * (2 * len(stacks) + len(late) + 2),
+            in_specs=[VMEM] * (2 * len(stacks)) + [HBM] * len(late) + [VMEM] * 2,
             out_specs=[VMEM, VMEM],
+            scratch_shapes=[
+                scratch((side - 1, width, cols - early_of(cols)), BF16),
+                pltpu.SemaphoreType.DMA((side - 1,)),
+            ],
             cost_estimate=pl.CostEstimate(
                 flops=2 * height * cols * width * len(stacks),
                 bytes_accessed=2 * width * cols * len(stacks),
                 transcendentals=0,
             ),
             compiler_params=pltpu.CompilerParams(vmem_limit_bytes=12 << 20),
-        )(*stacks, *weights, *late, member, base)
+        )(*stacks, *weights, *[stay(w) for w in late], member, base)
 
     given = [project(r, BF16) for r in range(1, side)]
     pool_in = [move(p, across(r + 1)) for r, (_, p) in enumerate(given)]

time: 75.4 us -> 76.2 us (1.011)
  waiting for transfers between devices: 32.4 us -> 33.5 us
    ppermute x13, waiting for transfers between devices: 26.4 us -> 27.6 us  [move(): lax.ppermute(value, 'head', [(i, i ^ masks[i % 2]) for i in range(n)])]
    pallas_call x1, Pallas kernels: 4.45 us -> 3.44 us  [per_device(): pl.pallas_call(functools.partial(here_kernel, half_bits=half_bits), out_s...]
    pallas_call x2, Pallas kernels: 1.99 us -> 2.82 us  [project(): pl.pallas_call(functools.partial(add_kernel, count=side - 1, r=r, rows=to...]
where the time goes in v5:
time: 76.2 us; the launch traced here: 76 us
  waiting for transfers between devices  33.5 us (44%)
  Pallas kernels  24 us (31%)
  starting transfers between devices  16.4 us (22%)
  between operations  0.83 us (1%)
  matrix products  0.79 us (1%)
    ppermute x13, waiting for transfers between devices, move(): lax.ppermute(value, 'head', [(i, i ^ masks[i % 2]) for i in range(n)])  27.6 us
    ppermute x13, starting transfers between devices, move(): lax.ppermute(value, 'head', [(i, i ^ masks[i % 2]) for i in range(n)])  12 us
    pallas_call x1, Pallas kernels, per_device(): pl.pallas_call(functools.partial(kv_kernel, steps=steps, half_bits=half_b...  8.27 us
    ppermute x3, waiting for transfers between devices, per_device(): lax.ppermute(states, 'seq', [(i, i ^ s) for i in range(n_seq)])  5.95 us
    pallas_call x1, Pallas kernels, per_device(): pl.pallas_call(functools.partial(q_kernel, steps=4, half_bits=half_bits,...  5.63 us
    ppermute x3, starting transfers between devices, per_device(): lax.ppermute(states, 'seq', [(i, i ^ s) for i in range(n_seq)])  4.39 us
    pallas_call x1, Pallas kernels, per_device(): pl.pallas_call(functools.partial(here_kernel, half_bits=half_bits), out_s...  3.44 us
    pallas_call x2, Pallas kernels, project(): pl.pallas_call(functools.partial(add_kernel, count=side - 1, r=r, rows=to...  2.82 us
  transfers between devices with their start and end apart: 16, of which 8 were waited for; matrix products, arithmetic and copies ran while one was open for 2% of the time, Pallas kernels for 12%

profile of v5, /device:TPU:0, one launch (start us, length us, event | category | flops | bytes accessed | tf_op | source)
XLA Modules:
  0.0 76.0 jit_solution(5745353757543245243)
XLA Ops:
  0.6 8.3 %kv.1 = (bf16[512,256]{1,0:T(8,128)(2,1)S(1)}, bf16[512,256]{1,0:T(8,128)(2,1)S(1)}, bf16[2,128,128]{2,1,0:T(8,128)(2,1)S(1)}, bf16[512,8192]{1,0:T(8,128)(2,1)S(1)}, bf16[256,1280]{1,0:T(8,128)(2,1)}) custom-call(bf16[512,8192]{1,0:T(8,128)(2,1)} %x_ref.3, bf16[3,8192,256]{2,1,0:T(8,128)(2,1)} %w_ref.5, bf16[256,8192]{1,0:T(8,128)(2,1)} %w_ref.7), custom_call_target="tpu_custom_call" | custom-call | flops 4294967296 | bytes 16777216 | tf_op jit(solution)/shard_map/kv/pallas_call | solution.py:329
  8.9 5.6 %qlocal.1 = (bf16[512,256]{1,0:T(8,128)(2,1)S(1)}, f32[512,256]{1,0:T(8,128)S(1)}, bf16[256,2048]{1,0:T(8,128)(2,1)}, bf16[256,768]{1,0:T(8,128)(2,1)}) custom-call(bf16[512,8192]{1,0:T(8,128)(2,1)S(1)} %get-tuple-element.17.x_ref, bf16[3,8192,256]{2,1,0:T(8,128)(2,1)} %w_ref.5, bf16[512,256]{1,0:T(8,128)(2,1)S(1)} %get-tuple-element.18.k_ref, ...), custom_call_target="tpu_custom_call" | custom-call | flops 2147483648 | bytes 4194304 | tf_op jit(solution)/shard_map/qlocal/pallas_call | solution.py:360
  15.1 1.2 %cut.1 = bf16[256,2048]{1,0:T(8,128)(2,1)S(1)} custom-call(bf16[256,8192]{1,0:T(8,128)(2,1)} %w_ref.7), custom_call_target="tpu_custom_call" | custom-call | bytes 2097152 | tf_op jit(solution)/shard_map/cut/pallas_call | solution.py:312
  16.4 2.6 %collective-permute-start.5 = (bf16[256,2048]{1,0:T(8,128)(2,1)S(1)}, bf16[256,2048]{1,0:T(8,128)(2,1)S(1)}, u32[]{:S(2)}, u32[]{:S(2)}) collective-permute-start(bf16[256,2048]{1,0:T(8,128)(2,1)S(1)} %cut.1), channel_id=1, source_target_pairs={{0,2},{1,5},{2,0},{3,7},{4,6},{5,1},{6,4},{7,3},{8,10},{9,13},{10,... | collective-permute-start | bytes 3145736 | tf_op jit(solution)/shard_map/ppermute | solution.py:20
  18.9 1.6 %collective-permute-start = (bf16[2,128,128]{2,1,0:T(8,128)(2,1)S(1)}, bf16[2,128,128]{2,1,0:T(8,128)(2,1)S(1)}, u32[]{:S(2)}, u32[]{:S(2)}) collective-permute-start(bf16[2,128,128]{2,1,0:T(8,128)(2,1)S(1)} %get-tuple-element.22), channel_id=1, source_target_pairs={{0,8},{8,0},{16,24},{24,16},{1,9},{9,1},{17,25},{25,17},{2,10},{10... | collective-permute-start | bytes 196616 | tf_op jit(solution)/shard_map/ppermute | solution.py:358
  20.5 2.6 %collective-permute-start.1 = (bf16[2,128,128]{2,1,0:T(8,128)(2,1)S(1)}, bf16[2,128,128]{2,1,0:T(8,128)(2,1)S(1)}, u32[]{:S(2)}, u32[]{:S(2)}) collective-permute-start(bf16[2,128,128]{2,1,0:T(8,128)(2,1)S(1)} %get-tuple-element.22), channel_id=1, source_target_pairs={{0,16},{8,24},{16,0},{24,8},{1,17},{9,25},{17,1},{25,9},{2,18},{10... | collective-permute-start | bytes 196616 | tf_op jit(solution)/shard_map/ppermute | solution.py:358
  23.3 4.8 %collective-permute-done.1.refs_3_ = bf16[2,128,128]{2,1,0:T(8,128)(2,1)S(1)} collective-permute-done((bf16[2,128,128]{2,1,0:T(8,128)(2,1)S(1)}, bf16[2,128,128]{2,1,0:T(8,128)(2,1)S(1)}, u32[]{:S(2)}, u32[]{:S(2)}) %collective-permute-start.1) | collective-permute-done | bytes 65568 | tf_op jit(solution)/shard_map/ppermute | solution.py:358
  28.1 1.2 %collective-permute-done.2.refs_4_ = bf16[2,128,128]{2,1,0:T(8,128)(2,1)S(1)} collective-permute-done((bf16[2,128,128]{2,1,0:T(8,128)(2,1)S(1)}, bf16[2,128,128]{2,1,0:T(8,128)(2,1)S(1)}, u32[]{:S(2)}, u32[]{:S(2)}) %collective-permute-start.2) | collective-permute-done | bytes 65568 | tf_op jit(solution)/shard_map/ppermute | solution.py:358
  29.7 1.5 %collective-permute-start.7 = (bf16[256,768]{1,0:T(8,128)(2,1)}, bf16[256,768]{1,0:T(8,128)(2,1)}, u32[]{:S(2)}, u32[]{:S(2)}) collective-permute-start(bf16[256,768]{1,0:T(8,128)(2,1)} %get-tuple-element.24), channel_id=1, source_target_pairs={{0,5},{1,2},{2,7},{3,0},{4,1},{5,6},{6,3},{7,4},{8,13},{9,10},{10,... | collective-permute-start | bytes 1179656 | tf_op jit(solution)/shard_map/ppermute | solution.py:20
  31.5 0.7 collective-permute-start.3
  32.2 0.6 collective-permute-start.4
  32.9 3.4 %here.1.refs_6_.refs_5_ = f32[2,576,1024]{2,1,0:T(8,128)S(1)} custom-call(bf16[512,256]{1,0:T(8,128)(2,1)S(1)} %attend.1.own_ref, bf16[512,256]{1,0:T(8,128)(2,1)S(1)} %collective-permute-done.8.peer_ref, bf16[64,512]{1,0:T(8,128)(2,1)S(1)} %fusion.2.m_ref.refs_5_.refs_4_, bf16[512,8192]{1,0:T(8,128)(2,1)} %x_ref.3, bf16[256,8192]{1,0:T(8,128)(2,1)} %w_ref.7, ...), custom_call_target="tpu_custom_call" | custom-call | flops 1207959552 | bytes 2097152 | tf_op jit(solution)/shard_map/here/pallas_call | solution.py:409
  36.3 7.4 %collective-permute-done.3.refs_0_ = bf16[512,256]{1,0:T(8,128)(2,1)S(1)} collective-permute-done((bf16[512,256]{1,0:T(8,128)(2,1)S(1)}, bf16[512,256]{1,0:T(8,128)(2,1)S(1)}, u32[]{:S(2)}, u32[]{:S(2)}) %collective-permute-start.3) | collective-permute-done | bytes 262176 | tf_op jit(solution)/shard_map/ppermute | solution.py:20
  43.7 4.8 %collective-permute-done.4.refs_1_ = bf16[512,256]{1,0:T(8,128)(2,1)S(1)} collective-permute-done((bf16[512,256]{1,0:T(8,128)(2,1)S(1)}, bf16[512,256]{1,0:T(8,128)(2,1)S(1)}, u32[]{:S(2)}, u32[]{:S(2)}) %collective-permute-start.4) | collective-permute-done | bytes 262176 | tf_op jit(solution)/shard_map/ppermute | solution.py:20
  48.6 1.0 %shard_map.87 = (bf16[512,1024]{1,0:T(8,128)(2,1)S(1)}, bf16[64,1024]{1,0:T(8,128)(2,1)S(1)}) custom-call(bf16[512,256]{1,0:T(8,128)(2,1)S(1)} %collective-permute-done.3.refs_0_, bf16[512,256]{1,0:T(8,128)(2,1)S(1)} %collective-permute-done.4.refs_1_, bf16[256,2048]{1,0:T(8,128)(2,1)S(1)} %collective-permute-done.5.refs_2_, ...), custom_call_target="tpu_custom_call" | custom-call | flops 603979776 | bytes 1048576 | tf_op jit(solution)/shard_map/pallas_call | solution.py:434
  49.6 2.1 %collective-permute-start.11 = (bf16[64,1024]{1,0:T(8,128)(2,1)S(1)}, bf16[64,1024]{1,0:T(8,128)(2,1)S(1)}, u32[]{:S(2)}, u32[]{:S(2)}) collective-permute-start(bf16[64,1024]{1,0:T(8,128)(2,1)S(1)} %get-tuple-element.30), channel_id=1, source_target_pairs={{0,4},{1,3},{2,6},{3,1},{4,0},{5,7},{6,2},{7,5},{8,12},{9,11},{10,... | collective-permute-start | bytes 393224 | tf_op jit(solution)/shard_map/ppermute | solution.py:20
  51.7 1.8 %shard_map.86 = (f32[512,1024]{1,0:T(8,128)S(1)}, f32[64,1024]{1,0:T(8,128)S(1)}) custom-call(bf16[512,256]{1,0:T(8,128)(2,1)S(1)} %collective-permute-done.3.refs_0_, bf16[512,256]{1,0:T(8,128)(2,1)S(1)} %collective-permute-done.4.refs_1_, bf16[256,2048]{1,0:T(8,128)(2,1)S(1)} %collective-permute-done.5.refs_2_, ...), custom_call_target="tpu_custom_call" | custom-call | flops 603979776 | bytes 1048576 | tf_op jit(solution)/shard_map/pallas_call | solution.py:434
  53.7 0.9 %collective-permute-done.11 = bf16[64,1024]{1,0:T(8,128)(2,1)S(1)} collective-permute-done((bf16[64,1024]{1,0:T(8,128)(2,1)S(1)}, bf16[64,1024]{1,0:T(8,128)(2,1)S(1)}, u32[]{:S(2)}, u32[]{:S(2)}) %collective-permute-start.11) | collective-permute-done | bytes 131104 | tf_op jit(solution)/shard_map/ppermute | solution.py:20
  55.0 1.2 %collective-permute-done.12 = bf16[64,1024]{1,0:T(8,128)(2,1)S(1)} collective-permute-done((bf16[64,1024]{1,0:T(8,128)(2,1)S(1)}, bf16[64,1024]{1,0:T(8,128)(2,1)S(1)}, u32[]{:S(2)}, u32[]{:S(2)}) %collective-permute-start.12) | collective-permute-done | bytes 131104 | tf_op jit(solution)/shard_map/ppermute | solution.py:20
  56.3 3.0 %collective-permute-start.15 = (bf16[32,2048]{1,0:T(8,128)(2,1)S(1)}, bf16[32,2048]{1,0:T(8,128)(2,1)S(1)}, u32[]{:S(2)}, u32[]{:S(2)}) collective-permute-start(bf16[32,2048]{1,0:T(8,128)(2,1)S(1)} %convolution_convert_fusion.1), channel_id=1, source_target_pairs={{0,6},{1,7},{2,4},{3,5},{4,2},{5,3},{6,0},{7,1},{8,14},{9,15},{10,... | collective-permute-start | bytes 393224 | tf_op jit(solution)/shard_map/ppermute | solution.py:20
  60.7 2.9 %collective-permute-done.15.refs_2_ = bf16[32,2048]{1,0:T(8,128)(2,1)S(1)} collective-permute-done((bf16[32,2048]{1,0:T(8,128)(2,1)S(1)}, bf16[32,2048]{1,0:T(8,128)(2,1)S(1)}, u32[]{:S(2)}, u32[]{:S(2)}) %collective-permute-start.15) | collective-permute-done | bytes 131104 | tf_op jit(solution)/shard_map/ppermute | solution.py:20
  63.7 10.3 %collective-permute-done.14.refs_1_ = bf16[32,2048]{1,0:T(8,128)(2,1)S(1)} collective-permute-done((bf16[32,2048]{1,0:T(8,128)(2,1)S(1)}, bf16[32,2048]{1,0:T(8,128)(2,1)S(1)}, u32[]{:S(2)}, u32[]{:S(2)}) %collective-permute-start.14) | collective-permute-done | bytes 131104 | tf_op jit(solution)/shard_map/ppermute | solution.py:20
  74.0 1.0 %score.1 = f32[32,64]{1,0:T(8,128)} custom-call(bf16[64,8192]{1,0:T(8,128)(2,1)S(1)} %copy-done, bf16[32,2048]{1,0:T(8,128)(2,1)S(1)} %collective-permute-done.13.refs_0_, bf16[32,2048]{1,0:T(8,128)(2,1)S(1)} %collective-permute-done.14.refs_1_, bf16[32,2048]{1,0:T(8,128)(2,1)S(1)} %collective-permute-done.15.refs_2_, f32[32,64]{1,0:T(8,128)S(1)} %score_first.1.refs_3_), custom_call_target="tpu_custom_call" | custom-call | tf_op jit(solution)/shard_map/score/pallas_call | solution.py:495
  75.0 1.1 %mix.1 = bf16[512,1024]{1,0:T(8,128)(2,1)} custom-call(f32[512,1024]{1,0:T(8,128)S(1)} %get-tuple-element.26.refs_0_, bf16[512,1024]{1,0:T(8,128)(2,1)S(1)} %collective-permute-done.10.refs_1_), custom_call_target="tpu_custom_call" | custom-call | flops 524288 | bytes 4194304 | tf_op jit(solution)/shard_map/mix/pallas_call | solution.py:481
  (36 shorter events, 3.6 us)
Async XLA Ops:
  8.9 22.4 %copy-start.1 = (s32[1,512]{1,0:T(1,128)S(1)}, s32[1,512]{1,0:T(1,128)}, u32[]{:S(2)}) copy-start(s32[1,512]{1,0:T(1,128)} %param.10) | copy-start | bytes 6148
  8.9 22.3 %copy-start.2 = (s32[1,64]{1,0:T(1,128)S(1)}, s32[1,64]{1,0:T(1,128)}, u32[]{:S(2)}) copy-start(s32[1,64]{1,0:T(1,128)} %param.11) | copy-start | bytes 772
  14.6 17.6 %collective-permute-start.9 = (bf16[256,2048]{1,0:T(8,128)(2,1)}, bf16[256,2048]{1,0:T(8,128)(2,1)}, u32[]{:S(2)}, u32[]{:S(2)}) collective-permute-start(bf16[256,2048]{1,0:T(8,128)(2,1)} %get-tuple-element.25), channel_id=1, source_target_pairs={{0,1},{1,0},{2,3},{3,2},{4,5},{5,4},{6,7},{7,6},{8,9},{9,8},{10,11... | collective-permute-start | bytes 3145736 | tf_op jit(solution)/shard_map/ppermute | solution.py:20
  16.4 32.2 %collective-permute-start.5 = (bf16[256,2048]{1,0:T(8,128)(2,1)S(1)}, bf16[256,2048]{1,0:T(8,128)(2,1)S(1)}, u32[]{:S(2)}, u32[]{:S(2)}) collective-permute-start(bf16[256,2048]{1,0:T(8,128)(2,1)S(1)} %cut.1), channel_id=1, source_target_pairs={{0,2},{1,5},{2,0},{3,7},{4,6},{5,1},{6,4},{7,3},{8,10},{9,13},{10,... | collective-permute-start | bytes 3145736 | tf_op jit(solution)/shard_map/ppermute | solution.py:20
  18.9 4.4 %collective-permute-start = (bf16[2,128,128]{2,1,0:T(8,128)(2,1)S(1)}, bf16[2,128,128]{2,1,0:T(8,128)(2,1)S(1)}, u32[]{:S(2)}, u32[]{:S(2)}) collective-permute-start(bf16[2,128,128]{2,1,0:T(8,128)(2,1)S(1)} %get-tuple-element.22), channel_id=1, source_target_pairs={{0,8},{8,0},{16,24},{24,16},{1,9},{9,1},{17,25},{25,17},{2,10},{10... | collective-permute-start | bytes 196616 | tf_op jit(solution)/shard_map/ppermute | solution.py:358
  20.5 7.6 %collective-permute-start.1 = (bf16[2,128,128]{2,1,0:T(8,128)(2,1)S(1)}, bf16[2,128,128]{2,1,0:T(8,128)(2,1)S(1)}, u32[]{:S(2)}, u32[]{:S(2)}) collective-permute-start(bf16[2,128,128]{2,1,0:T(8,128)(2,1)S(1)} %get-tuple-element.22), channel_id=1, source_target_pairs={{0,16},{8,24},{16,0},{24,8},{1,17},{9,25},{17,1},{25,9},{2,18},{10... | collective-permute-start | bytes 196616 | tf_op jit(solution)/shard_map/ppermute | solution.py:358
  23.1 6.2 %collective-permute-start.2 = (bf16[2,128,128]{2,1,0:T(8,128)(2,1)S(1)}, bf16[2,128,128]{2,1,0:T(8,128)(2,1)S(1)}, u32[]{:S(2)}, u32[]{:S(2)}) collective-permute-start(bf16[2,128,128]{2,1,0:T(8,128)(2,1)S(1)} %get-tuple-element.22), channel_id=1, source_target_pairs={{0,24},{8,16},{16,8},{24,0},{1,25},{9,17},{17,9},{25,1},{2,26},{10... | collective-permute-start | bytes 196616 | tf_op jit(solution)/shard_map/ppermute | solution.py:358
  23.3 25.2 %collective-permute-start.6 = (bf16[256,1280]{1,0:T(8,128)(2,1)}, bf16[256,1280]{1,0:T(8,128)(2,1)S(1)}, u32[]{:S(2)}, u32[]{:S(2)}) collective-permute-start(bf16[256,1280]{1,0:T(8,128)(2,1)} %get-tuple-element.23), channel_id=1, source_target_pairs={{0,5},{1,2},{2,7},{3,0},{4,1},{5,6},{6,3},{7,4},{8,13},{9,10},{10,... | collective-permute-start | bytes 1966088 | tf_op jit(solution)/shard_map/ppermute | solution.py:20
  29.7 1.8 %collective-permute-start.8 = (bf16[512,256]{1,0:T(8,128)(2,1)S(1)}, bf16[512,256]{1,0:T(8,128)(2,1)S(1)}, u32[]{:S(2)}, u32[]{:S(2)}) collective-permute-start(bf16[512,256]{1,0:T(8,128)(2,1)S(1)} %attend.1.own_ref), channel_id=1, source_target_pairs={{0,1},{1,0},{2,3},{3,2},{4,5},{5,4},{6,7},{7,6},{8,9},{9,8},{10,11... | collective-permute-start | bytes 786440 | tf_op jit(solution)/shard_map/ppermute | solution.py:20
  29.7 21.9 %collective-permute-start.7 = (bf16[256,768]{1,0:T(8,128)(2,1)}, bf16[256,768]{1,0:T(8,128)(2,1)}, u32[]{:S(2)}, u32[]{:S(2)}) collective-permute-start(bf16[256,768]{1,0:T(8,128)(2,1)} %get-tuple-element.24), channel_id=1, source_target_pairs={{0,5},{1,2},{2,7},{3,0},{4,1},{5,6},{6,3},{7,4},{8,13},{9,10},{10,... | collective-permute-start | bytes 1179656 | tf_op jit(solution)/shard_map/ppermute | solution.py:20
  31.5 12.3 %collective-permute-start.3 = (bf16[512,256]{1,0:T(8,128)(2,1)S(1)}, bf16[512,256]{1,0:T(8,128)(2,1)S(1)}, u32[]{:S(2)}, u32[]{:S(2)}) collective-permute-start(bf16[512,256]{1,0:T(8,128)(2,1)S(1)} %attend.1.own_ref), channel_id=1, source_target_pairs={{0,2},{1,5},{2,0},{3,7},{4,6},{5,1},{6,4},{7,3},{8,10},{9,13},{10,... | collective-permute-start | bytes 786440 | tf_op jit(solution)/shard_map/ppermute | solution.py:20
  32.2 16.4 %collective-permute-start.4 = (bf16[512,256]{1,0:T(8,128)(2,1)S(1)}, bf16[512,256]{1,0:T(8,128)(2,1)S(1)}, u32[]{:S(2)}, u32[]{:S(2)}) collective-permute-start(bf16[512,256]{1,0:T(8,128)(2,1)S(1)} %attend.1.own_ref), channel_id=1, source_target_pairs={{0,5},{1,2},{2,7},{3,0},{4,1},{5,6},{6,3},{7,4},{8,13},{9,10},{10,... | collective-permute-start | bytes 786440 | tf_op jit(solution)/shard_map/ppermute | solution.py:20
  36.3 18.5 %copy-start.3 = (s32[64,1]{0,1:T(1,128)S(1)}, s32[64,1]{0,1:T(1,128)}, u32[]{:S(2)}) copy-start(s32[64,1]{0,1:T(1,128)} %param.12) | copy-start | bytes 772
  36.3 24.2 %copy-start = (bf16[64,8192]{1,0:T(8,128)(2,1)S(1)}, bf16[64,8192]{1,0:T(8,128)(2,1)}, u32[]{:S(2)}) copy-start(bf16[64,8192]{1,0:T(8,128)(2,1)} %c_ref.3) | copy-start | bytes 3145732
  49.6 5.1 %collective-permute-start.11 = (bf16[64,1024]{1,0:T(8,128)(2,1)S(1)}, bf16[64,1024]{1,0:T(8,128)(2,1)S(1)}, u32[]{:S(2)}, u32[]{:S(2)}) collective-permute-start(bf16[64,1024]{1,0:T(8,128)(2,1)S(1)} %get-tuple-element.30), channel_id=1, source_target_pairs={{0,4},{1,3},{2,6},{3,1},{4,0},{5,7},{6,2},{7,5},{8,12},{9,11},{10,... | collective-permute-start | bytes 393224 | tf_op jit(solution)/shard_map/ppermute | solution.py:20
  53.5 21.4 %collective-permute-start.10 = (bf16[512,1024]{1,0:T(8,128)(2,1)S(1)}, bf16[512,1024]{1,0:T(8,128)(2,1)S(1)}, u32[]{:S(2)}, u32[]{:S(2)}) collective-permute-start(bf16[512,1024]{1,0:T(8,128)(2,1)S(1)} %get-tuple-element.27), channel_id=1, source_target_pairs={{0,4},{1,3},{2,6},{3,1},{4,0},{5,7},{6,2},{7,5},{8,12},{9,11},{10,... | collective-permute-start | bytes 3145736 | tf_op jit(solution)/shard_map/ppermute | solution.py:20
  54.7 1.4 %collective-permute-start.12 = (bf16[64,1024]{1,0:T(8,128)(2,1)S(1)}, bf16[64,1024]{1,0:T(8,128)(2,1)S(1)}, u32[]{:S(2)}, u32[]{:S(2)}) collective-permute-start(bf16[64,1024]{1,0:T(8,128)(2,1)S(1)} %divide_convert_fusion), channel_id=1, source_target_pairs={{0,1},{1,0},{2,3},{3,2},{4,5},{5,4},{6,7},{7,6},{8,9},{9,8},{10,11... | collective-permute-start | bytes 393224 | tf_op jit(solution)/shard_map/ppermute | solution.py:20
  56.3 7.4 %collective-permute-start.15 = (bf16[32,2048]{1,0:T(8,128)(2,1)S(1)}, bf16[32,2048]{1,0:T(8,128)(2,1)S(1)}, u32[]{:S(2)}, u32[]{:S(2)}) collective-permute-start(bf16[32,2048]{1,0:T(8,128)(2,1)S(1)} %convolution_convert_fusion.1), channel_id=1, source_target_pairs={{0,6},{1,7},{2,4},{3,5},{4,2},{5,3},{6,0},{7,1},{8,14},{9,15},{10,... | collective-permute-start | bytes 393224 | tf_op jit(solution)/shard_map/ppermute | solution.py:20
  59.5 14.5 %collective-permute-start.14 = (bf16[32,2048]{1,0:T(8,128)(2,1)S(1)}, bf16[32,2048]{1,0:T(8,128)(2,1)S(1)}, u32[]{:S(2)}, u32[]{:S(2)}) collective-permute-start(bf16[32,2048]{1,0:T(8,128)(2,1)S(1)} %convolution_convert_fusion.2), channel_id=1, source_target_pairs={{0,4},{1,5},{2,6},{3,7},{4,0},{5,1},{6,2},{7,3},{8,12},{9,13},{10,... | collective-permute-start | bytes 393224 | tf_op jit(solution)/shard_map/ppermute | solution.py:20
  60.2 13.8 %collective-permute-start.13 = (bf16[32,2048]{1,0:T(8,128)(2,1)S(1)}, bf16[32,2048]{1,0:T(8,128)(2,1)S(1)}, u32[]{:S(2)}, u32[]{:S(2)}) collective-permute-start(bf16[32,2048]{1,0:T(8,128)(2,1)S(1)} %convolution_convert_fusion.3), channel_id=1, source_target_pairs={{0,2},{1,3},{2,0},{3,1},{4,6},{5,7},{6,4},{7,5},{8,10},{9,11},{10,... | collective-permute-start | bytes 393224 | tf_op jit(solution)/shard_map/ppermute | solution.py:20
